TPU v7x, 32 devices: a whole 2x2x4 slice. The times are simulated.
32 devices in a mesh: head: 4 (over z), span: 8 (over y, x, core).
Axes of the slice: x: 2, y: 2, z: 4, core: 2. Of those that a mesh axis runs over, the one named last changes fastest.
Arguments:
- tokens: bfloat16 [8, 4096, 512], P('span', 'head'), may hold values from -6 to 6
- segment_ids: int32 [8, 4096], P('span'), may hold values from 0 to 4, as said below
- first_gain: float32 [512], P(('head', 'span')), may hold values from 0.5 to 1.5
- first_shift: float32 [512], P(('head', 'span')), may hold values from -3 to 3
- project_weight: bfloat16 [3, 512, 512], P(None, ('head', 'span')), may hold values from -0.25 to 0.25
- project_bias: float32 [3, 512], P(None, ('head', 'span')), may hold values from -1.2 to 1.2
- output_weight: bfloat16 [512, 512], P(('head', 'span')), may hold values from -1 to 1
- output_bias: float32 [512], P(('head', 'span')), may hold values from -3 to 3
- second_gain: float32 [512], P(('head', 'span')), may hold values from 0.5 to 1.5
- second_shift: float32 [512], P(('head', 'span')), may hold values from -3 to 3
- expand_weight: bfloat16 [512, 2048], P(('head', 'span')), may hold values from -0.25 to 0.25
- expand_bias: float32 [2048], P(('head', 'span')), may hold values from -3 to 3
- reduce_weight: bfloat16 [2048, 512], P(('head', 'span')), may hold values from -0.125 to 0.125
- reduce_bias: float32 [512], P(('head', 'span')), may hold values from -3 to 3
- cotangent: bfloat16 [8, 4096, 512], P('span', 'head'), may hold values from -6 to 6
Outputs:
- layer_output: bfloat16 [8, 4096, 512], P('span', 'head')
- tokens_grad: bfloat16 [8, 4096, 512], P('span', 'head')
- first_gain_grad: float32 [512], P(('head', 'span'))
- first_shift_grad: float32 [512], P(('head', 'span'))
- project_weight_grad: float32 [3, 512, 512], P(None, ('head', 'span'))
- project_bias_grad: float32 [3, 512], P(None, ('head', 'span'))
- output_weight_grad: float32 [512, 512], P(('head', 'span'))
- output_bias_grad: float32 [512], P(('head', 'span'))
- second_gain_grad: float32 [512], P(('head', 'span'))
- second_shift_grad: float32 [512], P(('head', 'span'))
- expand_weight_grad: float32 [512, 2048], P(('head', 'span'))
- expand_bias_grad: float32 [2048], P(('head', 'span'))
- reduce_weight_grad: float32 [2048, 512], P(('head', 'span'))
- reduce_bias_grad: float32 [512], P(('head', 'span'))
Inputs may be any that keep to these rules, and one draw needn't show every extreme that they name: `segment_ids`: row r is spans 2r and 2r+1 laid end to end (8192 positions). Along a row the ids rise from 1 without falling, and every row ends with one or more padding positions of id 0, the only zeros of the row.
All inputs are finite; a program needn't handle non-finite values.
Results may differ from a plain program's by a relative error of at most 0.039.
Values may be sent and summed in bfloat16 or wider, within the bound.
A program may use at most 320 MiB of HBM per device.

v0:
```python
import jax
import jax.numpy as jnp
from jax import lax
from jax.sharding import PartitionSpec as P

HEADS = 8
HEAD_DIM = 64
BLOCK = 16


epsilon = 1e-05
highest = lax.Precision.HIGHEST


def swapped(value, axis, bit):
    mask = 2**bit
    pairs = [(source, source ^ mask) for source in range(lax.axis_size(axis))]
    return lax.ppermute(value, axis, pairs)


def normalize(values_in):
    center = values_in - jnp.mean(values_in, axis=-1, keepdims=True)
    inverse = lax.rsqrt(jnp.mean(center * center, axis=-1, keepdims=True) + epsilon)
    return (center * inverse, inverse)


def norm_backward(grad_normed, normed, inverse, gain):
    scaled = grad_normed * gain
    first_mean = jnp.mean(scaled, axis=-1, keepdims=True)
    second_mean = jnp.mean(scaled * normed, axis=-1, keepdims=True)
    return inverse * (scaled - first_mean - normed * second_mean)


def pair_sum(values_in):
    return values_in.reshape((values_in.shape[0] // 2, 2) + values_in.shape[1:]).sum(axis=1)


def spread_up(values_in):
    count = values_in.shape[0]
    return jnp.broadcast_to(values_in[:, None], (count, 2) + values_in.shape[1:]).reshape(
        (count * 2,) + values_in.shape[1:]
    )


def coarse_labels(labels):
    paired = labels.reshape(-1, 2)
    return jnp.where(paired[:, 0] == paired[:, 1], paired[:, 0], 0)


def windows(padded, blocks):
    shaped = padded.reshape((blocks + 2, BLOCK) + padded.shape[1:])
    return jnp.concatenate([shaped[:-2], shaped[1:-1], shaped[2:]], axis=1)


def unwindow(window_grads, blocks):
    pieces = window_grads.reshape(blocks, 3, BLOCK, -1)
    keep_pad = ((0, 0), (0, 0))
    summed = (
        jnp.pad(pieces[:, 0], ((0, 2),) + keep_pad)
        + jnp.pad(pieces[:, 1], ((1, 1),) + keep_pad)
        + jnp.pad(pieces[:, 2], ((2, 0),) + keep_pad)
    )
    return summed.reshape((blocks + 2) * BLOCK, pieces.shape[-1])


def allowed(query_labels, key_labels, height):
    blocks = query_labels.shape[0]
    query_side = query_labels.T[:, None, :]
    key_side = key_labels.T[None, :, :]
    matching = (query_side == key_side) & (key_side != 0)
    query_pos = lax.broadcasted_iota(jnp.int32, (BLOCK, 3 * BLOCK, blocks), 0)
    key_pos = lax.broadcasted_iota(jnp.int32, (BLOCK, 3 * BLOCK, blocks), 1)
    if height == 0:
        return matching | (query_pos + BLOCK == key_pos)
    half_block = BLOCK // 2
    return matching & (
        jnp.abs(query_pos // half_block - key_pos // half_block + BLOCK // half_block) >= 2
    )


def pick_edge(values_in, parity):
    return jnp.where(parity == 0, values_in[-BLOCK:], values_in[:BLOCK])


def extend(local_part, arriving, parity):
    zeroed = jnp.zeros_like(arriving)
    left_part = jnp.where(parity == 1, arriving, zeroed)
    right_part = jnp.where(parity == 0, arriving, zeroed)
    return jnp.concatenate([left_part, local_part, right_part], axis=0)


def place_edge(edge, extent, parity):
    at_end = jnp.pad(edge, ((extent - BLOCK, 0), (0, 0)))
    at_start = jnp.pad(edge, ((0, extent - BLOCK), (0, 0)))
    return jnp.where(parity == 0, at_end, at_start)


def level_stack(queries, keys, values, labels):
    count = (queries.shape[0] // BLOCK).bit_length()
    runs = (queries.astype(jnp.float32), keys.astype(jnp.float32), values.astype(jnp.float32))
    levels = [(runs[0], runs[1], runs[2], labels)]
    label_run = labels
    for height in range(1, count):
        runs = (pair_sum(runs[0]) * 0.5, pair_sum(runs[1]) * 0.5, pair_sum(runs[2]))
        label_run = coarse_labels(label_run)
        levels.append((runs[0], runs[1], runs[2], label_run))
    return (levels, runs)


def build_levels(queries, keys, values, labels):
    return level_stack(queries, keys, values, labels)[0]


def level_weights(height, query_coarse, key_pad, label_query, label_pad, heads):
    blocks = query_coarse.shape[0] // BLOCK
    query_block = query_coarse.reshape(blocks, BLOCK, heads, HEAD_DIM)
    key_window = windows(key_pad, blocks).reshape(blocks, 3 * BLOCK, heads, HEAD_DIM)
    allowed_pairs = allowed(label_query.reshape(blocks, BLOCK), windows(label_pad, blocks), height)
    scores = jnp.einsum(
        "bihd,bjhd->hijb", query_block, key_window, precision=highest
    ) * HEAD_DIM ** (-0.5)
    weights = jnp.where(allowed_pairs[None], jnp.exp(scores), 0.0)
    return (query_block, key_window, weights)


def level_forward(height, query_coarse, key_pad, value_pad, label_coarse, label_pad, heads):
    query_block, key_window, weights = level_weights(
        height, query_coarse, key_pad, label_coarse, label_pad, heads
    )
    blocks = query_block.shape[0]
    value_window = windows(value_pad, blocks).reshape(blocks, 3 * BLOCK, heads, HEAD_DIM)
    level_total = 2**height * jnp.sum(weights, axis=2)
    level_total = level_total.transpose(2, 1, 0).reshape(blocks * BLOCK, heads)
    numerator = jnp.einsum("hijb,bjhd->bihd", weights, value_window, precision=highest)
    return (level_total, numerator.reshape(blocks * BLOCK, heads * HEAD_DIM))


def level_backward(
    height, query_coarse, key_pad, value_pad, label_coarse, label_pad, grad_run, rest_run, heads
):
    factor = HEAD_DIM ** (-0.5)
    query_block, key_window, weights = level_weights(
        height, query_coarse, key_pad, label_coarse, label_pad, heads
    )
    blocks = query_block.shape[0]
    value_window = windows(value_pad, blocks).reshape(blocks, 3 * BLOCK, heads, HEAD_DIM)
    grad_block = grad_run.reshape(blocks, BLOCK, heads, HEAD_DIM)
    from_values = jnp.einsum("bihd,bjhd->hijb", grad_block, value_window, precision=highest)
    rest_block = rest_run.reshape(blocks, BLOCK, heads).transpose(2, 1, 0)[:, :, None, :]
    grad_scores = weights * (from_values - 2**height * rest_block)
    grad_query = jnp.einsum("hijb,bjhd->bihd", grad_scores, key_window, precision=highest) * factor
    grad_key = unwindow(
        jnp.einsum("hijb,bihd->bjhd", grad_scores, query_block, precision=highest) * factor, blocks
    )
    grad_value = unwindow(
        jnp.einsum("hijb,bihd->bjhd", weights, grad_block, precision=highest), blocks
    )
    return (grad_query.reshape(blocks * BLOCK, heads * HEAD_DIM), grad_key, grad_value)


def attend(queries, keys, values, labels, parity, heads):
    levels = build_levels(queries, keys, values, labels)
    edge_pairs = jnp.stack(
        [jnp.stack([pick_edge(entry[1], parity), pick_edge(entry[2], parity)]) for entry in levels]
    )
    edge_labels = jnp.stack([pick_edge(entry[3], parity) for entry in levels])
    arrived_pairs, arrived_labels = (
        swapped(edge_pairs.astype(jnp.bfloat16), "span", 0).astype(edge_pairs.dtype),
        swapped(edge_labels, "span", 0),
    )
    totals = None
    numerators = None
    for height in reversed(range(len(levels))):
        query_coarse, key_coarse, value_coarse, label_coarse = levels[height]
        key_pad = extend(key_coarse, arrived_pairs[height, 0], parity)
        value_pad = extend(value_coarse, arrived_pairs[height, 1], parity)
        label_pad = extend(label_coarse, arrived_labels[height], parity)
        level_total, numerator = level_forward(
            height, query_coarse, key_pad, value_pad, label_coarse, label_pad, heads
        )
        if totals is None:
            totals, numerators = (level_total, numerator)
        else:
            totals = spread_up(totals) + level_total
            numerators = spread_up(numerators) + numerator
    span_rows = queries.shape[0]
    output = (numerators.reshape(span_rows, heads, HEAD_DIM) / totals[:, :, None]).reshape(
        span_rows, heads * HEAD_DIM
    )
    return (output, totals, (arrived_pairs, arrived_labels))


def attend_back(queries, keys, values, labels, arrived, output, totals, grad_out, parity, heads):
    arrived_pairs, arrived_labels = arrived
    span_rows = queries.shape[0]
    grad_heads = grad_out.astype(jnp.float32).reshape(span_rows, heads, HEAD_DIM)
    grad_run = (grad_heads / totals[:, :, None]).reshape(span_rows, heads * HEAD_DIM)
    rest_run = jnp.sum(output.reshape(span_rows, heads, HEAD_DIM) * grad_heads, axis=-1) / totals
    levels = build_levels(queries, keys, values, labels)
    query_grads, key_grads, value_grads, key_edges, value_edges = ([], [], [], [], [])
    for height in range(len(levels)):
        if height > 0:
            grad_run = pair_sum(grad_run)
            rest_run = pair_sum(rest_run)
        query_coarse, key_coarse, value_coarse, label_coarse = levels[height]
        key_pad = extend(key_coarse, arrived_pairs[height, 0], parity)
        value_pad = extend(value_coarse, arrived_pairs[height, 1], parity)
        label_pad = extend(label_coarse, arrived_labels[height], parity)
        grad_query, grad_key, grad_value = level_backward(
            height,
            query_coarse,
            key_pad,
            value_pad,
            label_coarse,
            label_pad,
            grad_run,
            rest_run,
            heads,
        )
        query_grads.append(grad_query)
        key_grads.append(grad_key[BLOCK:-BLOCK])
        value_grads.append(grad_value[BLOCK:-BLOCK])
        key_edges.append(jnp.where(parity == 1, grad_key[:BLOCK], grad_key[-BLOCK:]))
        value_edges.append(jnp.where(parity == 1, grad_value[:BLOCK], grad_value[-BLOCK:]))
    sending = jnp.stack(
        [jnp.stack([key_edges[height], value_edges[height]]) for height in range(len(levels))]
    )
    returned = swapped(sending.astype(jnp.bfloat16), "span", 0).astype(sending.dtype)
    summed_query = None
    summed_key = None
    summed_value = None
    for height in reversed(range(len(levels))):
        extent = key_grads[height].shape[0]
        key_own = key_grads[height] + place_edge(returned[height, 0], extent, parity)
        value_own = value_grads[height] + place_edge(returned[height, 1], extent, parity)
        shrink = 0.5**height
        if summed_query is None:
            summed_query = query_grads[height] * shrink
            summed_key = key_own * shrink
            summed_value = value_own
        else:
            summed_query = spread_up(summed_query) + query_grads[height] * shrink
            summed_key = spread_up(summed_key) + key_own * shrink
            summed_value = spread_up(summed_value) + value_own
    return (summed_query, summed_key, summed_value)


def shards(
    tokens,
    segment_ids,
    first_gain,
    first_shift,
    project_weight,
    project_bias,
    output_weight,
    output_bias,
    second_gain,
    second_shift,
    expand_weight,
    expand_bias,
    reduce_weight,
    reduce_bias,
    cotangent,
):
    (
        gain_one,
        shift_one,
        proj_weight,
        proj_bias,
        out_weight,
        out_bias,
        gain_two,
        shift_two,
        up_weight,
        up_bias,
        down_weight,
        down_bias,
    ) = (
        lax.all_gather(
            first_gain.astype(jnp.bfloat16), ("head", "span"), axis=0, tiled=True
        ).astype(first_gain.dtype),
        lax.all_gather(
            first_shift.astype(jnp.bfloat16), ("head", "span"), axis=0, tiled=True
        ).astype(first_shift.dtype),
        lax.all_gather(project_weight, ("head", "span"), axis=1, tiled=True),
        lax.all_gather(
            project_bias.astype(jnp.bfloat16), ("head", "span"), axis=1, tiled=True
        ).astype(project_bias.dtype),
        lax.all_gather(output_weight, ("head", "span"), axis=0, tiled=True),
        lax.all_gather(
            output_bias.astype(jnp.bfloat16), ("head", "span"), axis=0, tiled=True
        ).astype(output_bias.dtype),
        lax.all_gather(
            second_gain.astype(jnp.bfloat16), ("head", "span"), axis=0, tiled=True
        ).astype(second_gain.dtype),
        lax.all_gather(
            second_shift.astype(jnp.bfloat16), ("head", "span"), axis=0, tiled=True
        ).astype(second_shift.dtype),
        lax.all_gather(expand_weight, ("head", "span"), axis=0, tiled=True),
        lax.all_gather(
            expand_bias.astype(jnp.bfloat16), ("head", "span"), axis=0, tiled=True
        ).astype(expand_bias.dtype),
        lax.all_gather(reduce_weight, ("head", "span"), axis=0, tiled=True),
        lax.all_gather(
            reduce_bias.astype(jnp.bfloat16), ("head", "span"), axis=0, tiled=True
        ).astype(reduce_bias.dtype),
    )
    tok_rows = tokens.shape[1]
    breadth = tokens.shape[2]
    head_count = lax.axis_size("head")
    local_heads = HEADS // head_count
    group_width = breadth // head_count
    span_rows = tok_rows * head_count
    head_place = lax.axis_index("head")
    parity = lax.axis_index("span") % 2
    inputs = tokens[0].astype(jnp.float32)
    normed_one, inverse_one = normalize(inputs)
    act_one = (normed_one * gain_one + shift_one).astype(jnp.bfloat16)
    labels = segment_ids[0]
    part_weight = lax.dynamic_slice_in_dim(proj_weight, head_place * group_width, group_width, 2)
    part_bias = lax.dynamic_slice_in_dim(proj_bias, head_place * group_width, group_width, 1)
    act_rows = lax.all_gather(act_one, "head", axis=0, tiled=True)
    projected = (
        jnp.einsum("td,cde->cte", act_rows, part_weight, preferred_element_type=jnp.float32)
        + part_bias[:, None, :]
    )
    qkv = projected.astype(jnp.bfloat16)
    output, totals, arrived = attend(qkv[0], qkv[1], qkv[2], labels, parity, local_heads)
    output_low = output.astype(jnp.bfloat16)
    mixed = lax.all_to_all(
        output_low.reshape(head_count, tok_rows, group_width),
        "head",
        split_axis=0,
        concat_axis=2,
        tiled=True,
    ).reshape(tok_rows, breadth)
    attn_out = jnp.dot(mixed, out_weight, preferred_element_type=jnp.float32) + out_bias
    hidden_one = inputs + attn_out
    normed_two, inverse_two = normalize(hidden_one)
    act_two = (normed_two * gain_two + shift_two).astype(jnp.bfloat16)
    pre_up = jnp.dot(act_two, up_weight, preferred_element_type=jnp.float32) + up_bias
    activated, gelu_back = jax.vjp(jax.nn.gelu, pre_up)
    act_up = activated.astype(jnp.bfloat16)
    result = (
        hidden_one + jnp.dot(act_up, down_weight, preferred_element_type=jnp.float32) + down_bias
    )
    grad_y = cotangent[0]
    grad_down_w = jnp.dot(act_up.T, grad_y, preferred_element_type=jnp.float32)
    grad_down_b = jnp.sum(grad_y.astype(jnp.float32), axis=0)
    grad_act = jnp.dot(grad_y, down_weight.T, preferred_element_type=jnp.float32)
    grad_pre = gelu_back(grad_act)[0].astype(jnp.bfloat16)
    grad_up_w = jnp.dot(act_two.T, grad_pre, preferred_element_type=jnp.float32)
    grad_up_b = jnp.sum(grad_pre.astype(jnp.float32), axis=0)
    grad_norm_two = jnp.dot(grad_pre, up_weight.T, preferred_element_type=jnp.float32)
    grad_gain_two = jnp.sum(grad_norm_two * normed_two, axis=0)
    grad_shift_two = jnp.sum(grad_norm_two, axis=0)
    grad_hidden = grad_y.astype(jnp.float32) + norm_backward(
        grad_norm_two, normed_two, inverse_two, gain_two
    )
    grad_branch = grad_hidden.astype(jnp.bfloat16)
    grad_out_w = jnp.dot(mixed.T, grad_branch, preferred_element_type=jnp.float32)
    grad_out_b = jnp.sum(grad_branch.astype(jnp.float32), axis=0)
    grad_mixed = jnp.dot(grad_branch, out_weight.T, preferred_element_type=jnp.float32).astype(
        jnp.bfloat16
    )
    grad_attn = lax.all_to_all(
        grad_mixed.reshape(1, tok_rows, breadth), "head", split_axis=2, concat_axis=0, tiled=True
    ).reshape(span_rows, group_width)
    grad_query, grad_key, grad_value = attend_back(
        qkv[0], qkv[1], qkv[2], labels, arrived, output, totals, grad_attn, parity, local_heads
    )
    grad_qkv = jnp.stack([grad_query, grad_key, grad_value]).astype(jnp.bfloat16)
    grad_part_w = jnp.einsum("td,cte->cde", act_rows, grad_qkv, preferred_element_type=jnp.float32)
    grad_part_b = jnp.sum(grad_qkv.astype(jnp.float32), axis=1)
    grad_proj_w = lax.dynamic_update_slice_in_dim(
        jnp.zeros((3, breadth, breadth), jnp.float32), grad_part_w, head_place * group_width, 2
    )
    grad_proj_b = lax.dynamic_update_slice_in_dim(
        jnp.zeros((3, breadth), jnp.float32), grad_part_b, head_place * group_width, 1
    )
    grad_norm_one = lax.psum_scatter(
        jnp.einsum("cte,cde->td", grad_qkv, part_weight, preferred_element_type=jnp.float32).astype(
            jnp.bfloat16
        ),
        "head",
        scatter_dimension=0,
        tiled=True,
    ).astype(jnp.float32)
    grad_gain_one = jnp.sum(grad_norm_one * normed_one, axis=0)
    grad_shift_one = jnp.sum(grad_norm_one, axis=0)
    grad_input = grad_hidden + norm_backward(grad_norm_one, normed_one, inverse_one, gain_one)
    dense_grads = (
        lax.psum_scatter(grad_gain_one, ("head", "span"), scatter_dimension=0, tiled=True),
        lax.psum_scatter(grad_shift_one, ("head", "span"), scatter_dimension=0, tiled=True),
        lax.psum_scatter(grad_proj_w, ("head", "span"), scatter_dimension=1, tiled=True),
        lax.psum_scatter(grad_proj_b, ("head", "span"), scatter_dimension=1, tiled=True),
        lax.psum_scatter(grad_out_w, ("head", "span"), scatter_dimension=0, tiled=True),
        lax.psum_scatter(grad_out_b, ("head", "span"), scatter_dimension=0, tiled=True),
        lax.psum_scatter(grad_gain_two, ("head", "span"), scatter_dimension=0, tiled=True),
        lax.psum_scatter(grad_shift_two, ("head", "span"), scatter_dimension=0, tiled=True),
        lax.psum_scatter(grad_up_w, ("head", "span"), scatter_dimension=0, tiled=True),
        lax.psum_scatter(grad_up_b, ("head", "span"), scatter_dimension=0, tiled=True),
        lax.psum_scatter(grad_down_w, ("head", "span"), scatter_dimension=0, tiled=True),
        lax.psum_scatter(grad_down_b, ("head", "span"), scatter_dimension=0, tiled=True),
    )
    return (
        result.astype(jnp.bfloat16)[None],
        grad_input.astype(jnp.bfloat16)[None],
        dense_grads[0],
        dense_grads[1],
        dense_grads[2],
        dense_grads[3],
        dense_grads[4],
        dense_grads[5],
        dense_grads[6],
        dense_grads[7],
        dense_grads[8],
        dense_grads[9],
        dense_grads[10],
        dense_grads[11],
    )


def solution(mesh):
    return jax.shard_map(
        shards,
        mesh=mesh,
        in_specs=(
            P("span", "head", None),
            P("span", None),
            P(("head", "span")),
            P(("head", "span")),
            P(None, ("head", "span"), None),
            P(None, ("head", "span")),
            P(("head", "span"), None),
            P(("head", "span")),
            P(("head", "span")),
            P(("head", "span")),
            P(("head", "span"), None),
            P(("head", "span")),
            P(("head", "span"), None),
            P(("head", "span")),
            P("span", "head", None),
        ),
        out_specs=(
            P("span", "head", None),
            P("span", "head", None),
            P(("head", "span")),
            P(("head", "span")),
            P(None, ("head", "span"), None),
            P(None, ("head", "span")),
            P(("head", "span"), None),
            P(("head", "span")),
            P(("head", "span")),
            P(("head", "span")),
            P(("head", "span"), None),
            P(("head", "span")),
            P(("head", "span"), None),
            P(("head", "span")),
        ),
        check_vma=False,
    )
```

profile of v0, /device:TPU:0, one launch (start us, length us, event | category | flops | bytes accessed | tf_op | source)
XLA Modules:
  0.0 2071.2 jit_solution(9146165787959422954)
XLA Ops:
  14.1 42.3 %all-reduce.101 = (bf16[512]{0:T(512)(128)(2,1)S(1)}, bf16[512]{0:T(512)(128)(2,1)S(1)}, bf16[512]{0:T(512)(128)(2,1)}, bf16[512]{0:T(512)(128)(2,1)}, bf16[512]...) all-reduce(bf16[512]{0:T(512)(128)(2,1)S(1)} %dynamic-update-slice., ...), channel_id=1, replica_groups=mesh['head'=4,'span'=8] {'head','span'}, use_global_device_ids=true, to_apply=%add.87 | all-reduce | flops 5120 | bytes 20480
  72.1 41.6 %all-gather = bf16[32,16,3]{1,2,0:T(4,128)(2,1)S(1)} all-gather(bf16[1,16,3]{1,2,0:T(4,128)(2,1)S(1)} %convert_bitcast_fusion.4), channel_id=1, replica_groups=mesh['head'=4,'span'=8] {'head','span'}, dimensions={0}, use_global_device_ids=true | all-gather | bytes 3168 | tf_op jit(solution)/shard_map/all_gather | solution.py:286
  126.8 23.9 %all-gather.8.cloned.1.call-done = bf16[4096,512]{1,0:T(8,128)(2,1)} async-done(((bf16[1024,512]{1,0:T(8,128)(2,1)}), bf16[4096,512]{1,0:T(8,128)(2,1)}) %all-gather.8.cloned.1.call-update) | async-done | bytes 4194320 | tf_op jit(solution)/shard_map/all_gather | solution.py:322
  167.8 8.6 reduce_sum.588
  178.3 10.0 reduce_sum.589
  245.5 10.0 reduce_sum.616
  451.4 9.1 pad_maximum_fusion.1
  476.7 5.8 concatenate.509
  509.8 12.6 fusion.370
  541.4 7.1 fusion.82
  573.5 14.4 fusion.371
  587.9 14.6 fusion.40
  614.9 6.3 copy.1679
  653.1 56.8 %all_gather.44 = bf16[512,512]{1,0:T(8,128)(2,1)} all-gather(bf16[16,512]{1,0:T(8,128)(2,1)S(1)} %copy-done.217), channel_id=1, replica_groups=mesh['head'=4,'span'=8] {'head','span'}, dimensions={0}, use_global_device_ids=true | all-gather | bytes 540672 | tf_op jit(solution)/shard_map/all_gather | solution.py:289
  714.1 7.6 fusion.358
  721.7 10.7 convert_reduce_fusion
  742.4 6.8 reduce.70
  754.7 6.1 reshape.2174
  770.5 6.3 copy.1689
  780.7 10.1 div.197.clone
  790.9 6.4 div.204
  814.5 15.4 copy.1844
  848.2 10.4 broadcast_divide_fusion
  858.7 24.6 %fusion.16 = f32[2,16,48,256]{2,1,3,0:T(8,128)S(1)} fusion(f32[2,16,48,256]{2,1,3,0:T(8,128)S(1)} %copy-done.2, f32[2,16,256]{1,2,0:T(8,128)S(1)} %get-tuple-element.54, f32[256,16,2,64]{3,2,1,0:T(2,128)S(1)} %broadcast_divide_fusion, f32[256,48,2,64]{3,1,2,0:T(8,128)} %copy-done), kind=kOutput, calls=%fused_computation.27 | convolution fusion | flops 302776320 | bytes 11567104 | tf_op jit(solution)/shard_map/bihd,bjhd->hijb/dot_general | solution.py:148
  883.3 12.7 multiply_bitcast_fusion.2
  896.0 12.8 multiply_bitcast_fusion
  908.9 12.9 divide_reduce_fusion
  924.4 12.8 fusion.57
  937.3 6.9 multiply_bitcast_fusion.4
  944.2 12.0 multiply_bitcast_fusion.1
  962.4 6.7 fusion.116
  1095.6 6.7 convolution_bitcast_fusion.2
  1116.6 12.4 convolution_bitcast_fusion.1
  1129.0 10.8 copy.1742
  1160.6 23.2 %convolution_bitcast_fusion = f32[256,48,2,64]{3,1,2,0:T(8,128)} fusion(f32[256,16,2,64]{3,2,1,0:T(2,128)S(1)} %copy-done.5, f32[2,16,48,256]{2,1,3,0:T(8,128)S(1)} %copy-done.3), kind=kOutput, calls=%fused_computation.25 | convolution fusion | flops 301989888 | bytes 9961472 | tf_op jit(solution)/shard_map/hijb,bihd->bjhd/dot_general | solution.py:156
  1183.9 10.8 copy.1748
  1194.7 5.7 fusion.360
  1254.7 6.4 copy.1737
  1320.9 7.4 fusion.357
  1329.5 9.6 fusion.181
  1339.8 8.9 fusion.99
  1348.7 85.8 %reduce-scatter.19.cloned.1.call-done = f32[16,3]{1,0:T(8,128)} async-done(((f32[512,3]{1,0:T(8,128)}), f32[16,3]{1,0:T(8,128)}) %reduce-scatter.19.cloned.1.call-update) | async-done | bytes 208
  1435.8 73.6 %reduce-scatter.9.cloned.1.call-done = bf16[1024,512]{1,0:T(8,128)(2,1)} async-done(((bf16[4096,512]{1,0:T(8,128)(2,1)}), bf16[1024,512]{1,0:T(8,128)(2,1)}) %reduce-scatter.9.cloned.1.call-update) | async-done | bytes 1048592 | tf_op jit(solution)/shard_map/reduce_scatter | solution.py:381
  1512.0 41.2 %all-reduce.100 = (f32[512]{0:T(512)S(1)}, f32[512]{0:T(512)S(1)}, f32[512]{0:T(512)S(1)}, f32[512]{0:T(512)S(1)}, f32[512]{0:T(512)S(1)}, /*index=5*/f32[2048]{0:T(1024)S(1)}, f32[512]{0:T(512)S(1)}) all-reduce(f32[512]{0:T(512)S(1)} %get-tuple-element.16, ...), channel_id=3, replica_groups=mesh['head'=4,'span'=8] {'head','span'}, use_global_device_ids=true, to_apply=%region_60.61.clone | all-reduce | flops 5120 | bytes 40960
  1560.0 87.6 %reduce-scatter.13.cloned.1.call-done = f32[16,512]{1,0:T(8,128)} async-done(((f32[512,512]{1,0:T(8,128)}), f32[16,512]{1,0:T(8,128)}) %reduce-scatter.13.cloned.1.call-update) | async-done | bytes 32784 | tf_op jit(solution)/shard_map/reduce_scatter | solution.py:397
  1647.6 137.5 %reduce-scatter.11.cloned.1.call-done = f32[3,16,512]{2,1,0:T(8,128)} async-done(((f32[3,512,512]{2,1,0:T(8,128)}), f32[3,16,512]{2,1,0:T(8,128)}) %reduce-scatter.11.cloned.1.call-update) | async-done | bytes 98320 | tf_op jit(solution)/shard_map/reduce_scatter | solution.py:395
  1785.2 139.5 %reduce-scatter.15.cloned.1.call-done = f32[16,2048]{1,0:T(8,128)} async-done(((f32[512,2048]{1,0:T(8,128)}), f32[16,2048]{1,0:T(8,128)}) %reduce-scatter.15.cloned.1.call-update) | async-done | bytes 131088 | tf_op jit(solution)/shard_map/reduce_scatter | solution.py:401
  1924.7 139.4 %reduce-scatter.17.cloned.1.call-done = f32[64,512]{1,0:T(8,128)} async-done(((f32[2048,512]{1,0:T(8,128)}), f32[64,512]{1,0:T(8,128)}) %reduce-scatter.17.cloned.1.call-update) | async-done | bytes 131088 | tf_op jit(solution)/shard_map/reduce_scatter | solution.py:403
  (1334 shorter events, 801.6 us)
Async XLA Ops:
  7.2 53.0 %copy-start.12 = (bf16[1,1024,512]{2,1,0:T(8,128)(2,1)S(1)}, bf16[1,1024,512]{2,1,0:T(8,128)(2,1)}, u32[]{:S(2)}) copy-start(bf16[1,1024,512]{2,1,0:T(8,128)(2,1)} %param.15) | copy-start | bytes 3145732
  7.2 119.6 %all-gather.6.cloned.1.call-start = ((), (), s32[]{:S(2)}) async-start(), calls=%async_computation.8 | async-start | bytes 1622016 | tf_op jit(solution)/shard_map/all_gather | solution.py:285
  7.9 142.8 %all-gather.8.cloned.1.call-start = ((), (), s32[]{:S(2)}) async-start(), calls=%async_computation.9 | async-start | bytes 5242880 | tf_op jit(solution)/shard_map/all_gather | solution.py:322
  61.6 652.5 %all-gather.10.cloned.1.call-start = ((), (), s32[]{:S(2)}) async-start(), calls=%async_computation.10 | async-start | bytes 2162688 | tf_op jit(solution)/shard_map/all_gather | solution.py:299
  62.3 659.4 %all-gather.12.cloned.1.call-start = ((), (), s32[]{:S(2)}) async-start(), calls=%async_computation.11 | async-start | bytes 2162688 | tf_op jit(solution)/shard_map/all_gather | solution.py:303
  70.8 43.5 %collective-permute-start.1 = (s32[9,16]{1,0:T(8,128)S(1)}, s32[9,16]{1,0:T(8,128)S(1)}, u32[]{:S(2)}, u32[]{:S(2)}) collective-permute-start(s32[9,16]{1,0:T(8,128)S(1)} %stack.313), channel_id=1, source_target_pairs={{0,1},{1,0},{2,3},{3,2},{4,5},{5,4},{6,7},{7,6},{8,9},{9,8},{10,11... | collective-permute-start | bytes 1736 | tf_op jit(solution)/shard_map/ppermute | solution.py:18
  242.6 97.5 %collective-permute-start = (bf16[9,2,16,128]{3,2,1,0:T(8,128)(2,1)}, bf16[9,2,16,128]{3,2,1,0:T(8,128)(2,1)}, u32[]{:S(2)}, u32[]{:S(2)}) collective-permute-start(bf16[9,2,16,128]{3,2,1,0:T(8,128)(2,1)} %constant_dynamic-update-slice_fusion), channel_id=1, source_target_pairs={{0,1},{1,0},{2,3},{3,2},{4,5},{5,4},{6,7},{7,6},{8,9},{9,8},{10,11... | collective-permute-start | bytes 221192 | tf_op jit(solution)/shard_map/ppermute | solution.py:18
  409.7 28.4 %copy-start.116 = (f32[128,128]{1,0:T(8,128)S(1)}, f32[128,128]{1,0:T(8,128)}, u32[]{:S(2)}) copy-start(f32[128,128]{1,0:T(8,128)} %reduce_sum.603) | copy-start | bytes 196612
  410.4 21.5 %copy-start.135 = (f32[64,128]{1,0:T(8,128)S(1)}, f32[64,128]{1,0:T(8,128)}, u32[]{:S(2)}) copy-start(f32[64,128]{1,0:T(8,128)} %reduce_sum.608) | copy-start | bytes 98308
  412.3 23.2 %copy-start.158 = (f32[16,128]{0,1:T(8,128)S(1)}, f32[16,128]{0,1:T(8,128)}, u32[]{:S(2)}) copy-start(f32[16,128]{0,1:T(8,128)} %get-tuple-element.128) | copy-start | bytes 24580
  412.3 23.3 %copy-start.160 = (f32[16,128]{0,1:T(8,128)S(1)}, f32[16,128]{0,1:T(8,128)}, u32[]{:S(2)}) copy-start(f32[16,128]{0,1:T(8,128)} %get-tuple-element.104) | copy-start | bytes 24580
  412.3 25.7 %copy-start.157 = (f32[16,128]{0,1:T(8,128)S(1)}, f32[16,128]{0,1:T(8,128)}, u32[]{:S(2)}) copy-start(f32[16,128]{0,1:T(8,128)} %get-tuple-element.127) | copy-start | bytes 24580
  412.3 25.7 %copy-start.159 = (f32[16,128]{0,1:T(8,128)S(1)}, f32[16,128]{0,1:T(8,128)}, u32[]{:S(2)}) copy-start(f32[16,128]{0,1:T(8,128)} %get-tuple-element.105) | copy-start | bytes 24580
  537.8 22.9 %copy-start.105 = (f32[2,16,48,8]{2,1,3,0:T(8,128)}, f32[2,16,48,8]{2,1,3,0:T(8,128)S(1)}, u32[]{:S(2)}) copy-start(f32[2,16,48,8]{2,1,3,0:T(8,128)S(1)} %get-tuple-element.260) | copy-start | bytes 147460
  539.0 20.7 %copy-start.125 = (f32[2,16,48,4]{2,1,3,0:T(8,128)}, f32[2,16,48,4]{2,1,3,0:T(8,128)S(1)}, u32[]{:S(2)}) copy-start(f32[2,16,48,4]{2,1,3,0:T(8,128)S(1)} %get-tuple-element.258) | copy-start | bytes 73732
  541.4 20.4 slice-start
  566.7 21.1 %copy-start = (f32[256,48,2,64]{3,1,2,0:T(8,128)}, f32[256,48,2,64]{3,1,2,0:T(8,128)S(1)}, u32[]{:S(2)}) copy-start(f32[256,48,2,64]{3,1,2,0:T(8,128)S(1)} %copy_dynamic-update-slice_fusion.3) | copy-start | bytes 18874372
  649.2 62.1 %copy-start.13 = (bf16[1,1024,512]{2,1,0:T(8,128)(2,1)S(1)}, bf16[1,1024,512]{2,1,0:T(8,128)(2,1)}, u32[]{:S(2)}) copy-start(bf16[1,1024,512]{2,1,0:T(8,128)(2,1)} %param.15) | copy-start | bytes 3145732
  649.3 60.6 %all-to-all-start = ((bf16[4,1024,128]{2,1,0:T(8,128)(2,1)}), bf16[4,1024,128]{2,1,0:T(8,128)(2,1)S(1)}, u32[]{:S(2)}, u32[]{:S(2)}) async-start(bf16[4,1024,128]{2,1,0:T(8,128)(2,1)} %fusion.59), calls=%async_computation | async-start | bytes 2097152 | tf_op jit(solution)/shard_map/all_to_all | solution.py:330
  653.0 82.9 %copy-start.213 = (f32[512]{0:T(512)}, f32[512]{0:T(512)S(1)}, u32[]{:S(2)}) copy-start(f32[512]{0:T(512)S(1)} %convert_element_type.362) | copy-start | bytes 6148
  653.0 61.1 %copy-start.215 = (f32[512]{0:T(512)}, f32[512]{0:T(512)S(1)}, u32[]{:S(2)}) copy-start(f32[512]{0:T(512)S(1)} %convert_element_type.364) | copy-start | bytes 6148
  653.0 68.7 %copy-start.221 = (f32[2048]{0:T(1024)}, f32[2048]{0:T(1024)S(1)}, u32[]{:S(2)}) copy-start(f32[2048]{0:T(1024)S(1)} %convert_element_type.367) | copy-start | bytes 24580
  713.6 22.3 %copy-start.11 = (f32[1024,512]{1,0:T(8,128)}, f32[1024,512]{1,0:T(8,128)S(1)}, u32[]{:S(2)}) copy-start(f32[1024,512]{1,0:T(8,128)S(1)} %get-tuple-element.272) | copy-start | bytes 6291460
  713.6 22.3 %copy-start.175 = (f32[1024]{0:T(1024)}, f32[1024]{0:T(1024)S(1)}, u32[]{:S(2)}) copy-start(f32[1024]{0:T(1024)S(1)} %broadcast_multiply_fusion.23) | copy-start | bytes 12292
  714.0 21.8 %copy-start.178 = (f32[1024]{0:T(1024)}, f32[1024]{0:T(1024)S(1)}, u32[]{:S(2)}) copy-start(f32[1024]{0:T(1024)S(1)} %add_rsqrt_fusion) | copy-start | bytes 12292
  751.2 46.1 %all-to-all-start.1 = ((bf16[4,2,65536]{2,1,0:T(2,128)(2,1)}), bf16[4,2,65536]{2,1,0:T(2,128)(2,1)S(1)}, u32[]{:S(2)}, u32[]{:S(2)}) async-start(bf16[4,2,65536]{2,1,0:T(2,128)(2,1)} %reshape.2326), calls=%async_computation.1 | async-start | bytes 2097152 | tf_op jit(solution)/shard_map/all_to_all | solution.py:366
  754.7 679.8 %reduce-scatter.19.cloned.1.call-start = ((), (), s32[]{:S(2)}) async-start(), calls=%async_computation.17 | async-start | bytes 270336
  804.7 39.8 %copy-start.19 = (f32[4,1,1024,128]{3,2,0,1:T(8,128)}, f32[4,1,1024,128]{3,2,0,1:T(8,128)S(1)}, u32[]{:S(2)}) copy-start(f32[4,1,1024,128]{3,2,0,1:T(8,128)S(1)} %copy.1685) | copy-start | bytes 6291460
  848.2 35.1 %slice-start.6 = ((s8[12582912]{0:T(1024)(128)(4,1)}), s8[4194304]{0:T(1024)(128)(4,1)S(1)}, s32[]{:S(2)}) async-start(s8[12582912]{0:T(1024)(128)(4,1)} %bitcast.1070), calls=%async_computation.24 | async-start | bytes 8388608
  858.7 24.6 %copy-start.4 = (f32[256,16,2,64]{3,2,1,0:T(2,128)}, f32[256,16,2,64]{3,2,1,0:T(2,128)S(1)}, u32[]{:S(2)}) copy-start(f32[256,16,2,64]{3,2,1,0:T(2,128)S(1)} %broadcast_divide_fusion) | copy-start | bytes 6291460
  858.7 24.6 %slice-start.7 = ((s8[12582912]{0:T(1024)(128)(4,1)}), s8[4194304]{0:T(1024)(128)(4,1)S(1)}, s32[]{:S(2)}) async-start(s8[12582912]{0:T(1024)(128)(4,1)} %bitcast.1070), calls=%async_computation.25 | async-start | bytes 8388608
  858.7 24.6 %slice-start.8 = ((s8[12582912]{0:T(1024)(128)(4,1)}), s8[4194304]{0:T(1024)(128)(4,1)S(1)}, s32[]{:S(2)}) async-start(s8[12582912]{0:T(1024)(128)(4,1)} %bitcast.1070), calls=%async_computation.26 | async-start | bytes 8388608
  908.9 28.3 %slice-start.11 = ((s8[6291456]{0:T(1024)(128)(4,1)}), s8[2097152]{0:T(1024)(128)(4,1)S(1)}, s32[]{:S(2)}) async-start(s8[6291456]{0:T(1024)(128)(4,1)} %bitcast.1074), calls=%async_computation.29 | async-start | bytes 4194304
  1285.5 4.8 collective-permute-start.2
  1300.4 209.0 %reduce-scatter.9.cloned.1.call-start = ((), (), s32[]{:S(2)}) async-start(), calls=%async_computation.12 | async-start | bytes 5242880 | tf_op jit(solution)/shard_map/reduce_scatter | solution.py:381
  1305.9 341.7 %reduce-scatter.13.cloned.1.call-start = ((), (), s32[]{:S(2)}) async-start(), calls=%async_computation.14 | async-start | bytes 1081344 | tf_op jit(solution)/shard_map/reduce_scatter | solution.py:397
  1310.4 474.8 %reduce-scatter.11.cloned.1.call-start = ((), (), s32[]{:S(2)}) async-start(), calls=%async_computation.13 | async-start | bytes 3244032 | tf_op jit(solution)/shard_map/reduce_scatter | solution.py:395
  1320.8 603.9 %reduce-scatter.15.cloned.1.call-start = ((), (), s32[]{:S(2)}) async-start(), calls=%async_computation.15 | async-start | bytes 4325376 | tf_op jit(solution)/shard_map/reduce_scatter | solution.py:401
  1328.3 735.8 %reduce-scatter.17.cloned.1.call-start = ((), (), s32[]{:S(2)}) async-start(), calls=%async_computation.16 | async-start | bytes 4325376 | tf_op jit(solution)/shard_map/reduce_scatter | solution.py:403
  1339.7 169.7 %copy-start.14 = (bf16[1,1024,512]{2,1,0:T(8,128)(2,1)S(1)}, bf16[1,1024,512]{2,1,0:T(8,128)(2,1)}, u32[]{:S(2)}) copy-start(bf16[1,1024,512]{2,1,0:T(8,128)(2,1)} %param.15) | copy-start | bytes 3145732
  1339.8 169.7 %copy-start.194 = (f32[1024]{0:T(1024)S(1)}, f32[1024]{0:T(1024)}, u32[]{:S(2)}) copy-start(f32[1024]{0:T(1024)} %copy-done.193) | copy-start | bytes 12292
  1339.8 169.7 %copy-start.198 = (f32[1024]{0:T(1024)S(1)}, f32[1024]{0:T(1024)}, u32[]{:S(2)}) copy-start(f32[1024]{0:T(1024)} %copy-done.197) | copy-start | bytes 12292
  1339.8 169.7 %copy-start.212 = (f32[512]{0:T(512)S(1)}, f32[512]{0:T(512)}, u32[]{:S(2)}) copy-start(f32[512]{0:T(512)} %copy-done.211) | copy-start | bytes 6148
  1348.6 163.3 %copy-start.223 = (f32[2048]{0:T(1024)S(1)}, f32[2048]{0:T(1024)}, u32[]{:S(2)}) copy-start(f32[2048]{0:T(1024)} %get-tuple-element.274) | copy-start | bytes 24580
  1348.6 163.3 %copy-start.224 = (f32[512]{0:T(512)S(1)}, f32[512]{0:T(512)}, u32[]{:S(2)}) copy-start(f32[512]{0:T(512)} %get-tuple-element.52) | copy-start | bytes 6148
  1348.7 163.3 %copy-start.225 = (f32[512]{0:T(512)S(1)}, f32[512]{0:T(512)}, u32[]{:S(2)}) copy-start(f32[512]{0:T(512)} %get-tuple-element.134) | copy-start | bytes 6148
  1348.7 163.3 %copy-start.227 = (f32[512]{0:T(512)S(1)}, f32[512]{0:T(512)}, u32[]{:S(2)}) copy-start(f32[512]{0:T(512)} %get-tuple-element.14) | copy-start | bytes 6148
  1348.7 163.3 %copy-start.228 = (f32[512]{0:T(512)S(1)}, f32[512]{0:T(512)}, u32[]{:S(2)}) copy-start(f32[512]{0:T(512)} %get-tuple-element.19) | copy-start | bytes 6148
  (217 other events, 1109.4 us)
Sparse Core Ops, SparseCore 0:
  10.9 57.6 all-gather.5
  70.8 79.8 all-gather.7
  153.5 54.7 all-gather.9
  211.1 55.2 all-gather.11
  1300.5 133.8 reduce-scatter.18
  1436.7 72.6 reduce-scatter.8
  1512.2 135.3 reduce-scatter.12
  1650.6 134.5 reduce-scatter.10
  1788.0 136.5 reduce-scatter.14
  1927.4 136.7 reduce-scatter.16
where the time goes:
time: 2090 us; the launch traced here: 2070 us
  waiting for transfers between devices  689 us (33%)
  local copies, waits for them, and re-layouts  569 us (27%)
  matrix products  333 us (16%)
  other arithmetic  271 us (13%)
  blocking collectives  182 us (9%)
    reduce_scatter x1, waiting for transfers between devices, shards(): lax.psum_scatter(grad_up_w, ('head', 'span'), scatter_dimension=0, tiled=...  139 us
    reduce_scatter x1, waiting for transfers between devices, shards(): lax.psum_scatter(grad_down_w, ('head', 'span'), scatter_dimension=0, tile...  139 us
    reduce_scatter x1, waiting for transfers between devices, shards(): lax.psum_scatter(grad_proj_w, ('head', 'span'), scatter_dimension=1, tile...  138 us
    unnamed x573, local copies, waits for them, and re-layouts  109 us
    reduce_sum x40, other arithmetic, pair_sum(): values_in.reshape((values_in.shape[0] // 2, 2) + values_in.shape[1:])  94.5 us
    concatenate x57, local copies, waits for them, and re-layouts, windows(): return jnp.concatenate([shaped[:-2], shaped[1:-1], shaped[2:]], axis=1)  89.8 us
    reduce_scatter x1, waiting for transfers between devices, shards(): lax.psum_scatter(grad_out_w, ('head', 'span'), scatter_dimension=0, tiled...  87.6 us
    unnamed x11, waiting for transfers between devices  87.3 us
  transfers between devices with their start and end apart: 15, of which 7 were waited for; matrix products, arithmetic and copies ran while one was open for 30% of the time, Pallas kernels for 0%

commit v1 on v0

v1 whole, which is shorter than its diff:
```python
import functools
import jax
import jax.numpy as jnp
from jax import lax
from jax.experimental import pallas as pl
from jax.experimental.pallas import tpu as pltpu
from jax.sharding import PartitionSpec as P

F32, BF16, I32 = jnp.float32, jnp.bfloat16, jnp.int32
MESH = pl.DeviceIdType.MESH
VMEM = pltpu.VMEM
NEG = -1e30
EPS = 1e-5
TOK = 1024
TILE = 256
D = 512
FF = 2048
EXT = 2384
LEVEL_SIZE = (1024, 512, 256, 128, 64, 32, 16)
COARSE_AT = (None, 0, 512, 768, 896, 960, 992)
EXT_AT = (0, 1056, 1600, 1888, 2048, 2144, 2208)
WIDE_AT = 2256
TRANS_B = (((1,), (1,)), ((), ()))
TRANS_A = (((0,), (0,)), ((), ()))


def mm(a, b):
    return jnp.dot(a, b, preferred_element_type=F32)


def mm_bt(a, b):
    return lax.dot_general(a, b, TRANS_B, preferred_element_type=F32)


def mm_at(a, b):
    return lax.dot_general(a, b, TRANS_A, preferred_element_type=F32)


def iota(shape, dim):
    return lax.broadcasted_iota(I32, shape, dim)


def split(v):
    high = v.astype(BF16)
    return high, (v - high.astype(F32)).astype(BF16)


def covers(t, c, block):
    if block == 0:
        return ((t & 255) >> 1) == c
    if block == 1:
        return ((t & 511) >> 2) == c
    if block == 2:
        return (t >> 3) == c
    level, start = mixed_levels(c)
    return (jnp.right_shift(t, level) == c - start) & (c < 124)


def mixed_levels(c):
    a, b, d, e = ((c >= edge).astype(I32) for edge in (64, 96, 112, 120))
    return 4 + a + b + d + e, 64 * a + 32 * b + 16 * d + 8 * e


def ones_where(cond):
    return jnp.where(cond, 1.0, 0.0).astype(BF16)


def identity(n):
    return ones_where(iota((n, n), 0) == iota((n, n), 1))


def fill_spread(spt):
    @pl.loop(0, TOK // TILE)
    def _(j):
        for block in range(4):
            t = iota((TILE, 128), 0) + j * TILE
            c = iota((TILE, 128), 1)
            spt[pl.ds(j * TILE, TILE), 128 * block:128 * block + 128] = ones_where(covers(t, c, block))


def fill_pool(sp):
    @pl.loop(0, TOK // TILE)
    def _(j):
        for block in range(4):
            t = iota((128, TILE), 1) + j * TILE
            c = iota((128, TILE), 0)
            sp[128 * block:128 * block + 128, pl.ds(pl.multiple_of(j * TILE, TILE), TILE)] = ones_where(covers(t, c, block))


def pre_kernel(tok, seg, weight, vecs, a1_out, fine, coarse, acc, acc_ids):
    j = pl.program_id(0)
    h = lax.axis_index("head")
    v = tok[...].astype(F32)
    center = v - jnp.mean(v, axis=-1, keepdims=True)
    inverse = lax.rsqrt(jnp.mean(center * center, axis=-1, keepdims=True) + EPS)
    a1 = (center * inverse * vecs[0:1, :] + vecs[1:2, :]).astype(BF16)
    a1_out[...] = a1
    for part in range(3):
        r = (mm(a1, weight[part]) + vecs[2 + part:3 + part, :]).astype(BF16)
        if part == 0:
            r = r * jnp.array(0.125, BF16)
        fine[:, D * part:D * part + D] = r
    ids = seg[:, pl.ds(pl.multiple_of(h * TOK + j * TILE, TILE), TILE)].astype(F32)
    ids_b = jnp.broadcast_to(ids, (128, TILE)).astype(BF16)
    sq_b = jnp.broadcast_to(ids * ids, (128, TILE)).astype(BF16)
    fine[:, 3 * D:3 * D + 128] = mm_bt(identity(TILE), ids_b).astype(BF16)
    c, t = iota((192, TILE), 0), iota((192, TILE), 1)
    near = ones_where(jnp.where(c < 128, t >> 1, (t >> 2) + 128) == c)
    x = fine[:, 0:3 * D]
    r = mm(near, x)
    lab = labels_of(mm_bt(near, ids_b), mm_bt(near, sq_b), jnp.where(iota((192, 128), 0) < 128, 2.0, 4.0))
    at1, at2 = pl.multiple_of(j * 128, 128), pl.multiple_of(512 + j * 64, 64)
    coarse[pl.ds(at1, 128), 0:2 * D] = (r[0:128, 0:2 * D] * 0.5).astype(BF16)
    coarse[pl.ds(at1, 128), 2 * D:3 * D] = r[0:128, 2 * D:].astype(BF16)
    coarse[pl.ds(at1, 128), 3 * D:] = lab[0:128].astype(BF16)
    coarse[pl.ds(at2, 64), 0:2 * D] = (r[128:192, 0:2 * D] * 0.25).astype(BF16)
    coarse[pl.ds(at2, 64), 2 * D:3 * D] = r[128:192, 2 * D:].astype(BF16)
    coarse[pl.ds(at2, 64), 3 * D:] = lab[128:192].astype(BF16)
    tt, cc = iota((128, TILE), 1) + j * TILE, iota((128, TILE), 0)
    far = jnp.concatenate([ones_where(covers(tt, cc, 2)), ones_where(covers(tt, cc, 3))], axis=0)

    @pl.when(j == 0)
    def _():
        acc[...] = jnp.zeros_like(acc)
        acc_ids[...] = jnp.zeros_like(acc_ids)
    acc[...] += mm(far, x)
    acc_ids[:, 0:128] += mm_bt(far, ids_b)
    acc_ids[:, 128:256] += mm_bt(far, sq_b)

    @pl.when(j == TOK // TILE - 1)
    def _():
        row = iota((TILE, 128), 0)
        level, _unused = mixed_levels(row - 128)
        times = jnp.where(row < 128, 8.0, (1 << level).astype(F32))
        lab = labels_of(acc_ids[:, 0:128], acc_ids[:, 128:256], times)
        shrink = 1.0 / times
        for k in range(8):
            coarse[768:1024, 128 * k:128 * k + 128] = (acc[:, 128 * k:128 * k + 128] * shrink).astype(BF16)
        coarse[768:1024, 2 * D:3 * D] = acc[:, 2 * D:].astype(BF16)
        coarse[768:1024, 3 * D:] = lab.astype(BF16)


def labels_of(total, squares, times):
    return jnp.where(times * squares == total * total, total / times, 0.0)


def before_attention(tok, seg, weight, vecs):
    wide = 3 * D + 128
    return pl.pallas_call(
        pre_kernel,
        grid=(TOK // TILE,),
        out_shape=[jax.ShapeDtypeStruct((TOK, D), BF16), jax.ShapeDtypeStruct((TOK, wide), BF16),
                   jax.ShapeDtypeStruct((TOK, wide), BF16)],
        in_specs=[pl.BlockSpec((TILE, D), lambda j: (j, 0)),
                  pl.BlockSpec(seg.shape, lambda j: (0, 0)),
                  pl.BlockSpec((3, D, D), lambda j: (0, 0, 0), pipeline_mode=pl.Buffered(1)),
                  pl.BlockSpec((16, D), lambda j: (0, 0))],
        out_specs=[pl.BlockSpec((TILE, D), lambda j: (j, 0)), pl.BlockSpec((TILE, wide), lambda j: (j, 0)),
                   pl.BlockSpec((TOK, wide), lambda j: (0, 0))],
        scratch_shapes=[VMEM((TILE, 3 * D), F32), VMEM((TILE, 256), F32)],
        compiler_params=pltpu.CompilerParams(dimension_semantics=("arbitrary",), vmem_limit_bytes=60 << 20),
        name="before_attention",
    )(tok, seg, weight, vecs)


def row_place():
    h, s = lax.axis_index("head"), lax.axis_index("span")
    return (s % 2) * 4 + h


def row_device(place):
    s = lax.axis_index("span")
    return {"head": place % 4, "span": (s // 2) * 2 + place // 4}


def greet(devices):
    barrier = pltpu.get_barrier_semaphore()
    for d in devices:
        pl.semaphore_signal(barrier, inc=1, device_id=d, device_id_type=MESH)
    pl.semaphore_wait(barrier, len(devices))


def rcopy(src, dst, send, recv, device):
    return pltpu.make_async_remote_copy(src_ref=src, dst_ref=dst, send_sem=send, recv_sem=recv,
                                        device_id=device, device_id_type=MESH)


def edges_kernel(fine, coarse, halo, wide, local, send, recv):
    p = row_place()
    others = [lax.rem(p + d, 8) for d in range(1, 8)]
    greet([row_device(o) for o in others])
    right, left = row_device(others[0]), row_device(others[6])
    lanes = pl.ds(D, 2 * D + 128)
    copies = []
    for l, size in enumerate(LEVEL_SIZE):
        src, at = (fine, 0) if l == 0 else (coarse, COARSE_AT[l])
        copies.append(rcopy(src.at[pl.ds(at + size - 16, 16), lanes], halo.at[0, l], send.at[l], recv.at[l], right))
        copies.append(rcopy(src.at[pl.ds(at, 16), lanes], halo.at[1, l], send.at[7 + l], recv.at[7 + l], left))
    block = coarse.at[pl.ds(1008, 16), lanes]
    for d in range(1, 8):
        copies.append(rcopy(block, wide.at[p], send.at[13 + d], recv.at[13 + d], row_device(others[d - 1])))
    for cp in copies:
        cp.start()
    own = pltpu.make_async_copy(block, wide.at[p], local)
    own.start()
    own.wait()
    for cp in copies:
        cp.wait()


def exchange_edges(fine, coarse):
    lanes = 2 * D + 128
    return pl.pallas_call(
        edges_kernel,
        out_shape=[jax.ShapeDtypeStruct((2, 7, 16, lanes), BF16), jax.ShapeDtypeStruct((8, 16, lanes), BF16)],
        in_specs=[pl.BlockSpec(memory_space=pl.ANY)] * 2,
        out_specs=[pl.BlockSpec(memory_space=pl.ANY)] * 2,
        scratch_shapes=[pltpu.SemaphoreType.DMA, pltpu.SemaphoreType.DMA((21,)), pltpu.SemaphoreType.DMA((21,))],
        compiler_params=pltpu.CompilerParams(collective_id=2, has_side_effects=True),
        name="exchange_edges",
    )(fine, coarse)


def edges_back_kernel(ext, halo, wide, local, send, recv):
    p = row_place()
    others = [lax.rem(p + d, 8) for d in range(1, 8)]
    greet([row_device(o) for o in others])
    right, left = row_device(others[0]), row_device(others[6])
    copies = []
    for l, size in enumerate(LEVEL_SIZE):
        at = EXT_AT[l]
        copies.append(rcopy(ext.at[:, pl.ds(at + 16 + size, 16)], halo.at[0, l], send.at[l], recv.at[l], right))
        copies.append(rcopy(ext.at[:, pl.ds(at, 16)], halo.at[1, l], send.at[7 + l], recv.at[7 + l], left))
    for d in range(1, 8):
        o = others[d - 1]
        copies.append(rcopy(ext.at[:, pl.ds(pl.multiple_of(WIDE_AT + 16 * o, 16), 16)], wide.at[p], send.at[13 + d], recv.at[13 + d], row_device(o)))
    for cp in copies:
        cp.start()
    own = pltpu.make_async_copy(ext.at[:, pl.ds(pl.multiple_of(WIDE_AT + 16 * p, 16), 16)], wide.at[p], local)
    own.start()
    own.wait()
    for cp in copies:
        cp.wait()


def return_edges(ext):
    return pl.pallas_call(
        edges_back_kernel,
        out_shape=[jax.ShapeDtypeStruct((2, 7, 2, 16, D), BF16), jax.ShapeDtypeStruct((8, 2, 16, D), BF16)],
        in_specs=[pl.BlockSpec(memory_space=pl.ANY)],
        out_specs=[pl.BlockSpec(memory_space=pl.ANY)] * 2,
        scratch_shapes=[pltpu.SemaphoreType.DMA, pltpu.SemaphoreType.DMA((21,)), pltpu.SemaphoreType.DMA((21,))],
        compiler_params=pltpu.CompilerParams(collective_id=3, has_side_effects=True),
        name="return_edges",
    )(ext)


def build_ext(dst, x0, xc, halo, wide, first=None, last=None):
    def put(at, v):
        dst[at:at + v.shape[0], :] = v.astype(dst.dtype)

    for l, size in enumerate(LEVEL_SIZE):
        at = EXT_AT[l]
        a, b = halo[0, l], halo[1, l]
        if first is not None:
            a, b = a.astype(F32) * first, b.astype(F32) * last
        put(at, a)
        put(at + 16, x0[...] if l == 0 else xc[COARSE_AT[l]:COARSE_AT[l] + size, :])
        put(at + 16 + size, b)
    for e in range(8):
        put(WIDE_AT + 16 * e, wide[e])


def fill_bias(bias, bias_mixed, lx, l0, lc, hl, rl):
    p = row_place()
    build_ext(lx, l0, lc, hl, rl, jnp.where(p > 0, 1.0, 0.0), jnp.where(p < 7, 1.0, 0.0))

    def matching(at, size, q):
        kl = lx[pl.ds(at, size), :]
        ql = jnp.transpose(q.astype(F32))[0:1, :]
        return (kl == ql) & (kl != 0.0)

    r, c = iota((160, 128), 0), iota((160, 128), 1)
    near = jnp.abs((r >> 4) - 1 - (c >> 4)) <= 1
    far = near & (jnp.abs((r >> 3) - 2 - (c >> 3)) >= 2)
    same = (r - 16) == c

    @pl.loop(0, 8)
    def _(i):
        at = pl.multiple_of(128 * i, 16)
        ok = matching(at, 160, l0[pl.ds(at, 128), :]) & near | same
        bias[pl.ds(pl.multiple_of(160 * i, 16), 160), :] = jnp.where(ok, 0.0, NEG)

    @pl.loop(8, 15)
    def _(i):
        q = lc[pl.ds(pl.multiple_of(128 * (i - 8), 16), 128), :]
        ok = matching(tile_at(i), 160, q) & far
        bias[pl.ds(pl.multiple_of(160 * i, 16), 160), :] = jnp.where(ok, 0.0, NEG)

    r, c = iota((336, 128), 0), iota((336, 128), 1)
    inner = (r >= 96).astype(I32) + (r >= 160).astype(I32)
    start = jnp.where(inner == 0, 0, jnp.where(inner == 1, 96, 160))
    e, k = (r - 208) >> 4, (r - 208) & 15
    upper = (k >= 8).astype(I32)
    level_k = jnp.where(r < 208, 4 + inner, 7 + upper)
    pos_k = jnp.where(r < 208, r - start - 16, jnp.where(k < 8, e * 8 + k, e * 4 + k - 8))
    level_q, start_q = mixed_levels(c)
    pos_q = c - start_q + jnp.where(level_q == 7, p * 8, jnp.where(level_q == 8, p * 4, 0))
    shape = (level_k == level_q) & (jnp.abs((pos_k >> 4) - (pos_q >> 4)) <= 1) & (jnp.abs((pos_k >> 3) - (pos_q >> 3)) >= 2)
    ok = matching(2048, 336, lc[896:1024, :]) & shape
    bias_mixed[...] = jnp.where(ok, 0.0, NEG)


def tile_at(i):
    level = (i >= 8).astype(I32) + (i >= 12).astype(I32) + (i >= 14).astype(I32)
    return pl.multiple_of(128 * i + 32 * level, 16)


def tile_times(i):
    level = (i >= 8).astype(I32) + (i >= 12).astype(I32) + (i >= 14).astype(I32)
    return (1 << level).astype(F32)


def mixed_times(shape):
    level, _unused = mixed_levels(iota(shape, len(shape) - 1))
    return (1 << level).astype(F32)


def head_masks(rows):
    lane = iota((rows, 128), 1)
    return ones_where(lane < 64), ones_where(lane >= 64)


def by_head(x, masks):
    return jnp.concatenate([x * masks[0], x * masks[1]], axis=0)


def own_blocks(x):
    return jnp.concatenate([x[0:64, 0:128], x[64:128, 128:256]], axis=0)


def twice(x):
    return jnp.concatenate([x, x], axis=1)


def coarse_columns(ref, j):
    pair = pl.multiple_of(1536 + 128 * (j // 2), 128)
    return jnp.concatenate([ref[:, pl.ds(pl.multiple_of(1024 + 128 * j, 128), 128)], ref[:, pl.ds(pair, 128)],
                            ref[:, 1792:2048]], axis=1)


def attention_kernel(q0, k0, v0, l0, qc, kc, vc, lc, hk, hv, hl, rk, rv, rl, ao_out, iz_out,
                     kx, vx, qx, bias, bias_mixed, lx, spt, nz):
    g = pl.program_id(0)

    @pl.when(g == 0)
    def _():
        fill_bias(bias, bias_mixed, lx, l0, lc, hl, rl)
        fill_spread(spt)
    build_ext(kx, k0, kc, hk, rk)
    build_ext(vx, v0, vc, hv, rv)
    qx[0:1024, :] = q0[...]
    qx[1024:2048, :] = qc[...]
    masks = head_masks(128)

    def tile(at, size, i, b, times):
        kw, vw = kx[pl.ds(at, size), :], vx[pl.ds(at, size), :]
        q = by_head(qx[pl.ds(pl.multiple_of(128 * i, 128), 128), :], masks)
        e = jnp.exp(mm_bt(kw, q) + twice(b))
        z = jnp.sum(e, axis=0, keepdims=True) * times
        n = own_blocks(mm_at(vw, e.astype(BF16)))
        zb = jnp.concatenate([jnp.broadcast_to(z[:, 0:128], (64, 128)), jnp.broadcast_to(z[:, 128:256], (64, 128))], axis=0)
        cols = pl.ds(pl.multiple_of(128 * i, 128), 128)
        nz[0:128, cols] = n.astype(BF16)
        nz[128:256, cols] = zb.astype(BF16)

    def body(i, carry):
        tile(tile_at(i), 160, i, bias[pl.ds(pl.multiple_of(160 * i, 16), 160), :], tile_times(i))
        return carry
    lax.fori_loop(0, 15, body, 0)
    tile(2048, 336, 15, bias_mixed[...], twice(mixed_times((1, 128))))
    eye = identity(TILE)

    @pl.loop(0, TOK // TILE)
    def _(j):
        rows = pl.ds(pl.multiple_of(j * TILE, TILE), TILE)
        r = mm_bt(eye, nz[:, rows]) + mm_bt(spt[rows, :], coarse_columns(nz, j))
        inverse = 1.0 / r[:, 128:256]
        iz_out[rows, :] = inverse
        ao_out[rows, :] = (r[:, 0:128] * inverse).astype(BF16)


def pair_specs():
    def cols(shift):
        return pl.BlockSpec((TOK, 128), lambda g, shift=shift: (0, g + shift))
    label = pl.BlockSpec((TOK, 128), lambda g: (0, 12))
    each = [cols(0), cols(4), cols(8), label]
    halo = [pl.BlockSpec((2, 7, 16, 128), lambda g, s=s: (0, 0, 0, g + s)) for s in (0, 4)]
    halo.append(pl.BlockSpec((2, 7, 16, 128), lambda g: (0, 0, 0, 8)))
    wide = [pl.BlockSpec((8, 16, 128), lambda g, s=s: (0, 0, g + s)) for s in (0, 4)]
    wide.append(pl.BlockSpec((8, 16, 128), lambda g: (0, 0, 8)))
    return each + each + halo + wide


def attention(fine, coarse, halo, wide):
    out = pl.BlockSpec((TOK, 128), lambda g: (0, g))
    return pl.pallas_call(
        attention_kernel,
        grid=(4,),
        out_shape=[jax.ShapeDtypeStruct((TOK, D), BF16), jax.ShapeDtypeStruct((TOK, D), F32)],
        in_specs=pair_specs(),
        out_specs=[out, out],
        scratch_shapes=[VMEM((EXT, 128), BF16), VMEM((EXT, 128), BF16), VMEM((2048, 128), BF16),
                        VMEM((15 * 160, 128), F32), VMEM((336, 128), F32), VMEM((EXT, 128), F32),
                        VMEM((TOK, 512), BF16), VMEM((256, 2048), BF16)],
        compiler_params=pltpu.CompilerParams(dimension_semantics=("arbitrary",), vmem_limit_bytes=60 << 20),
        name="attention",
    )(*([fine] * 4 + [coarse] * 4 + [halo] * 3 + [wide] * 3))


def attention_back_kernel(q0, k0, v0, l0, qc, kc, vc, lc, hk, hv, hl, rk, rv, rl, ao, iz, da, dq_out, ext_out,
                          kx, vx, qx, gx, bias, bias_mixed, lx, spt, sp, rm, dk, dv, dqt):
    g = pl.program_id(0)

    @pl.when(g == 0)
    def _():
        fill_bias(bias, bias_mixed, lx, l0, lc, hl, rl)
        fill_spread(spt)
        fill_pool(sp)
    build_ext(kx, k0, kc, hk, rk)
    build_ext(vx, v0, vc, hv, rv)
    qx[0:1024, :] = q0[...]
    qx[1024:2048, :] = qc[...]
    heads = ones_where(iota((16, 128), 0) == (iota((16, 128), 1) >> 6))

    @pl.loop(0, TOK // TILE)
    def _(j):
        rows = pl.ds(pl.multiple_of(j * TILE, TILE), TILE)
        gf = da[rows, :].astype(F32) * iz[rows, :]
        gx[rows, :] = gf.astype(BF16)
        high, low = split(gf * ao[rows, :].astype(F32))
        rm[:, rows] = mm_bt(heads, high) + mm_bt(heads, low)

    def pooled(c_rows, t_rows, dst):
        s = sp[c_rows, t_rows]
        gx[dst, :] = mm(s, gx[t_rows, :]).astype(BF16)
        high, low = split(rm[:, t_rows])
        return mm_bt(high, s) + mm_bt(low, s)

    @pl.loop(0, 4)
    def _(j):
        dst = pl.ds(pl.multiple_of(1024 + 128 * j, 128), 128)
        rm[:, dst] = pooled(pl.ds(0, 128), pl.ds(pl.multiple_of(j * 256, 256), 256), dst) * 2.0

    for j in range(2):
        dst = pl.ds(1536 + 128 * j, 128)
        rm[:, dst] = pooled(pl.ds(128, 128), pl.ds(j * 512, 512), dst) * 4.0
    rm[:, pl.ds(1792, 128)] = pooled(pl.ds(256, 128), pl.ds(0, 1024), pl.ds(1792, 128)) * 8.0
    rm[:, pl.ds(1920, 128)] = pooled(pl.ds(384, 128), pl.ds(0, 1024), pl.ds(1920, 128)) * mixed_times((16, 128))
    dk[...] = jnp.zeros_like(dk)
    dv[...] = jnp.zeros_like(dv)
    masks = head_masks(128)

    def tile(at, size, i, b, shrink):
        keys = pl.ds(at, size)
        cols = pl.ds(pl.multiple_of(128 * i, 128), 128)
        kw, vw = kx[keys, :], vx[keys, :]
        q, gg = by_head(qx[cols, :], masks), by_head(gx[cols, :], masks)
        e = jnp.exp(mm_bt(kw, q) + twice(b))
        rest = jnp.concatenate([rm[0:1, cols], rm[1:2, cols]], axis=1)
        ds = (e * (mm_bt(vw, gg) - rest)).astype(BF16)
        dk[keys, :] += mm(ds, q)
        dv[keys, :] += mm(e.astype(BF16), gg)
        dqt[:, cols] = (own_blocks(mm_at(kw, ds)) * shrink).astype(BF16)

    def body(i, carry):
        tile(tile_at(i), 160, i, bias[pl.ds(pl.multiple_of(160 * i, 16), 160), :], 0.125 / tile_times(i))
        return carry
    lax.fori_loop(0, 15, body, 0)
    tile(2048, 336, 15, bias_mixed[...], 0.125 / mixed_times((1, 128)))
    eye = identity(TILE)

    @pl.loop(0, TOK // TILE)
    def _(j):
        rows = pl.ds(pl.multiple_of(j * TILE, TILE), TILE)
        dq_out[rows, :] = (mm_bt(eye, dqt[:, rows]) + mm_bt(spt[rows, :], coarse_columns(dqt, j))).astype(BF16)
    ext_out[0] = dk[...].astype(BF16)
    ext_out[1] = dv[...].astype(BF16)


def attention_back(fine, coarse, halo, wide, ao, iz, da):
    pair = pl.BlockSpec((TOK, 128), lambda g: (0, g))
    ext = pl.BlockSpec((2, EXT, 128), lambda g: (0, 0, g))
    return pl.pallas_call(
        attention_back_kernel,
        grid=(4,),
        out_shape=[jax.ShapeDtypeStruct((TOK, D), BF16), jax.ShapeDtypeStruct((2, EXT, D), BF16)],
        in_specs=pair_specs() + [pair, pair, pair],
        out_specs=[pair, ext],
        scratch_shapes=[VMEM((EXT, 128), BF16), VMEM((EXT, 128), BF16), VMEM((2048, 128), BF16), VMEM((2048, 128), BF16),
                        VMEM((15 * 160, 128), F32), VMEM((336, 128), F32), VMEM((EXT, 128), F32),
                        VMEM((TOK, 512), BF16), VMEM((512, TOK), BF16), VMEM((16, 2048), F32),
                        VMEM((EXT, 128), F32), VMEM((EXT, 128), F32), VMEM((128, 2048), BF16)],
        compiler_params=pltpu.CompilerParams(dimension_semantics=("arbitrary",), vmem_limit_bytes=60 << 20),
        name="attention_back",
    )(*([fine] * 4 + [coarse] * 4 + [halo] * 3 + [wide] * 3 + [ao, iz, da]))


C0 = 0.7978845608028654
C1 = 0.044715


def middle_kernel(tok, ao, cot, wo, w1, w2, vecs, b1, out, dh1_out, da_out, gwo, gw1, gw2, gvec, gb1,
                  awo, aw1, aw2, avec, ab1):
    j = pl.program_id(0)

    @pl.when(j == 0)
    def _():
        awo[...] = jnp.zeros_like(awo)
        aw1[...] = jnp.zeros_like(aw1)
        aw2[...] = jnp.zeros_like(aw2)
        avec[...] = jnp.zeros_like(avec)
        ab1[...] = jnp.zeros_like(ab1)
    mixed = ao[...]
    h1 = tok[...].astype(F32) + mm(mixed, wo[...]) + vecs[5:6, :]
    center = h1 - jnp.mean(h1, axis=-1, keepdims=True)
    inverse = lax.rsqrt(jnp.mean(center * center, axis=-1, keepdims=True) + EPS)
    xh = center * inverse
    gain = vecs[6:7, :]
    a2 = (xh * gain + vecs[7:8, :]).astype(BF16)
    dy = cot[...]
    y = h1 + vecs[8:9, :]
    da2 = jnp.zeros((TILE, D), F32)
    for k in range(FF // D):
        cols = slice(D * k, D * k + D)
        u = mm(a2, w1[:, cols]) + b1[:, cols]
        u2 = u * u
        th = jnp.tanh(u * (C0 + (C0 * C1) * u2))
        half = 0.5 * (1.0 + th)
        g = (u * half).astype(BF16)
        slope = half + 0.5 * u * (1.0 - th * th) * (C0 + (3.0 * C0 * C1) * u2)
        y = y + mm(g, w2[cols, :])
        du = (mm_bt(dy, w2[cols, :]) * slope).astype(BF16)
        aw2[cols, :] += mm_at(g, dy)
        aw1[:, cols] += mm_at(a2, du)
        ab1[:, cols] += jnp.sum(du.astype(F32), axis=0, keepdims=True)
        da2 = da2 + mm_bt(du, w1[:, cols])
    out[...] = y.astype(BF16)
    dyf = dy.astype(F32)
    e = da2 * gain
    dh1 = dyf + inverse * (e - jnp.mean(e, axis=-1, keepdims=True) - xh * jnp.mean(e * xh, axis=-1, keepdims=True))
    dh1_out[...] = dh1
    db = dh1.astype(BF16)
    awo[...] += mm_at(mixed, db)
    da_out[...] = mm_bt(db, wo[...]).astype(BF16)
    avec[5:6, :] += jnp.sum(db.astype(F32), axis=0, keepdims=True)
    avec[6:7, :] += jnp.sum(da2 * xh, axis=0, keepdims=True)
    avec[7:8, :] += jnp.sum(da2, axis=0, keepdims=True)
    avec[8:9, :] += jnp.sum(dyf, axis=0, keepdims=True)

    @pl.when(j == TOK // TILE - 1)
    def _():
        gwo[...] = awo[...].astype(BF16)
        gw1[...] = aw1[...].astype(BF16)
        gw2[...] = aw2[...].astype(BF16)
        gvec[...] = avec[...]
        gb1[...] = ab1[...]


def whole(shape):
    return pl.BlockSpec(shape, lambda j: (0,) * len(shape), pipeline_mode=pl.Buffered(1))


def middle(tok, ao, cot, wo, w1, w2, vecs, b1):
    tile = pl.BlockSpec((TILE, D), lambda j: (j, 0))
    S = jax.ShapeDtypeStruct
    return pl.pallas_call(
        middle_kernel,
        grid=(TOK // TILE,),
        out_shape=[S((TOK, D), BF16), S((TOK, D), F32), S((TOK, D), BF16), S((D, D), BF16), S((D, FF), BF16), S((FF, D), BF16),
                   S((16, D), F32), S((1, FF), F32)],
        in_specs=[tile, tile, tile, whole((D, D)), whole((D, FF)), whole((FF, D)), whole((16, D)), whole((1, FF))],
        out_specs=[tile, tile, tile, whole((D, D)), whole((D, FF)), whole((FF, D)), whole((16, D)), whole((1, FF))],
        scratch_shapes=[VMEM((D, D), F32), VMEM((D, FF), F32), VMEM((FF, D), F32), VMEM((16, D), F32), VMEM((1, FF), F32)],
        compiler_params=pltpu.CompilerParams(dimension_semantics=("arbitrary",), vmem_limit_bytes=60 << 20),
        name="middle",
    )(tok, ao, cot, wo, w1, w2, vecs, b1)


def post_kernel(tok, a1, dq, ext, halo, wide, dh1, weight, vecs, out, gw, gvec, spt, kv, kvc, aw, avec):
    j = pl.program_id(0)

    @pl.when(j == 0)
    def _():
        fill_spread(spt)
        aw[...] = jnp.zeros_like(aw)
        avec[...] = jnp.zeros_like(avec)
        for half in range(2):
            lanes = slice(D * half, D * half + D)
            for l, size in enumerate(LEVEL_SIZE):
                at = EXT_AT[l] + 16
                dst, to = (kv, 0) if l == 0 else (kvc, COARSE_AT[l])
                shrink = 0.5 ** l if half == 0 else 1.0
                first, last = halo[0, l, half].astype(F32), halo[1, l, half].astype(F32)
                if size == 16:
                    v = ext[half, at:at + 16, :].astype(F32) + first + last
                    dst[to:to + 16, lanes] = (v * shrink).astype(BF16)
                    continue
                dst[to:to + 16, lanes] = ((ext[half, at:at + 16, :].astype(F32) + first) * shrink).astype(BF16)
                end = to + size - 16
                dst[end:end + 16, lanes] = ((ext[half, at + size - 16:at + size, :].astype(F32) + last) * shrink).astype(BF16)
                if size > 32:
                    dst[to + 16:end, lanes] = ext[half, at + 16:at + size - 16, :] * jnp.array(shrink, BF16)
            v = wide[0, half].astype(F32)
            for e in range(1, 8):
                v = v + wide[e, half].astype(F32)
            if half == 0:
                v = v * jnp.where(iota((16, D), 0) < 8, 0.5 ** 7, 0.5 ** 8)
            kvc[1008:1024, lanes] = v.astype(BF16)

    rows = pl.ds(pl.multiple_of(j * TILE, TILE), TILE)
    s = spt[rows, :]
    x1 = kvc[pl.ds(pl.multiple_of(j * 128, 128), 128), :]
    x2 = kvc[pl.ds(pl.multiple_of(512 + 128 * (j // 2), 128), 128), :]
    x3 = kvc[768:1024, :]
    dkv = (kv[rows, :].astype(F32) + mm(s[:, 0:128], x1) + mm(s[:, 128:256], x2) + mm(s[:, 256:512], x3)).astype(BF16)
    parts = (dq[...], dkv[:, 0:D], dkv[:, D:2 * D])
    a = a1[...]
    da1 = jnp.zeros((TILE, D), F32)
    for c in range(3):
        aw[c] += mm_at(a, parts[c])
        avec[2 + c:3 + c, :] += jnp.sum(parts[c].astype(F32), axis=0, keepdims=True)
        da1 = da1 + mm_bt(parts[c], weight[c])
    v = tok[...].astype(F32)
    center = v - jnp.mean(v, axis=-1, keepdims=True)
    inverse = lax.rsqrt(jnp.mean(center * center, axis=-1, keepdims=True) + EPS)
    xh = center * inverse
    e = da1 * vecs[0:1, :]
    dv = inverse * (e - jnp.mean(e, axis=-1, keepdims=True) - xh * jnp.mean(e * xh, axis=-1, keepdims=True))
    out[...] = (dh1[...] + dv).astype(BF16)
    avec[0:1, :] += jnp.sum(da1 * xh, axis=0, keepdims=True)
    avec[1:2, :] += jnp.sum(da1, axis=0, keepdims=True)

    @pl.when(j == TOK // TILE - 1)
    def _():
        gw[...] = aw[...].astype(BF16)
        gvec[...] = avec[...]


def after_attention(tok, a1, dq, ext, halo, wide, dh1, weight, vecs):
    tile = pl.BlockSpec((TILE, D), lambda j: (j, 0))
    S = jax.ShapeDtypeStruct
    return pl.pallas_call(
        post_kernel,
        grid=(TOK // TILE,),
        out_shape=[S((TOK, D), BF16), S((3, D, D), BF16), S((8, D), F32)],
        in_specs=[tile, tile, tile, whole((2, EXT, D)), whole((2, 7, 2, 16, D)), whole((8, 2, 16, D)), tile, whole((3, D, D)), whole((16, D))],
        out_specs=[tile, whole((3, D, D)), whole((8, D))],
        scratch_shapes=[VMEM((TOK, 512), BF16), VMEM((TOK, 2 * D), BF16), VMEM((TOK, 2 * D), BF16), VMEM((3, D, D), F32), VMEM((8, D), F32)],
        compiler_params=pltpu.CompilerParams(dimension_semantics=("arbitrary",), vmem_limit_bytes=60 << 20),
        name="after_attention",
    )(tok, a1, dq, ext, halo, wide, dh1, weight, vecs)


def where_am_i():
    h = lax.axis_index("head")
    s = lax.axis_index("span")
    return h, s, s // 4, (s // 2) % 2, s % 2


def peers_of(h, s, y, x, c):
    zs = [lax.rem(h + d, 4) for d in (1, 2, 3)]
    px = {"span": y * 4 + (1 - x) * 2 + c}
    py = {"span": (1 - y) * 4 + x * 2 + c}
    pc = {"span": y * 4 + x * 2 + 1 - c}
    return zs, px, py, pc


def gather_kernel(n, orders, *refs):
    ins, outs = refs[:n], refs[n:2 * n]
    lsem, ssem, rsem = refs[2 * n:]
    h, s, y, x, c = where_am_i()
    zs, px, py, pc = peers_of(h, s, y, x, c)
    greet([{"head": z} for z in zs] + [px, py, pc])
    pend = []
    zc = []
    for i in range(n):
        own = pltpu.make_async_copy(ins[i], outs[i].at[h, y, x, c], lsem.at[i])
        own.start()
        cs = []
        for k, z in enumerate(zs):
            cp = rcopy(ins[i], outs[i].at[h, y, x, c], ssem.at[i, k], rsem.at[i, k], {"head": z})
            cp.start()
            cs.append(cp)
        zc.append((own, cs))
    s2 = []
    for i in range(n):
        own, cs = zc[i]
        own.wait()
        for cp in cs:
            cp.wait()
        dev = px if orders[i] == 0 else py
        src = outs[i].at[:, y, x, c]
        cp = rcopy(src, src, ssem.at[i, 3], rsem.at[i, 3], dev)
        cp.start()
        s2.append(cp)
    s3 = []
    for i in range(n):
        s2[i].wait()
        if orders[i] == 0:
            src, dev = outs[i].at[:, y, :, c], py
        else:
            src, dev = outs[i].at[:, :, x, c], px
        cp = rcopy(src, src, ssem.at[i, 4], rsem.at[i, 4], dev)
        cp.start()
        s3.append(cp)
    s4 = []
    for i in range(n):
        s3[i].wait()
        src = outs[i].at[:, :, :, c]
        cp = rcopy(src, src, ssem.at[i, 5], rsem.at[i, 5], pc)
        cp.start()
        s4.append(cp)
    for cp in s4:
        cp.wait()


def gather_all(shards, orders, cid=0, space=pl.ANY):
    n = len(shards)
    return pl.pallas_call(
        functools.partial(gather_kernel, n, orders),
        out_shape=[jax.ShapeDtypeStruct((4, 2, 2, 2) + a.shape, a.dtype) for a in shards],
        in_specs=[pl.BlockSpec(memory_space=pl.ANY)] * n,
        out_specs=[pl.BlockSpec(memory_space=space)] * n,
        scratch_shapes=[pltpu.SemaphoreType.DMA((n,)), pltpu.SemaphoreType.DMA((n, 6)), pltpu.SemaphoreType.DMA((n, 6))],
        compiler_params=pltpu.CompilerParams(collective_id=cid, has_side_effects=True),
        name="gather_params",
    )(*shards)


def scatter_kernel(n, orders, *refs):
    ins, outs = refs[:n], refs[n:2 * n]
    a = 2 * n
    r1, r2, r3, r4 = (refs[a + k * n:a + (k + 1) * n] for k in range(4))
    ssem, rsem = refs[a + 4 * n:]
    h, s, y, x, c = where_am_i()
    zs, px, py, pc = peers_of(h, s, y, x, c)
    greet([{"head": z} for z in zs] + [px, py, pc])
    cs = []
    for i in range(n):
        cp = rcopy(ins[i].at[:, :, :, 1 - c], r1[i], ssem.at[i, 0], rsem.at[i, 0], pc)
        cp.start()
        cs.append(cp)
    s2 = []
    for i in range(n):
        cs[i].wait()

        @pl.loop(0, 4)
        def _(hh):
            for yy in range(2):
                for xx in range(2):
                    r1[i][hh, yy, xx] = (r1[i][hh, yy, xx].astype(F32) + ins[i][hh, yy, xx, c].astype(F32)).astype(r1[i].dtype)
        if orders[i] == 0:
            src, dev = r1[i].at[:, :, 1 - x], px
        else:
            src, dev = r1[i].at[:, 1 - y], py
        cp = rcopy(src, r2[i], ssem.at[i, 1], rsem.at[i, 1], dev)
        cp.start()
        s2.append(cp)
    s3 = []
    for i in range(n):
        s2[i].wait()

        @pl.loop(0, 4)
        def _(hh):
            for v in range(2):
                mine = r1[i][hh, v, x] if orders[i] == 0 else r1[i][hh, y, v]
                r2[i][hh, v] = (r2[i][hh, v].astype(F32) + mine.astype(F32)).astype(r2[i].dtype)
        if orders[i] == 0:
            src, dev = r2[i].at[:, 1 - y], py
        else:
            src, dev = r2[i].at[:, 1 - x], px
        cp = rcopy(src, r3[i], ssem.at[i, 2], rsem.at[i, 2], dev)
        cp.start()
        s3.append(cp)
    s4 = []
    for i in range(n):
        s3[i].wait()
        me = y if orders[i] == 0 else x

        @pl.loop(0, 4)
        def _(hh):
            r3[i][hh] = (r3[i][hh].astype(F32) + r2[i][hh, me].astype(F32)).astype(r3[i].dtype)
        zz = []
        for k, z in enumerate(zs):
            cp = rcopy(r3[i].at[z], r4[i].at[k], ssem.at[i, 3 + k], rsem.at[i, 3 + k], {"head": z})
            cp.start()
            zz.append(cp)
        s4.append(zz)
    for i in range(n):
        for cp in s4[i]:
            cp.wait()
        acc = r3[i][h].astype(F32)
        for k in range(3):
            acc = acc + r4[i][k].astype(F32)
        outs[i][...] = acc


def scatter_all(grads, orders, cid=1):
    n = len(grads)
    sh = [g.shape[4:] for g in grads]
    V = pltpu.VMEM
    return pl.pallas_call(
        functools.partial(scatter_kernel, n, orders),
        out_shape=[jax.ShapeDtypeStruct(s, F32) for s in sh],
        in_specs=[pl.BlockSpec(memory_space=pltpu.VMEM)] * n,
        out_specs=[pl.BlockSpec(memory_space=pltpu.VMEM)] * n,
        scratch_shapes=[V((4, 2, 2) + s, g.dtype) for s, g in zip(sh, grads)]
        + [V((4, 2) + s, g.dtype) for s, g in zip(sh, grads)]
        + [V((4,) + s, g.dtype) for s, g in zip(sh, grads)]
        + [V((3,) + s, g.dtype) for s, g in zip(sh, grads)]
        + [pltpu.SemaphoreType.DMA((n, 6)), pltpu.SemaphoreType.DMA((n, 6))],
        compiler_params=pltpu.CompilerParams(collective_id=cid, has_side_effects=True, vmem_limit_bytes=60 << 20),
        name="scatter_grads",
    )(*grads)


BOTH = ("head", "span")


def pack_vectors(first_gain, first_shift, project_bias, output_bias, second_gain, second_shift, reduce_bias, expand_bias):
    a = jnp.stack([first_gain, first_shift, project_bias[0], project_bias[1], project_bias[2], output_bias, second_gain, second_shift])
    b = jnp.pad(reduce_bias[None, :], ((0, 7), (0, 0)))
    return jnp.concatenate([a, b, expand_bias.reshape(8, 8), jnp.zeros((8, 88), F32)], axis=1)


def unpack_vectors(g):
    vecs = g[:, :, 0:32].reshape(32, 8, 2, 16).transpose(2, 1, 0, 3).reshape(16, D)
    return vecs, g[:, :, 32:40].reshape(1, FF)


def pack_gradients(vec, b1):
    a = vec[0:8].reshape(8, 32, 16).transpose(1, 0, 2)
    b = jnp.pad(vec[8].reshape(32, 1, 16), ((0, 0), (0, 7), (0, 0)))
    return jnp.concatenate([a, b, b1.reshape(32, 8, 8), jnp.zeros((32, 8, 88), F32)], axis=2)


def shards(tokens, segment_ids, first_gain, first_shift, project_weight, project_bias, output_weight, output_bias,
           second_gain, second_shift, expand_weight, expand_bias, reduce_weight, reduce_bias, cotangent):
    tok, cot = tokens[0], cotangent[0]
    near = lax.axis_size("head") == 4 and lax.axis_size("span") == 8
    if near:
        packed = pack_vectors(first_gain, first_shift, project_bias, output_bias, second_gain, second_shift, reduce_bias, expand_bias)
        wq, wo, w1, w2, vec = gather_all([project_weight.reshape(48, D), output_weight, expand_weight, reduce_weight, packed], ORDERS)
        wq = wq.reshape(32, 3, 16, D).transpose(1, 0, 2, 3).reshape(3, D, D)
        wo, w1, w2 = wo.reshape(D, D), w1.reshape(D, FF), w2.reshape(FF, D)
        vecs, b1 = unpack_vectors(vec.reshape(32, 8, 128))
    else:
        def full(v, axis=0):
            return lax.all_gather(v, BOTH, axis=axis, tiled=True)
        wq, wo, w1, w2 = full(project_weight, 1), full(output_weight), full(expand_weight), full(reduce_weight)
        rows = [full(first_gain), full(first_shift), *full(project_bias, 1), full(output_bias), full(second_gain), full(second_shift), full(reduce_bias)]
        vecs = jnp.pad(jnp.stack(rows), ((0, 7), (0, 0)))
        b1 = full(expand_bias)[None]
    a1, fine, coarse = before_attention(tok, segment_ids, wq, vecs)
    halo, wide = exchange_edges(fine, coarse)
    ao, iz = attention(fine, coarse, halo, wide)
    out, dh1, da, gwo, gw1, gw2, gvec, gb1 = middle(tok, ao, cot, wo, w1, w2, vecs, b1)
    dq, ext = attention_back(fine, coarse, halo, wide, ao, iz, da)
    halo_b, wide_b = return_edges(ext)
    dtok, gwq, gvec_b = after_attention(tok, a1, dq, ext, halo_b, wide_b, dh1, wq, vecs)
    vec = jnp.concatenate([gvec_b[0:5], gvec[5:9]], axis=0)
    if near:
        grid = (4, 2, 2, 2)
        sums = scatter_all([gwq.reshape(3, 32, 16, D).transpose(1, 0, 2, 3).reshape(grid + (48, D)), gwo.reshape(grid + (16, D)),
                            gw1.reshape(grid + (16, FF)), gw2.reshape(grid + (64, D)), pack_gradients(vec, gb1).reshape(grid + (8, 128))], ORDERS)
        gwq, gwo, gw1, gw2, packed = sums
        gwq = gwq.reshape(3, 16, D)
        row = [packed[r, 0:16] for r in range(8)]
        small = (row[0], row[1], packed[2:5, 0:16], row[5], row[6], row[7], packed[:, 32:40].reshape(64), packed[0, 16:32])
    else:
        def part(v, axis=0):
            return lax.psum_scatter(v.astype(F32), BOTH, scatter_dimension=axis, tiled=True)
        gwq, gwo, gw1, gw2 = part(gwq, 1), part(gwo), part(gw1), part(gw2)
        small = (part(vec[0]), part(vec[1]), part(vec[2:5], 1), part(vec[5]), part(vec[6]), part(vec[7]), part(gb1[0]), part(vec[8]))
    return (out[None], dtok[None], small[0], small[1], gwq, small[2], gwo, small[3], small[4], small[5], gw1, small[6], gw2, small[7])


ORDERS = (1, 0, 0, 1, 0)


def solution(mesh):
    token, row, matrix = P("span", "head", None), P(BOTH), P(BOTH, None)
    three, bias = P(None, BOTH, None), P(None, BOTH)
    params = (row, row, three, bias, matrix, row, row, row, matrix, row, matrix, row)
    return jax.shard_map(shards, mesh=mesh, in_specs=(token, P("span", None)) + params + (token,),
                         out_specs=(token, token) + params, check_vma=False)
```

time: 2090 us -> 297 us (0.14)
  waiting for transfers between devices: 689 us -> 0 us
  local copies, waits for them, and re-layouts: 569 us -> 21.3 us
  matrix products: 333 us -> 0 us
  Pallas kernels: 0 us -> 271 us
  other arithmetic: 271 us -> 2.8 us
  blocking collectives: 182 us -> 0 us
    reduce_scatter x5 -> x0, waiting for transfers between devices: 578 us -> none  [the longest x1 139 us: shards(): lax.psum_scatter(grad_up_w, ('head', 'span'), scatter_dimension=0, tiled=...]
    dot_general x66 -> x0, matrix products: 333 us -> none  [the longest x9 57.3 us: level_backward(): jnp.einsum('hijb,bihd->bjhd', weights, grad_block, precision=highest)]
    pallas_call x0 -> x9, Pallas kernels: none -> 271 us  [the longest x1 51 us: scatter_all(): pl.pallas_call(functools.partial(scatter_kernel, n, orders), out_shape=[j...]
    reduce_sum x47 -> x0, other arithmetic: 106 us -> none  [the longest x40 94.5 us: pair_sum(): values_in.reshape((values_in.shape[0] // 2, 2) + values_in.shape[1:])]
    unnamed x573 -> x11, local copies, waits for them, and re-layouts: 109 us -> 6.17 us
    all_gather x2 -> x0, blocking collectives: 98.4 us -> none  [the longest x1 56.8 us: shards(): lax.all_gather(output_weight, ('head', 'span'), axis=0, tiled=True)]
    concatenate x57 -> x2, local copies, waits for them, and re-layouts: 89.8 us -> 0.17 us  [the longest x1 0.1 us: pack_gradients(): jnp.concatenate([a, b, b1.reshape(32, 8, 8), jnp.zeros((32, 8, 88), F32)]...]
    unnamed x11 -> x0, waiting for transfers between devices: 87.3 us -> none
  transfers between devices with their start and end apart: 15 -> 0, of which waited for: 7 -> 0; matrix products, arithmetic and copies ran while one was open for 30% -> 0% of each run, Pallas kernels for 0% -> 0%
where the time goes in v1:
time: 297 us; the launch traced here: 296 us
  Pallas kernels  271 us (91%)
  local copies, waits for them, and re-layouts  21.3 us (7%)
    pallas_call x1, Pallas kernels, scatter_all(): pl.pallas_call(functools.partial(scatter_kernel, n, orders), out_shape=[j...  51 us
    pallas_call x1, Pallas kernels, gather_all(): pl.pallas_call(functools.partial(gather_kernel, n, orders), out_shape=[ja...  49.6 us
    pallas_call x1, Pallas kernels, attention_back(): pl.pallas_call(attention_back_kernel, grid=(4,), out_shape=[jax.ShapeDtyp...  44.6 us
    pallas_call x1, Pallas kernels, attention(): pl.pallas_call(attention_kernel, grid=(4,), out_shape=[jax.ShapeDtypeStru...  33.7 us
    pallas_call x1, Pallas kernels, middle(): pl.pallas_call(middle_kernel, grid=(TOK // TILE,), out_shape=[S((TOK, D),...  27.1 us
    pallas_call x1, Pallas kernels, exchange_edges(): pl.pallas_call(edges_kernel, out_shape=[jax.ShapeDtypeStruct((2, 7, 16, l...  22.9 us
    pallas_call x1, Pallas kernels, return_edges(): pl.pallas_call(edges_back_kernel, out_shape=[jax.ShapeDtypeStruct((2, 7,...  19.8 us
    pallas_call x1, Pallas kernels, after_attention(): pl.pallas_call(post_kernel, grid=(TOK // TILE,), out_shape=[S((TOK, D), B...  12.5 us

profile of v1, /device:TPU:0, one launch (start us, length us, event | category | flops | bytes accessed | tf_op | source)
XLA Modules:
  0.0 296.2 jit_solution(12692089358105716190)
XLA Ops:
  0.6 0.7 reshape.93
  1.4 0.8 stack.24
  2.1 0.1 pad.19.clone
  2.2 1.3 fusion.1.refs_4_
  3.5 49.6 %gather_params.1 = (bf16[4,2,2,2,48,512]{5,4,3,2,1,0:T(8,128)(2,1)}, bf16[4,2,2,2,16,512]{5,4,3,2,1,0:T(8,128)(2,1)}, bf16[4,2,2,2,16,2048]{5,4,3,2,1,0:T(8,128)...) custom-call(bf16[48,512]{1,0:T(8,128)(2,1)} %bitcast.73, bf16[16,512]{1,0:T(8,128)(2,1)} %refs_1_.1, ...), custom_call_target="tpu_custom_call" | custom-call | tf_op jit(solution)/shard_map/gather_params/pallas_call | solution.py:730
  53.2 0.0 copy-start
  53.2 2.8 copy.33
  55.9 0.0 copy-done
  55.9 0.1 copy.39
  56.0 0.1 copy.35
  56.2 0.8 reshape.98.vecs
  56.9 10.0 %before_attention.1 = (bf16[1024,512]{1,0:T(8,128)(2,1)}, bf16[1024,1664]{1,0:T(8,128)(2,1)}, bf16[1024,1664]{1,0:T(8,128)(2,1)}) custom-call(bf16[1024,512]{1,0:T(8,128)(2,1)} %bitcast.52, s32[1,4096]{1,0:T(1,128)} %seg.1, bf16[3,512,512]{2,1,0:T(8,128)(2,1)} %bitcast.50, f32[16,512]{1,0:T(8,128)} %reshape.98.vecs), custom_call_target="tpu_custom_call" | custom-call | tf_op jit(solution)/shard_map/before_attention/pallas_call | solution.py:149
  67.0 22.9 %exchange_edges.1 = (bf16[2,7,16,1152]{3,2,1,0:T(8,128)(2,1)}, bf16[8,16,1152]{2,1,0:T(8,128)(2,1)}) custom-call(bf16[1024,1664]{1,0:T(8,128)(2,1)} %get-tuple-element.48.fine.q0.k0.v0.l0, bf16[1024,1664]{1,0:T(8,128)(2,1)} %get-tuple-element.49.coarse.qc.kc.vc.lc), custom_call_target="tpu_custom_call" | custom-call | tf_op jit(solution)/shard_map/exchange_edges/pallas_call | solution.py:213
  89.9 33.7 %attention.1 = (bf16[1024,512]{1,0:T(8,128)(2,1)}, f32[1024,512]{1,0:T(8,128)}) custom-call(bf16[1024,1664]{1,0:T(8,128)(2,1)} %get-tuple-element.48.fine.q0.k0.v0.l0, bf16[1024,1664]{1,0:T(8,128)(2,1)} %get-tuple-element.48.fine.q0.k0.v0.l0, bf16[1024,1664]{1,0:T(8,128)(2,1)} %get-tuple-element.48.fine.q0.k0.v0.l0, ...), custom_call_target="tpu_custom_call" | custom-call | tf_op jit(solution)/shard_map/attention/pallas_call | solution.py:407
  123.6 0.1 slice.62
  123.7 0.7 reshape.102.b1
  124.4 27.1 %middle.1 = (bf16[1024,512]{1,0:T(8,128)(2,1)}, f32[1024,512]{1,0:T(8,128)}, bf16[1024,512]{1,0:T(8,128)(2,1)}, bf16[512,512]{1,0:T(8,128)(2,1)}, bf16[512,2048]...) custom-call(bf16[1024,512]{1,0:T(8,128)(2,1)} %bitcast.53, ...), custom_call_target="tpu_custom_call" | custom-call | tf_op jit(solution)/shard_map/middle/pallas_call | solution.py:577
  151.6 44.6 %attention_back.1 = (bf16[1024,512]{1,0:T(8,128)(2,1)}, bf16[2,2384,512]{2,1,0:T(8,128)(2,1)}) custom-call(bf16[1024,1664]{1,0:T(8,128)(2,1)} %get-tuple-element.48.fine.q0.k0.v0.l0, bf16[1024,1664]{1,0:T(8,128)(2,1)} %get-tuple-element.48.fine.q0.k0.v0.l0, bf16[1024,1664]{1,0:T(8,128)(2,1)} %get-tuple-element.48.fine.q0.k0.v0.l0, ...), custom_call_target="tpu_custom_call" | custom-call | tf_op jit(solution)/shard_map/attention_back/pallas_call | solution.py:494
  196.1 19.8 %return_edges.1 = (bf16[2,7,2,16,512]{4,3,2,1,0:T(8,128)(2,1)}, bf16[8,2,16,512]{3,2,1,0:T(8,128)(2,1)}) custom-call(bf16[2,2384,512]{2,1,0:T(8,128)(2,1)} %get-tuple-element.61.ext), custom_call_target="tpu_custom_call" | custom-call | tf_op jit(solution)/shard_map/return_edges/pallas_call | solution.py:247
  215.9 12.5 %after_attention.1 = (bf16[1024,512]{1,0:T(8,128)(2,1)}, bf16[3,512,512]{2,1,0:T(8,128)(2,1)}, f32[8,512]{1,0:T(8,128)}) custom-call(bf16[1024,512]{1,0:T(8,128)(2,1)} %bitcast.54, bf16[1024,512]{1,0:T(8,128)(2,1)} %get-tuple-element.57.a1, bf16[1024,512]{1,0:T(8,128)(2,1)} %get-tuple-element.60.dq, bf16[2,2384,512]{2,1,0:T(8,128)(2,1)} %get-tuple-element.61.ext, ...), custom_call_target="tpu_custom_call" | custom-call | tf_op jit(solution)/shard_map/after_attention/pallas_call | solution.py:653
  228.4 0.0 copy-start.2
  228.5 0.0 copy-start.1
  228.5 2.7 copy.36
  231.2 0.5 broadcast.21
  231.7 0.0 copy-done.2
  231.7 0.7 reduce.7
  232.3 0.1 concatenate.20
  232.4 0.7 slice_reduce_fusion
  233.2 0.1 reshape_squeeze.3
  233.3 0.8 slice.50
  234.1 0.0 copy-done.1
  234.1 0.1 reshape.108
  234.2 0.1 copy.37
  234.3 0.8 maximum_maximum_fusion.refs_4_
  235.1 51.0 %scatter_grads.1 = (f32[48,512]{1,0:T(8,128)}, f32[16,512]{1,0:T(8,128)}, f32[16,2048]{1,0:T(8,128)}, f32[64,512]{1,0:T(8,128)}, f32[8,128]{1,0:T(8,128)}) custom-call(bf16[4,2,2,2,48,512]{5,4,3,2,1,0:T(8,128)(2,1)} %bitcast.55, bf16[4,2,2,2,16,512]{5,4,3,2,1,0:T(8,128)(2,1)} %bitcast.63, bf16[4,2,2,2,16,2048]{5,4,3,2,1,0:T(8,128)(2,1)} %bitcast.56, ...), custom_call_target="tpu_custom_call" | custom-call | tf_op jit(solution)/shard_map/scatter_grads/pallas_call | solution.py:813
  286.1 1.5 slice_bitcast_fusion
  287.6 1.3 slice.55
  288.8 0.7 slice.59
  289.6 0.6 reshape.110
  290.2 1.5 copy.45
  291.7 1.4 copy.46
  293.1 1.6 copy.47
  294.6 1.6 copy.48
  (3 shorter events, 0.0 us)
Async XLA Ops:
  53.2 2.8 copy-start
  228.4 3.2 %copy-start.2 = (f32[1,2048]{1,0:T(1,128)S(1)}, f32[1,2048]{1,0:T(1,128)}, u32[]{:S(2)}) copy-start(f32[1,2048]{1,0:T(1,128)} %get-tuple-element.72) | copy-start | bytes 24580
  228.5 5.6 %copy-start.1 = (f32[8,512]{1,0:T(8,128)S(1)}, f32[8,512]{1,0:T(8,128)}, u32[]{:S(2)}) copy-start(f32[8,512]{1,0:T(8,128)} %get-tuple-element.70) | copy-start | bytes 49156

commit v2 on v1

--- a/solution.py
+++ b/solution.py
@@ -349,9 +349,16 @@
                             ref[:, 1792:2048]], axis=1)
 
 
-def attention_kernel(q0, k0, v0, l0, qc, kc, vc, lc, hk, hv, hl, rk, rv, rl, ao_out, iz_out,
-                     kx, vx, qx, bias, bias_mixed, lx, spt, nz):
+def attention_kernel(n, orders, q0, k0, v0, l0, qc, kc, vc, lc, hk, hv, hl, rk, rv, rl, *refs):
+    ins, (ao_out, iz_out), outs = refs[:n], refs[n:n + 2], refs[n + 2:2 * n + 2]
+    kx, vx, qx, bias, bias_mixed, lx, spt, nz, *sems = refs[2 * n + 2:]
     g = pl.program_id(0)
+    steps = []
+    if n:
+        steps = gather_steps(ins, outs, orders, *sems)
+        pl.when(g == 0)(greet_all)
+        for k in range(4):
+            pl.when(g == k)(steps[k])
 
     @pl.when(g == 0)
     def _():
@@ -377,7 +384,7 @@
     def body(i, carry):
         tile(tile_at(i), 160, i, bias[pl.ds(pl.multiple_of(160 * i, 16), 160), :], tile_times(i))
         return carry
-    lax.fori_loop(0, 15, body, 0)
+    lax.fori_loop(0, 15, body, 0, unroll=5)
     tile(2048, 336, 15, bias_mixed[...], twice(mixed_times((1, 128))))
     eye = identity(TILE)
 
@@ -388,6 +395,8 @@
         inverse = 1.0 / r[:, 128:256]
         iz_out[rows, :] = inverse
         ao_out[rows, :] = (r[:, 0:128] * inverse).astype(BF16)
+    if n:
+        pl.when(g == 3)(steps[4])
 
 
 def pair_specs():
@@ -402,20 +411,25 @@
     return each + each + halo + wide
 
 
-def attention(fine, coarse, halo, wide):
+def attention(fine, coarse, halo, wide, parts, orders):
     out = pl.BlockSpec((TOK, 128), lambda g: (0, g))
+    n = len(parts)
+    anywhere = pl.BlockSpec(memory_space=pl.ANY)
+    sems = [pltpu.SemaphoreType.DMA((n,)), pltpu.SemaphoreType.DMA((n, 6)), pltpu.SemaphoreType.DMA((n, 6))] if n else []
+    remote = dict(collective_id=4, has_side_effects=True) if n else {}
     return pl.pallas_call(
-        attention_kernel,
+        functools.partial(attention_kernel, n, orders),
         grid=(4,),
-        out_shape=[jax.ShapeDtypeStruct((TOK, D), BF16), jax.ShapeDtypeStruct((TOK, D), F32)],
-        in_specs=pair_specs(),
-        out_specs=[out, out],
+        out_shape=[jax.ShapeDtypeStruct((TOK, D), BF16), jax.ShapeDtypeStruct((TOK, D), F32)]
+        + [jax.ShapeDtypeStruct((4, 2, 2, 2) + a.shape, a.dtype) for a in parts],
+        in_specs=pair_specs() + [anywhere] * n,
+        out_specs=[out, out] + [anywhere] * n,
         scratch_shapes=[VMEM((EXT, 128), BF16), VMEM((EXT, 128), BF16), VMEM((2048, 128), BF16),
                         VMEM((15 * 160, 128), F32), VMEM((336, 128), F32), VMEM((EXT, 128), F32),
-                        VMEM((TOK, 512), BF16), VMEM((256, 2048), BF16)],
-        compiler_params=pltpu.CompilerParams(dimension_semantics=("arbitrary",), vmem_limit_bytes=60 << 20),
+                        VMEM((TOK, 512), BF16), VMEM((256, 2048), BF16)] + sems,
+        compiler_params=pltpu.CompilerParams(dimension_semantics=("arbitrary",), vmem_limit_bytes=60 << 20, **remote),
         name="attention",
-    )(*([fine] * 4 + [coarse] * 4 + [halo] * 3 + [wide] * 3))
+    )(*([fine] * 4 + [coarse] * 4 + [halo] * 3 + [wide] * 3), *parts)
 
 
 def attention_back_kernel(q0, k0, v0, l0, qc, kc, vc, lc, hk, hv, hl, rk, rv, rl, ao, iz, da, dq_out, ext_out,
@@ -476,7 +490,7 @@
     def body(i, carry):
         tile(tile_at(i), 160, i, bias[pl.ds(pl.multiple_of(160 * i, 16), 160), :], 0.125 / tile_times(i))
         return carry
-    lax.fori_loop(0, 15, body, 0)
+    lax.fori_loop(0, 15, body, 0, unroll=5)
     tile(2048, 336, 15, bias_mixed[...], 0.125 / mixed_times((1, 128)))
     eye = identity(TILE)
 
@@ -676,53 +690,68 @@
     return zs, px, py, pc
 
 
-def gather_kernel(n, orders, *refs):
-    ins, outs = refs[:n], refs[n:2 * n]
-    lsem, ssem, rsem = refs[2 * n:]
+def gather_steps(ins, outs, orders, lsem, ssem, rsem):
+    h, s, y, x, c = where_am_i()
+    zs, px, py, pc = peers_of(h, s, y, x, c)
+    n = len(ins)
+
+    def own(i):
+        return pltpu.make_async_copy(ins[i], outs[i].at[h, y, x, c], lsem.at[i])
+
+    def along_z(i, k):
+        return rcopy(ins[i], outs[i].at[h, y, x, c], ssem.at[i, k], rsem.at[i, k], {"head": zs[k]})
+
+    def second(i):
+        src = outs[i].at[:, y, x, c]
+        return rcopy(src, src, ssem.at[i, 3], rsem.at[i, 3], py if orders[i] else px)
+
+    def third(i):
+        src = outs[i].at[:, :, x, c] if orders[i] else outs[i].at[:, y, :, c]
+        return rcopy(src, src, ssem.at[i, 4], rsem.at[i, 4], px if orders[i] else py)
+
+    def fourth(i):
+        src = outs[i].at[:, :, :, c]
+        return rcopy(src, src, ssem.at[i, 5], rsem.at[i, 5], pc)
+
+    def step0():
+        for i in range(n):
+            own(i).start()
+            for k in range(3):
+                along_z(i, k).start()
+
+    def step1():
+        for i in range(n):
+            own(i).wait()
+            for k in range(3):
+                along_z(i, k).wait()
+            second(i).start()
+
+    def step2():
+        for i in range(n):
+            second(i).wait()
+            third(i).start()
+
+    def step3():
+        for i in range(n):
+            third(i).wait()
+            fourth(i).start()
+
+    def step4():
+        for i in range(n):
+            fourth(i).wait()
+    return step0, step1, step2, step3, step4
+
+
+def greet_all():
     h, s, y, x, c = where_am_i()
     zs, px, py, pc = peers_of(h, s, y, x, c)
     greet([{"head": z} for z in zs] + [px, py, pc])
-    pend = []
-    zc = []
-    for i in range(n):
-        own = pltpu.make_async_copy(ins[i], outs[i].at[h, y, x, c], lsem.at[i])
-        own.start()
-        cs = []
-        for k, z in enumerate(zs):
-            cp = rcopy(ins[i], outs[i].at[h, y, x, c], ssem.at[i, k], rsem.at[i, k], {"head": z})
-            cp.start()
-            cs.append(cp)
-        zc.append((own, cs))
-    s2 = []
-    for i in range(n):
-        own, cs = zc[i]
-        own.wait()
-        for cp in cs:
-            cp.wait()
-        dev = px if orders[i] == 0 else py
-        src = outs[i].at[:, y, x, c]
-        cp = rcopy(src, src, ssem.at[i, 3], rsem.at[i, 3], dev)
-        cp.start()
-        s2.append(cp)
-    s3 = []
-    for i in range(n):
-        s2[i].wait()
-        if orders[i] == 0:
-            src, dev = outs[i].at[:, y, :, c], py
-        else:
-            src, dev = outs[i].at[:, :, x, c], px
-        cp = rcopy(src, src, ssem.at[i, 4], rsem.at[i, 4], dev)
-        cp.start()
-        s3.append(cp)
-    s4 = []
-    for i in range(n):
-        s3[i].wait()
-        src = outs[i].at[:, :, :, c]
-        cp = rcopy(src, src, ssem.at[i, 5], rsem.at[i, 5], pc)
-        cp.start()
-        s4.append(cp)
-    for cp in s4:
-        cp.wait()
+
+
+def gather_kernel(n, orders, *refs):
+    greet_all()
+    for step in gather_steps(refs[:n], refs[n:2 * n], orders, *refs[2 * n:]):
+        step()
 
 
 def gather_all(shards, orders, cid=0, space=pl.ANY):
@@ -851,9 +880,9 @@
     near = lax.axis_size("head") == 4 and lax.axis_size("span") == 8
     if near:
         packed = pack_vectors(first_gain, first_shift, project_bias, output_bias, second_gain, second_shift, reduce_bias, expand_bias)
-        wq, wo, w1, w2, vec = gather_all([project_weight.reshape(48, D), output_weight, expand_weight, reduce_weight, packed], ORDERS)
+        wq, vec = gather_all([project_weight.reshape(48, D), packed], (1, 0))
+        parts = [output_weight, expand_weight, reduce_weight]
         wq = wq.reshape(32, 3, 16, D).transpose(1, 0, 2, 3).reshape(3, D, D)
-        wo, w1, w2 = wo.reshape(D, D), w1.reshape(D, FF), w2.reshape(FF, D)
         vecs, b1 = unpack_vectors(vec.reshape(32, 8, 128))
     else:
         def full(v, axis=0):
@@ -862,9 +891,12 @@
         rows = [full(first_gain), full(first_shift), *full(project_bias, 1), full(output_bias), full(second_gain), full(second_shift), full(reduce_bias)]
         vecs = jnp.pad(jnp.stack(rows), ((0, 7), (0, 0)))
         b1 = full(expand_bias)[None]
+        parts = []
     a1, fine, coarse = before_attention(tok, segment_ids, wq, vecs)
     halo, wide = exchange_edges(fine, coarse)
-    ao, iz = attention(fine, coarse, halo, wide)
+    ao, iz, *weights = attention(fine, coarse, halo, wide, parts, (0, 0, 1))
+    if near:
+        wo, w1, w2 = weights[0].reshape(D, D), weights[1].reshape(D, FF), weights[2].reshape(FF, D)
     out, dh1, da, gwo, gw1, gw2, gvec, gb1 = middle(tok, ao, cot, wo, w1, w2, vecs, b1)
     dq, ext = attention_back(fine, coarse, halo, wide, ao, iz, da)
     halo_b, wide_b = return_edges(ext)

time: 297 us -> 276 us (0.929)
  Pallas kernels: 271 us -> 251 us
    pallas_call x1, Pallas kernels: 49.6 us -> 28 us  [gather_all(): pl.pallas_call(functools.partial(gather_kernel, n, orders), out_shape=[ja...]
    pallas_call x1, Pallas kernels: 33.7 us -> 42 us  [attention(): pl.pallas_call(functools.partial(attention_kernel, n, orders), grid=(4,),...]
    pallas_call x1, Pallas kernels: 44.6 us -> 36.3 us  [attention_back(): pl.pallas_call(attention_back_kernel, grid=(4,), out_shape=[jax.ShapeDtyp...]
where the time goes in v2:
time: 276 us
  Pallas kernels  251 us (91%)
  local copies, waits for them, and re-layouts  21.3 us (8%)
  other arithmetic  2.8 us (1%)
    pallas_call x1, Pallas kernels, scatter_all(): pl.pallas_call(functools.partial(scatter_kernel, n, orders), out_shape=[j...  51.2 us
    pallas_call x1, Pallas kernels, attention(): pl.pallas_call(functools.partial(attention_kernel, n, orders), grid=(4,),...  42 us
    pallas_call x1, Pallas kernels, attention_back(): pl.pallas_call(attention_back_kernel, grid=(4,), out_shape=[jax.ShapeDtyp...  36.3 us
    pallas_call x1, Pallas kernels, gather_all(): pl.pallas_call(functools.partial(gather_kernel, n, orders), out_shape=[ja...  28 us
    pallas_call x1, Pallas kernels, middle(): pl.pallas_call(middle_kernel, grid=(TOK // TILE,), out_shape=[S((TOK, D),...  27.1 us
    pallas_call x1, Pallas kernels, exchange_edges(): pl.pallas_call(edges_kernel, out_shape=[jax.ShapeDtypeStruct((2, 7, 16, l...  22.7 us
    pallas_call x1, Pallas kernels, return_edges(): pl.pallas_call(edges_back_kernel, out_shape=[jax.ShapeDtypeStruct((2, 7,...  20.9 us
    pallas_call x1, Pallas kernels, after_attention(): pl.pallas_call(post_kernel, grid=(TOK // TILE,), out_shape=[S((TOK, D), B...  12.3 us

profile of v2, /device:TPU:0, one launch (start us, length us, event | category | flops | bytes accessed | tf_op | source)
XLA Modules:
  0.0 275.5 jit_solution(16191415977952330605)
XLA Ops:
  0.6 0.7 reshape.93
  1.4 0.8 stack.24
  2.1 0.1 pad.19.clone
  2.2 1.3 fusion.1.refs_1_
  3.5 28.0 %gather_params.1 = (bf16[4,2,2,2,48,512]{5,4,3,2,1,0:T(8,128)(2,1)}, f32[4,2,2,2,8,128]{5,4,3,2,1,0:T(8,128)}) custom-call(bf16[48,512]{1,0:T(8,128)(2,1)} %bitcast.73, f32[8,128]{1,0:T(8,128)} %fusion.1.refs_1_), custom_call_target="tpu_custom_call" | custom-call | tf_op jit(solution)/shard_map/gather_params/pallas_call | solution.py:759
  31.5 0.0 copy-start
  31.5 2.8 copy.33
  34.3 0.0 copy-done
  34.3 0.1 copy.39
  34.4 0.1 copy.35
  34.5 0.8 reshape.98.vecs
  35.3 10.0 %before_attention.1 = (bf16[1024,512]{1,0:T(8,128)(2,1)}, bf16[1024,1664]{1,0:T(8,128)(2,1)}, bf16[1024,1664]{1,0:T(8,128)(2,1)}) custom-call(bf16[1024,512]{1,0:T(8,128)(2,1)} %bitcast.52, s32[1,4096]{1,0:T(1,128)} %seg.1, bf16[3,512,512]{2,1,0:T(8,128)(2,1)} %bitcast.50, f32[16,512]{1,0:T(8,128)} %reshape.98.vecs), custom_call_target="tpu_custom_call" | custom-call | tf_op jit(solution)/shard_map/before_attention/pallas_call | solution.py:149
  45.4 22.7 %exchange_edges.1 = (bf16[2,7,16,1152]{3,2,1,0:T(8,128)(2,1)}, bf16[8,16,1152]{2,1,0:T(8,128)(2,1)}) custom-call(bf16[1024,1664]{1,0:T(8,128)(2,1)} %get-tuple-element.48.fine.q0.k0.v0.l0, bf16[1024,1664]{1,0:T(8,128)(2,1)} %get-tuple-element.49.coarse.qc.kc.vc.lc), custom_call_target="tpu_custom_call" | custom-call | tf_op jit(solution)/shard_map/exchange_edges/pallas_call | solution.py:213
  68.1 42.0 %attention.1 = (bf16[1024,512]{1,0:T(8,128)(2,1)}, f32[1024,512]{1,0:T(8,128)}, bf16[4,2,2,2,16,512]{5,4,3,2,1,0:T(8,128)(2,1)}, bf16[4,2,2,2,16,2048]{5,4,3,2,1,0:T(8,128)(2,1)}, bf16[4,2,2,2,64,512]{5,4,3,2,1,0:T(8,128)(2,1)}) custom-call(bf16[1024,1664]{1,0:T(8,128)(2,1)} %get-tuple-element.48.fine.q0.k0.v0.l0, ...), custom_call_target="tpu_custom_call" | custom-call | tf_op jit(solution)/shard_map/attention/pallas_call | solution.py:420
  110.0 0.1 slice.62
  110.1 0.7 reshape.102.b1
  110.9 27.1 %middle.1 = (bf16[1024,512]{1,0:T(8,128)(2,1)}, f32[1024,512]{1,0:T(8,128)}, bf16[1024,512]{1,0:T(8,128)(2,1)}, bf16[512,512]{1,0:T(8,128)(2,1)}, bf16[512,2048]...) custom-call(bf16[1024,512]{1,0:T(8,128)(2,1)} %bitcast.53, ...), custom_call_target="tpu_custom_call" | custom-call | tf_op jit(solution)/shard_map/middle/pallas_call | solution.py:591
  138.0 36.3 %attention_back.1 = (bf16[1024,512]{1,0:T(8,128)(2,1)}, bf16[2,2384,512]{2,1,0:T(8,128)(2,1)}) custom-call(bf16[1024,1664]{1,0:T(8,128)(2,1)} %get-tuple-element.48.fine.q0.k0.v0.l0, bf16[1024,1664]{1,0:T(8,128)(2,1)} %get-tuple-element.48.fine.q0.k0.v0.l0, bf16[1024,1664]{1,0:T(8,128)(2,1)} %get-tuple-element.48.fine.q0.k0.v0.l0, ...), custom_call_target="tpu_custom_call" | custom-call | tf_op jit(solution)/shard_map/attention_back/pallas_call | solution.py:508
  174.4 20.9 %return_edges.1 = (bf16[2,7,2,16,512]{4,3,2,1,0:T(8,128)(2,1)}, bf16[8,2,16,512]{3,2,1,0:T(8,128)(2,1)}) custom-call(bf16[2,2384,512]{2,1,0:T(8,128)(2,1)} %get-tuple-element.61.ext), custom_call_target="tpu_custom_call" | custom-call | tf_op jit(solution)/shard_map/return_edges/pallas_call | solution.py:247
  195.2 12.3 %after_attention.1 = (bf16[1024,512]{1,0:T(8,128)(2,1)}, bf16[3,512,512]{2,1,0:T(8,128)(2,1)}, f32[8,512]{1,0:T(8,128)}) custom-call(bf16[1024,512]{1,0:T(8,128)(2,1)} %bitcast.54, bf16[1024,512]{1,0:T(8,128)(2,1)} %get-tuple-element.57.a1, bf16[1024,512]{1,0:T(8,128)(2,1)} %get-tuple-element.60.dq, bf16[2,2384,512]{2,1,0:T(8,128)(2,1)} %get-tuple-element.61.ext, ...), custom_call_target="tpu_custom_call" | custom-call | tf_op jit(solution)/shard_map/after_attention/pallas_call | solution.py:667
  207.6 0.0 copy-start.2
  207.6 0.0 copy-start.1
  207.6 2.7 copy.36
  210.3 0.5 broadcast.21
  210.8 0.0 copy-done.2
  210.8 0.7 reduce.7
  211.4 0.1 concatenate.20
  211.6 0.7 slice_reduce_fusion
  212.3 0.1 reshape_squeeze.3
  212.4 0.8 slice.50
  213.2 0.0 copy-done.1
  213.2 0.1 reshape.108
  213.3 0.1 copy.37
  213.4 0.8 maximum_maximum_fusion.refs_4_
  214.2 51.2 %scatter_grads.1 = (f32[48,512]{1,0:T(8,128)}, f32[16,512]{1,0:T(8,128)}, f32[16,2048]{1,0:T(8,128)}, f32[64,512]{1,0:T(8,128)}, f32[8,128]{1,0:T(8,128)}) custom-call(bf16[4,2,2,2,48,512]{5,4,3,2,1,0:T(8,128)(2,1)} %bitcast.55, bf16[4,2,2,2,16,512]{5,4,3,2,1,0:T(8,128)(2,1)} %bitcast.63, bf16[4,2,2,2,16,2048]{5,4,3,2,1,0:T(8,128)(2,1)} %bitcast.56, ...), custom_call_target="tpu_custom_call" | custom-call | tf_op jit(solution)/shard_map/scatter_grads/pallas_call | solution.py:842
  265.4 1.5 slice_bitcast_fusion
  266.9 1.3 slice.55
  268.2 0.7 slice.59
  268.9 0.6 reshape.110
  269.5 1.5 copy.45
  271.0 1.4 copy.46
  272.4 1.6 copy.47
  274.0 1.6 copy.48
  (3 shorter events, 0.0 us)
Async XLA Ops:
  31.5 2.8 %copy-start = (f32[4,2,2,2,8,128]{5,4,3,2,1,0:T(8,128)S(1)}, f32[4,2,2,2,8,128]{5,4,3,2,1,0:T(8,128)}, u32[]{:S(2)}) copy-start(f32[4,2,2,2,8,128]{5,4,3,2,1,0:T(8,128)} %get-tuple-element.47) | copy-start | bytes 393220
  207.6 3.2 %copy-start.2 = (f32[1,2048]{1,0:T(1,128)S(1)}, f32[1,2048]{1,0:T(1,128)}, u32[]{:S(2)}) copy-start(f32[1,2048]{1,0:T(1,128)} %get-tuple-element.72) | copy-start | bytes 24580
  207.6 5.6 %copy-start.1 = (f32[8,512]{1,0:T(8,128)S(1)}, f32[8,512]{1,0:T(8,128)}, u32[]{:S(2)}) copy-start(f32[8,512]{1,0:T(8,128)} %get-tuple-element.70) | copy-start | bytes 49156

commit v3 on v0

v3 whole, which is shorter than its diff:
```python
import functools
import jax
import jax.numpy as jnp
from jax import lax
from jax.experimental import pallas as pl
from jax.experimental.pallas import tpu as pltpu
from jax.sharding import PartitionSpec as P

F32, BF16, I32 = jnp.float32, jnp.bfloat16, jnp.int32
MESH = pl.DeviceIdType.MESH
VMEM = pltpu.VMEM
NEG = -1e30
EPS = 1e-5
TOK = 1024
TILE = 256
D = 512
FF = 2048
EXT = 2384
SIZES = (1024, 512, 256, 128, 64, 32, 16)
EXT_AT = (0, 1056, 1600, 1888, 2048, 2144, 2208)
WIDE_AT = 2256
TRANS_B = (((1,), (1,)), ((), ()))
TRANS_A = (((0,), (0,)), ((), ()))


def mm(a, b):
    return jnp.dot(a, b, preferred_element_type=F32)


def mm_bt(a, b):
    return lax.dot_general(a, b, TRANS_B, preferred_element_type=F32)


def mm_at(a, b):
    return lax.dot_general(a, b, TRANS_A, preferred_element_type=F32)


def iota(shape, dim):
    return lax.broadcasted_iota(I32, shape, dim)


def split(v):
    high = v.astype(BF16)
    return high, (v - high.astype(F32)).astype(BF16)


def covers(t, c, block):
    if block == 0:
        return ((t & 255) >> 1) == c
    if block == 1:
        return ((t & 511) >> 2) == c
    if block == 2:
        return (t >> 3) == c
    level, start = mixed_levels(c)
    return (jnp.right_shift(t, level) == c - start) & (c < 124)


def mixed_levels(c):
    a, b, d, e = ((c >= edge).astype(I32) for edge in (64, 96, 112, 120))
    return 4 + a + b + d + e, 64 * a + 32 * b + 16 * d + 8 * e


def ones_where(cond):
    return jnp.where(cond, 1.0, 0.0).astype(BF16)


def identity(n):
    return ones_where(iota((n, n), 0) == iota((n, n), 1))


def fill_spread(spt):
    @pl.loop(0, TOK // TILE)
    def _(j):
        for block in range(4):
            t = iota((TILE, 128), 0) + j * TILE
            c = iota((TILE, 128), 1)
            spt[pl.ds(j * TILE, TILE), 128 * block:128 * block + 128] = ones_where(covers(t, c, block))


def fill_pool(sp):
    @pl.loop(0, TOK // TILE)
    def _(j):
        for block in range(4):
            t = iota((128, TILE), 1) + j * TILE
            c = iota((128, TILE), 0)
            sp[128 * block:128 * block + 128, pl.ds(pl.multiple_of(j * TILE, TILE), TILE)] = ones_where(covers(t, c, block))


TILES = TOK // TILE
LABEL = 2 * D
WIDE = 2 * D + 128
BIAS_MIXED = 15 * 160
BIASES = BIAS_MIXED + 336


def tile_level(i):
    return 0 if i < 8 else 1 if i < 12 else 2 if i < 14 else 3


def tile_at(i):
    return 2048 if i == 15 else 128 * i + 32 * tile_level(i)


def tile_keys(i):
    return 336 if i == 15 else 160


def tile_times(i):
    if i < 15:
        return float(2 ** tile_level(i))
    level, _unused = mixed_levels(iota((1, 128), 1))
    return (1 << level).astype(F32)


INNER = (1, 2, 3, 4, 5, 6, 9, 10)
OUTER = (0, 7, 8, 11, 12, 13, 14, 15)


def labels_of(total, squares, times):
    return jnp.where(times * squares == total * total, total / times, 0.0)


def head_masks(rows):
    lane = iota((rows, 128), 1)
    return ones_where(lane < 64), ones_where(lane >= 64)


def by_head(x, masks):
    return jnp.concatenate([x * masks[0], x * masks[1]], axis=0)


def own_blocks(x):
    return jnp.concatenate([x[0:64, 0:128], x[64:128, 128:256]], axis=0)


def twice(x):
    return jnp.concatenate([x, x], axis=1)


def two_rows(a, b):
    row = iota((16, a.shape[1]), 0)
    return jnp.where(row == 0, a, jnp.where(row == 1, b, 0.0))


def lanes_of(g, base=0):
    return pl.ds(pl.multiple_of(base + g * 128, 128), 128)


def coarse_cols(ref, base, j):
    return jnp.concatenate([ref[:, base + 128 * j:base + 128 * j + 128],
                            ref[:, base + 512 + 128 * (j // 2):base + 640 + 128 * (j // 2)],
                            ref[:, base + 768:base + 1024]], axis=1)


def coarse_blocks():
    return ([(128 * j, 0, 256 * j, 256) for j in range(4)] + [(512 + 128 * j, 1, 512 * j, 512) for j in range(2)]
            + [(768, 2, 0, 1024), (896, 3, 0, 1024)])


def where_am_i():
    h = lax.axis_index("head")
    s = lax.axis_index("span")
    return h, s, s // 4, (s // 2) % 2, s % 2


class Peers:
    def __init__(self, near):
        h, s = lax.axis_index("head"), lax.axis_index("span")
        odd = s % 2
        self.place = odd * 4 + h
        self.odd = odd
        self.h = h
        other = s + 1 - 2 * odd
        self.z_index = [lax.rem(h + d, 4) for d in (1, 2, 3)]
        self.zs = [{"head": z} for z in self.z_index]
        self.core = {"span": other}
        opposite = {"head": 3 - h, "span": other}
        step = 1 - 2 * odd
        self.right = {"head": lax.rem(h + 1, 4), "span": s + step * ((h + 1) // 4)}
        self.left = {"head": lax.rem(h + 3, 4), "span": s + step * (1 - (h + 3) // 4)}
        self.greeted = self.zs + [self.core, opposite]
        if near:
            y, x = s // 4, (s // 2) % 2
            self.y, self.x, self.c = y, x, odd
            self.px = {"span": y * 4 + (1 - x) * 2 + odd}
            self.py = {"span": (1 - y) * 4 + x * 2 + odd}
            self.greeted += [self.px, self.py]


def greet(devices):
    barrier = pltpu.get_barrier_semaphore()
    for d in devices:
        pl.semaphore_signal(barrier, inc=1, device_id=d, device_id_type=MESH)
    pl.semaphore_wait(barrier, len(devices))


def rcopy(src, dst, send, recv, device):
    return pltpu.make_async_remote_copy(src_ref=src, dst_ref=dst, send_sem=send, recv_sem=recv,
                                        device_id=device, device_id_type=MESH)


class Gather:
    def __init__(self, me, shard, full, swap, local, send, recv):
        self.me, self.shard, self.full, self.swap, self.local, self.send, self.recv = me, shard, full, swap, local, send, recv

    def own(self):
        m = self.me
        return pltpu.make_async_copy(self.shard, self.full(m.h, m.y, m.x, m.c), self.local)

    def hop(self, k):
        m, a = self.me, slice(None)
        if k < 3:
            return rcopy(self.shard, self.full(m.h, m.y, m.x, m.c), self.send.at[k], self.recv.at[k], m.zs[k])
        if k == 3:
            ref, dev = self.full(a, m.y, m.x, m.c), m.py if self.swap else m.px
        elif k == 4:
            ref, dev = (self.full(a, a, m.x, m.c), m.px) if self.swap else (self.full(a, m.y, a, m.c), m.py)
        else:
            ref, dev = self.full(a, a, a, m.c), m.core
        return rcopy(ref, ref, self.send.at[k], self.recv.at[k], dev)

    def start(self, stage):
        if stage == 0:
            self.own().start()
            for k in range(3):
                self.hop(k).start()
        else:
            self.hop(2 + stage).start()

    def wait(self, stage):
        if stage == 0:
            self.own().wait()
            for k in range(3):
                self.hop(k).wait()
        else:
            self.hop(2 + stage).wait()


class Scatter:
    def __init__(self, me, grad, mine, swap, bufs, send, recv):
        self.me, self.grad, self.mine, self.swap, self.bufs, self.send, self.recv = me, grad, mine, swap, bufs, send, recv

    def hops(self, stage):
        m, s, r = self.me, self.send, self.recv
        r1, r2, r3, r4 = self.bufs
        if stage == 0:
            return [rcopy(self.grad(1 - m.c), r1, s.at[0], r.at[0], m.core)]
        if stage == 1:
            src, dev = (r1.at[:, 1 - m.y], m.py) if self.swap else (r1.at[:, :, 1 - m.x], m.px)
            return [rcopy(src, r2, s.at[1], r.at[1], dev)]
        if stage == 2:
            src, dev = (r2.at[:, 1 - m.x], m.px) if self.swap else (r2.at[:, 1 - m.y], m.py)
            return [rcopy(src, r3, s.at[2], r.at[2], dev)]
        return [rcopy(r3.at[m.z_index[k]], r4.at[k], s.at[3 + k], r.at[3 + k], m.zs[k]) for k in range(3)]

    def start(self, stage):
        for cp in self.hops(stage):
            cp.start()

    def wait(self, stage):
        for cp in self.hops(stage):
            cp.wait()

    def add(self, stage):
        m = self.me
        r1, r2, r3, r4 = self.bufs

        def into(dst, key, other):
            dst[key] = (dst[key].astype(F32) + other.astype(F32)).astype(dst.dtype)
        if stage == 0:
            @pl.loop(0, 4)
            def _(hh):
                for yy in range(2):
                    for xx in range(2):
                        into(r1, (hh, yy, xx), self.mine(hh, yy, xx))
        elif stage == 1:
            @pl.loop(0, 4)
            def _(hh):
                for v in range(2):
                    into(r2, (hh, v), r1[hh, m.y, v] if self.swap else r1[hh, v, m.x])
        else:
            @pl.loop(0, 4)
            def _(hh):
                into(r3, (hh,), r2[hh, m.x if self.swap else m.y])

    def result(self):
        r1, r2, r3, r4 = self.bufs
        acc = r3[self.me.h].astype(F32)
        for k in range(3):
            acc = acc + r4[k].astype(F32)
        return acc


def scatter_bufs(shape, dtype):
    return [VMEM((4, 2, 2) + shape, dtype), VMEM((4, 2) + shape, dtype), VMEM((4,) + shape, dtype), VMEM((3,) + shape, dtype)]


def split3(v):
    high, rest = split(v)
    mid = rest
    low = (v - high.astype(F32) - mid.astype(F32)).astype(BF16)
    return high, mid, low


def mm_exact(v, ones):
    a, b, c = split3(v)
    return mm(a, ones) + mm(b, ones) + mm(c, ones)


def small_rows(vt, g1, s1, pb, ob, g2, s2, rb, eb):
    vt[...] = jnp.zeros_like(vt)
    for r, ref in enumerate((g1, s1, None, None, None, ob, g2, s2)):
        vt[r:r + 1, 0:16] = pb[r - 2:r - 1, :] if ref is None else ref[...]
    vt[0:1, 16:32] = rb[...]
    for r in range(8):
        vt[r:r + 1, 32:40] = eb[0:1, 8 * r:8 * r + 8]


def unpack_small(gathered, vecs, b1):
    v = gathered[...].reshape(256, 128)
    row, n = iota((256, D), 0), iota((256, D), 1)
    lane, col = iota((128, D), 0), iota((128, D), 1)
    mine = (row >> 3) == (n >> 4)
    for half in range(2):
        x = mm_exact(v, ones_where(lane == (col & 15) + 16 * half))
        vecs[8 * half:8 * half + 8, :] = jnp.sum(jnp.where(mine, x, 0.0).reshape(32, 8, D), axis=0)
    x = mm_exact(v, ones_where(lane == (col & 7) + 32))
    for q in range(4):
        ok = ((row >> 3) == ((n + 512 * q) >> 6)) & ((row & 7) == ((n >> 3) & 7))
        b1[0:1, D * q:D * q + D] = jnp.sum(jnp.where(ok, x, 0.0), axis=0, keepdims=True)


def fill_bias(bias, kvx, labq, place, tiles):
    def matching(i):
        kl = kvx[tile_at(i):tile_at(i) + tile_keys(i), LABEL:WIDE].astype(F32)
        return (kl == labq[i:i + 1, :]) & (kl != 0.0)

    r, c = iota((160, 128), 0), iota((160, 128), 1)
    near = jnp.abs((r >> 4) - 1 - (c >> 4)) <= 1
    far = near & (jnp.abs((r >> 3) - 2 - (c >> 3)) >= 2)
    same = (r - 16) == c
    for i in tiles:
        if i == 15:
            continue
        ok = matching(i) & near | same if i < 8 else matching(i) & far
        bias[160 * i:160 * i + 160, :] = jnp.where(ok, 0.0, NEG)
    if 15 not in tiles:
        return
    r, c = iota((336, 128), 0), iota((336, 128), 1)
    inner = (r >= 96).astype(I32) + (r >= 160).astype(I32)
    start = jnp.where(inner == 0, 0, jnp.where(inner == 1, 96, 160))
    e, k = (r - 208) >> 4, (r - 208) & 15
    upper = (k >= 8).astype(I32)
    level_k = jnp.where(r < 208, 4 + inner, 7 + upper)
    pos_k = jnp.where(r < 208, r - start - 16, jnp.where(k < 8, e * 8 + k, e * 4 + k - 8))
    level_q, start_q = mixed_levels(c)
    pos_q = c - start_q + jnp.where(level_q == 7, place * 8, jnp.where(level_q == 8, place * 4, 0))
    shape = (level_k == level_q) & (jnp.abs((pos_k >> 4) - (pos_q >> 4)) <= 1) & (jnp.abs((pos_k >> 3) - (pos_q >> 3)) >= 2)
    bias[BIAS_MIXED:BIASES, :] = jnp.where(matching(15) & shape, 0.0, NEG)


def bias_of(bias, i):
    return twice(bias[160 * i:160 * i + 160, :] if i < 15 else bias[BIAS_MIXED:BIASES, :])


def forward_kernel(near, *refs):
    refs = list(refs)

    def take(n):
        out = refs[:n]
        del refs[:n]
        return out
    tok, seg = take(2)
    if near:
        wq_in, = take(1)
        small = take(8)
        ffn_in = take(3)
    else:
        wq, vecs = take(2)
    kvx_o, qx_o, bias_o, a1_o, ao_o, iz_o, sp_o, spt_o = take(8)
    if near:
        wq_o, vecs_o, b1_o = take(3)
        ffn_o = take(3)
    kvx, qx, bias, a1, ao, iz, sp, spt, xh, labq, n0, nc, z0, out_sem, e_send, e_recv = take(16)
    if near:
        wq, vecs, b1, vt, vg, local, send, recv = take(8)
    me = Peers(near)
    place = me.place
    outs = []

    def emit(src, dst):
        cp = pltpu.make_async_copy(src, dst, out_sem.at[len(outs)])
        cp.start()
        outs.append(cp)

    for l, size in enumerate(SIZES):
        kvx[EXT_AT[l]:EXT_AT[l] + 16, :] = jnp.zeros((16, WIDE), BF16)
        kvx[EXT_AT[l] + 16 + size:EXT_AT[l] + 32 + size, :] = jnp.zeros((16, WIDE), BF16)
    if near:
        small_rows(vt, *small)
    greet(me.greeted)
    if near:
        lane = (pl.ds(0, 256), pl.ds(256, 256))
        first = [Gather(me, vt, lambda h, y, x, c: vg.at[h, y, x, c], False, local.at[0], send.at[0], recv.at[0])]
        for k in range(2):
            first.append(Gather(me, wq_in.at[:, :, lane[k]], lambda h, y, x, c, k=k: wq.at[:, h, y, x, c, :, lane[k]], k == 1,
                                local.at[1 + k], send.at[1 + k], recv.at[1 + k]))
        later = [Gather(me, ffn_in[k], lambda h, y, x, c, k=k: ffn_o[k].at[h, y, x, c], k == 2,
                        local.at[3 + k], send.at[3 + k], recv.at[3 + k]) for k in range(3)]

    def advance(group, stage):
        if near:
            for a in (first if group == 0 else later):
                if stage >= 0:
                    a.wait(stage)
                if stage < 3:
                    a.start(stage + 1)

    advance(0, -1)
    fill_pool(sp)
    fill_spread(spt)
    emit(sp, sp_o)
    emit(spt, spt_o)
    advance(0, 0)
    advance(1, -1)
    ids = seg[:, pl.ds(pl.multiple_of(me.h * TOK, TOK), TOK)].astype(F32)
    ids_b = jnp.broadcast_to(ids, (128, TOK)).astype(BF16)
    sq_b = jnp.broadcast_to(ids * ids, (128, TOK)).astype(BF16)
    eye = identity(TILE)
    for j in range(TILES):
        kvx[16 + TILE * j:16 + TILE * j + TILE, LABEL:WIDE] = mm_bt(eye, ids_b[:, TILE * j:TILE * j + TILE]).astype(BF16)
    for i in range(8):
        labq[i:i + 1, :] = ids[:, 128 * i:128 * i + 128]
    wide_at = pl.multiple_of(WIDE_AT + 16 * place, 16)

    def put_coarse(b, value, cols):
        at, block, _t, _n = coarse_blocks()[b]
        if block < 3:
            level = block + 1
            row = EXT_AT[level] + 16 + at - (0, 512, 768)[block]
            kvx[row:row + 128, cols] = value
        else:
            for level, a, n in ((4, 0, 64), (5, 64, 32), (6, 96, 16)):
                kvx[EXT_AT[level] + 16:EXT_AT[level] + 16 + n, cols] = value[a:a + n]
            kvx[pl.ds(wide_at, 16), cols] = value[112:128]

    for b, (at, block, t, n) in enumerate(coarse_blocks()):
        s = sp[128 * block:128 * block + 128, t:t + n]
        rows_level, _unused = mixed_levels(iota((128, 128), 0))
        cols_level, _unused = mixed_levels(iota((8, 128), 1))
        times_r = (1 << rows_level).astype(F32) if block == 3 else float(2 ** (block + 1))
        times_c = (1 << cols_level).astype(F32) if block == 3 else float(2 ** (block + 1))
        lab = labels_of(mm_bt(s, ids_b[:, t:t + n]), mm_bt(s, sq_b[:, t:t + n]), times_r)
        put_coarse(b, lab.astype(BF16), slice(LABEL, WIDE))
        row = labels_of(mm_bt(ids_b[0:8, t:t + n], s), mm_bt(sq_b[0:8, t:t + n], s), times_c)
        labq[8 + b:9 + b, :] = row[0:1, :]
    fill_bias(bias, kvx, labq, place, INNER)
    advance(0, 1)
    for j in range(TILES):
        v = tok[TILE * j:TILE * j + TILE, :].astype(F32)
        center = v - jnp.mean(v, axis=-1, keepdims=True)
        xh[TILE * j:TILE * j + TILE, :] = center * lax.rsqrt(jnp.mean(center * center, axis=-1, keepdims=True) + EPS)
    advance(0, 2)
    advance(1, 0)
    if near:
        first[0].wait(3)
        unpack_small(vg, vecs, b1)
        emit(vecs, vecs_o)
        emit(b1, b1_o)
    for j in range(TILES):
        rows = slice(TILE * j, TILE * j + TILE)
        a1[rows, :] = (xh[rows, :] * vecs[0:1, :] + vecs[1:2, :]).astype(BF16)
    emit(a1, a1_o)
    if near:
        first[1].wait(3)
        first[2].wait(3)
        emit(wq, wq_o)
    for c in range(3):
        w = wq[c].reshape(D, D)
        for j in range(TILES):
            r = (mm(a1[TILE * j:TILE * j + TILE, :], w) + vecs[2 + c:3 + c, :]).astype(BF16)
            if c == 0:
                qx[TILE * j:TILE * j + TILE, :] = r * jnp.array(0.125, BF16)
            else:
                kvx[16 + TILE * j:16 + TILE * j + TILE, D * (c - 1):D * c] = r
    for b, (at, block, t, n) in enumerate(coarse_blocks()):
        s = sp[128 * block:128 * block + 128, t:t + n]
        if block == 3:
            level, _unused = mixed_levels(iota((128, D), 0))
            shrink = 1.0 / (1 << level).astype(F32)
        else:
            shrink = 0.5 ** (block + 1)
        qx[1024 + at:1024 + at + 128, :] = (mm(s, qx[t:t + n, :]) * shrink).astype(BF16)
        put_coarse(b, (mm(s, kvx[16 + t:16 + t + n, 0:D]) * shrink).astype(BF16), slice(0, D))
        put_coarse(b, mm(s, kvx[16 + t:16 + t + n, D:2 * D]).astype(BF16), slice(D, 2 * D))
    to_right, to_left = [], []
    for l, size in enumerate(SIZES):
        at = EXT_AT[l]
        to_right.append(rcopy(kvx.at[pl.ds(at + size, 16)], kvx.at[pl.ds(at, 16)], e_send.at[l], e_recv.at[l], me.right))
        to_left.append(rcopy(kvx.at[pl.ds(at + 16, 16)], kvx.at[pl.ds(at + 16 + size, 16)], e_send.at[7 + l], e_recv.at[7 + l], me.left))
    own_wide = kvx.at[pl.ds(wide_at, 16)]
    wide_z = [rcopy(own_wide, own_wide, e_send.at[14 + k], e_recv.at[14 + k], me.zs[k]) for k in range(3)]
    four = kvx.at[pl.ds(pl.multiple_of(WIDE_AT + 64 * me.odd, 16), 64)]
    wide_core = rcopy(four, four, e_send.at[17], e_recv.at[17], me.core)
    not_last, not_first = place < 7, place > 0

    @pl.when(not_last)
    def _():
        for cp in to_right:
            cp.start()

    @pl.when(not_first)
    def _():
        for cp in to_left:
            cp.start()
    for cp in wide_z:
        cp.start()
    emit(qx, qx_o)
    masks = head_masks(128)

    def tile(g, i):
        keys = slice(tile_at(i), tile_at(i) + tile_keys(i))
        kw, vw = kvx[keys, lanes_of(g)], kvx[keys, lanes_of(g, D)]
        q = by_head(qx[128 * i:128 * i + 128, lanes_of(g)], masks)
        e = jnp.exp(mm_bt(kw, q) + bias_of(bias, i))
        times = tile_times(i)
        z = jnp.sum(e, axis=0, keepdims=True)
        z0_, z1_ = z[:, 0:128] * times, z[:, 128:256] * times
        n = own_blocks(mm_at(vw, e.astype(BF16)))
        if i < 8:
            cols = slice(128 * i, 128 * i + 128)
            n0[g, :, cols] = n
            z0[g, 0:1, cols] = z0_
            z0[g, 1:2, cols] = z1_
        else:
            cols = slice(128 * i - 1024, 128 * i - 896)
            high, low = split(two_rows(z0_, z1_))
            nc[g, :, cols] = jnp.concatenate([n.astype(BF16), high, low], axis=0)

    def run(tiles, lo, hi):
        @pl.loop(lo, hi)
        def _(g):
            for i in tiles:
                tile(g, i)
    run(INNER, 0, 1)
    advance(1, 1)
    for cp in wide_z:
        cp.wait()
    wide_core.start()
    run(INNER, 1, 4)
    advance(1, 2)

    @pl.when(not_last)
    def _():
        for cp in to_right:
            cp.wait_send()
        for cp in to_left:
            cp.wait_recv()

    @pl.when(not_first)
    def _():
        for cp in to_left:
            cp.wait_send()
        for cp in to_right:
            cp.wait_recv()
    wide_core.wait()
    emit(kvx, kvx_o)
    fill_bias(bias, kvx, labq, place, OUTER)
    emit(bias, bias_o)

    @pl.loop(0, 4)
    def _(g):
        for i in OUTER:
            tile(g, i)
        c_ref = nc.at[g]
        for j in range(TILES):
            cols = slice(TILE * j, TILE * j + TILE)
            r = mm(coarse_cols(c_ref, 0, j), sp[:, cols])
            n = n0[g, :, cols] + r[0:128]
            i0 = 1.0 / (z0[g, 0:1, cols] + r[128:129] + r[144:145])
            i1 = 1.0 / (z0[g, 1:2, cols] + r[129:130] + r[145:146])
            iz[g, 0:1, cols] = i0
            iz[g, 1:2, cols] = i1
            ao[pl.ds(pl.multiple_of(g * 128, 128), 64), cols] = (n[0:64] * i0).astype(BF16)
            ao[pl.ds(pl.multiple_of(g * 128 + 64, 64), 64), cols] = (n[64:128] * i1).astype(BF16)
    emit(ao, ao_o)
    emit(iz, iz_o)
    if near:
        for a in later:
            a.wait(3)
    for cp in outs:
        cp.wait()


ANY = pl.BlockSpec(memory_space=pl.ANY)
IN_VMEM = pl.BlockSpec(memory_space=pltpu.VMEM)
S = jax.ShapeDtypeStruct
SEM = pltpu.SemaphoreType.DMA


def forward(near, tok, seg, *params):
    grid = (4, 2, 2, 2)
    shapes = [S((EXT, WIDE), BF16), S((2048, D), BF16), S((BIASES, 128), F32), S((TOK, D), BF16), S((D, TOK), BF16),
              S((4, 2, TOK), F32), S((512, TOK), BF16), S((TOK, 512), BF16)]
    scratch = [VMEM(s.shape, s.dtype) for s in shapes] + [
        VMEM((TOK, D), F32), VMEM((16, 128), F32), VMEM((4, 128, TOK), F32), VMEM((4, 160, TOK), BF16), VMEM((4, 2, TOK), F32),
        SEM((16,)), SEM((18,)), SEM((18,))]
    if near:
        shapes += [S((3,) + grid + (16, D), BF16), S((16, D), F32), S((1, FF), F32)]
        shapes += [S(grid + a.shape, a.dtype) for a in params[9:]]
        scratch += [VMEM((3,) + grid + (16, D), BF16), VMEM((16, D), F32), VMEM((1, FF), F32), VMEM((8, 128), F32),
                    VMEM(grid + (8, 128), F32), SEM((6,)), SEM((6, 6)), SEM((6, 6))]
        specs = [IN_VMEM] * 9 + [ANY] * 3
    else:
        specs = [IN_VMEM] * 2
    return pl.pallas_call(
        functools.partial(forward_kernel, near),
        out_shape=shapes,
        in_specs=[IN_VMEM, IN_VMEM] + specs,
        out_specs=[ANY] * len(shapes),
        scratch_shapes=scratch,
        compiler_params=pltpu.CompilerParams(collective_id=0, has_side_effects=True, vmem_limit_bytes=60 << 20),
        name="forward",
    )(tok, seg, *params)


C0 = 0.7978845608028654
C1 = 0.044715


def middle_kernel(tok, ao, cot, wo, w1, w2, vecs, b1, out, dh1_out, da_out, gwo, gw1, gw2, gvec, gb1,
                  awo, aw1, aw2, avec, ab1):
    j = pl.program_id(0)

    @pl.when(j == 0)
    def _():
        awo[...] = jnp.zeros_like(awo)
        aw1[...] = jnp.zeros_like(aw1)
        aw2[...] = jnp.zeros_like(aw2)
        avec[...] = jnp.zeros_like(avec)
        ab1[...] = jnp.zeros_like(ab1)
    mixed = ao[...]
    h1 = tok[...].astype(F32) + mm_at(mixed, wo[...]) + vecs[5:6, :]
    center = h1 - jnp.mean(h1, axis=-1, keepdims=True)
    inverse = lax.rsqrt(jnp.mean(center * center, axis=-1, keepdims=True) + EPS)
    xh = center * inverse
    gain = vecs[6:7, :]
    a2 = (xh * gain + vecs[7:8, :]).astype(BF16)
    dy = cot[...]
    y = h1 + vecs[8:9, :]
    da2 = jnp.zeros((TILE, D), F32)
    for k in range(FF // D):
        cols = slice(D * k, D * k + D)
        u = mm(a2, w1[:, cols]) + b1[:, cols]
        u2 = u * u
        th = jnp.tanh(u * (C0 + (C0 * C1) * u2))
        half = 0.5 * (1.0 + th)
        g = (u * half).astype(BF16)
        slope = half + 0.5 * u * (1.0 - th * th) * (C0 + (3.0 * C0 * C1) * u2)
        y = y + mm(g, w2[cols, :])
        du = (mm_bt(dy, w2[cols, :]) * slope).astype(BF16)
        aw2[cols, :] += mm_at(g, dy)
        aw1[:, cols] += mm_at(a2, du)
        ab1[:, cols] += jnp.sum(du.astype(F32), axis=0, keepdims=True)
        da2 = da2 + mm_bt(du, w1[:, cols])
    out[...] = y.astype(BF16)
    dyf = dy.astype(F32)
    e = da2 * gain
    dh1 = dyf + inverse * (e - jnp.mean(e, axis=-1, keepdims=True) - xh * jnp.mean(e * xh, axis=-1, keepdims=True))
    dh1_out[...] = dh1
    db = dh1.astype(BF16)
    awo[...] += mm(mixed, db)
    da_out[...] = mm_bt(wo[...], db).astype(BF16)
    avec[5:6, :] += jnp.sum(db.astype(F32), axis=0, keepdims=True)
    avec[6:7, :] += jnp.sum(da2 * xh, axis=0, keepdims=True)
    avec[7:8, :] += jnp.sum(da2, axis=0, keepdims=True)
    avec[8:9, :] += jnp.sum(dyf, axis=0, keepdims=True)

    @pl.when(j == TOK // TILE - 1)
    def _():
        gwo[...] = awo[...].astype(BF16)
        gw1[...] = aw1[...].astype(BF16)
        gw2[...] = aw2[...].astype(BF16)
        gvec[...] = avec[...]
        gb1[...] = ab1[...]


def whole(shape):
    return pl.BlockSpec(shape, lambda j: (0,) * len(shape), pipeline_mode=pl.Buffered(1))


def middle(tok, ao, cot, wo, w1, w2, vecs, b1):
    tile = pl.BlockSpec((TILE, D), lambda j: (j, 0))
    flat = pl.BlockSpec((D, TILE), lambda j: (0, j))
    return pl.pallas_call(
        middle_kernel,
        grid=(TOK // TILE,),
        out_shape=[S((TOK, D), BF16), S((TOK, D), F32), S((D, TOK), BF16), S((D, D), BF16), S((D, FF), BF16), S((FF, D), BF16),
                   S((16, D), F32), S((1, FF), F32)],
        in_specs=[tile, flat, tile, whole((D, D)), whole((D, FF)), whole((FF, D)), whole((16, D)), whole((1, FF))],
        out_specs=[tile, tile, flat, whole((D, D)), whole((D, FF)), whole((FF, D)), whole((16, D)), whole((1, FF))],
        scratch_shapes=[VMEM((D, D), F32), VMEM((D, FF), F32), VMEM((FF, D), F32), VMEM((16, D), F32), VMEM((1, FF), F32)],
        compiler_params=pltpu.CompilerParams(dimension_semantics=("arbitrary",), vmem_limit_bytes=60 << 20),
        name="middle",
    )(tok, ao, cot, wo, w1, w2, vecs, b1)


def pack_small(rows, b1):
    row, n = iota((256, D), 0), iota((256, D), 1)
    lane, col = iota((128, D), 0), iota((128, D), 1)
    mine = (row >> 3) == (n >> 4)

    def moved(v, ok, ones):
        total = None
        for part in split3(jnp.where(ok, v, 0.0)):
            r = mm_bt(part, ones)
            total = r if total is None else total + r
        return total
    eight = jnp.broadcast_to(rows[0:8][None], (32, 8, D)).reshape(256, D)
    out = moved(eight, mine, ones_where(lane == (col & 15)))
    out = out + moved(jnp.broadcast_to(rows[8:9], (256, D)), mine & ((row & 7) == 0), ones_where(lane == (col & 15) + 16))
    last = ones_where(lane == (col & 7) + 32)
    for q in range(4):
        ok = ((row >> 3) == ((n + 512 * q) >> 6)) & ((row & 7) == ((n >> 3) & 7))
        out = out + moved(jnp.broadcast_to(b1[0:1, D * q:D * q + D], (256, D)), ok, last)
    return out.reshape(4, 2, 2, 2, 8, 128)


def backward_kernel(near, *refs):
    refs = list(refs)

    def take(n):
        out = refs[:n]
        del refs[:n]
        return out
    ins = take(13)
    gffn, (gvec, gb1) = take(3), take(2)
    tok_o, gq_o = take(2)
    small_o = take(8 if near else 1)
    gffn_o = take(3 if near else 0)
    kvx, qx, bias, a1, ao, iz, sp, spt, da, tok, dh1, wq, vecs = take(13)
    gr, rm, dqt, dkv, dq, edge, e_got, w_send, w_got, w_mid, aw, avec, tok_s, in_sem, out_sem, e_send, e_recv = take(17)
    if near:
        gq, gv, f_mine, f_sem, send, recv = take(6)
        bufs = [take(4) for _ in range(6)]
    me = Peers(near)
    place = me.place
    loads = {}
    targets = (da, ao, iz, sp, kvx, qx, bias, spt, a1, tok, dh1, wq, vecs)
    names = ("da", "ao", "iz", "sp", "kvx", "qx", "bias", "spt", "a1", "tok", "dh1", "wq", "vecs")
    for k, name in enumerate(names):
        loads[name] = pltpu.make_async_copy(ins[k], targets[k], in_sem.at[k])
        loads[name].start()
    greet(me.greeted)
    mine_copies = []
    if near:
        lane = (pl.ds(0, 256), pl.ds(256, 256))
        ffn = []
        for k in range(3):
            cp = pltpu.make_async_copy(gffn[k].at[:, :, :, me.c], f_mine[k], f_sem.at[k])
            cp.start()
            mine_copies.append(cp)
            ffn.append(Scatter(me, lambda c, k=k: gffn[k].at[:, :, :, c], lambda h, y, x, k=k: f_mine[k][h, y, x], k == 2,
                               bufs[k], send.at[k], recv.at[k]))
        last = [Scatter(me, lambda c: gv.at[:, :, :, c], lambda h, y, x: gv[h, y, x, me.c], False, bufs[3], send.at[3], recv.at[3])]
        for k in range(2):
            last.append(Scatter(me, lambda c, k=k: gq.at[:, :, :, c, :, :, lane[k]],
                                lambda h, y, x, k=k: gq[h, y, x, me.c, :, :, 256 * k:256 * k + 256], k == 1,
                                bufs[4 + k], send.at[4 + k], recv.at[4 + k]))

    def advance(group, stage):
        for a in group:
            if stage >= 0:
                a.wait(stage)
                a.add(stage)
            a.start(stage + 1)

    if near:
        advance(ffn, -1)
    for name in ("da", "ao", "iz", "sp"):
        loads[name].wait()
    masks = head_masks(128)

    @pl.loop(0, 4)
    def _(g):
        lo, hi = pl.ds(pl.multiple_of(g * 128, 128), 64), pl.ds(pl.multiple_of(g * 128 + 64, 64), 64)
        for j in range(TILES):
            cols = slice(TILE * j, TILE * j + TILE)
            g0 = da[lo, cols].astype(F32) * iz[g, 0:1, cols]
            g1 = da[hi, cols].astype(F32) * iz[g, 1:2, cols]
            r0 = jnp.sum(g0 * ao[lo, cols].astype(F32), axis=0, keepdims=True)
            r1 = jnp.sum(g1 * ao[hi, cols].astype(F32), axis=0, keepdims=True)
            rm[g, 0:1, cols] = r0
            rm[g, 1:2, cols] = r1
            high, low = split(two_rows(r0, r1))
            gr[g, :, cols] = jnp.concatenate([g0.astype(BF16), g1.astype(BF16), high, low], axis=0)
        for b, (at, block, t, n) in enumerate(coarse_blocks()):
            x = mm_bt(gr[g, :, t:t + n], sp[128 * block:128 * block + 128, t:t + n])
            cols = slice(1024 + at, 1152 + at)
            gr[g, 0:128, cols] = x[0:128].astype(BF16)
            times = tile_times(8 + b)
            rm[g, 0:1, cols] = (x[128:129] + x[144:145]) * times
            rm[g, 1:2, cols] = (x[129:130] + x[145:146]) * times
    dkv[...] = jnp.zeros_like(dkv)
    for name in ("kvx", "qx", "bias"):
        loads[name].wait()
    zero = jnp.zeros((64, 128), BF16)

    def tile(g, i):
        keys = slice(tile_at(i), tile_at(i) + tile_keys(i))
        cols = slice(128 * i, 128 * i + 128)
        kw, vw = kvx[keys, lanes_of(g)], kvx[keys, lanes_of(g, D)]
        q = by_head(qx[cols, lanes_of(g)], masks)
        gt = gr[g, 0:128, cols]
        gb = jnp.concatenate([jnp.concatenate([gt[0:64], zero], axis=1), jnp.concatenate([zero, gt[64:128]], axis=1)], axis=0)
        e = jnp.exp(mm_bt(kw, q) + bias_of(bias, i))
        rest = jnp.concatenate([rm[g, 0:1, cols], rm[g, 1:2, cols]], axis=1)
        ds = (e * (mm(vw, gb) - rest)).astype(BF16)
        dkv[keys, lanes_of(g)] += mm(ds, q)
        dkv[keys, lanes_of(g, D)] += mm_bt(e.astype(BF16), gb)
        dqt[g, :, cols] = (own_blocks(mm_at(kw, ds)) * (0.125 / tile_times(i))).astype(BF16)

    def run(tiles, lo, hi):
        @pl.loop(lo, hi)
        def _(g):
            for i in tiles:
                tile(g, i)
    run(OUTER, 0, 4)
    for l, size in enumerate(SIZES):
        edge[0, l] = dkv[EXT_AT[l] + 16 + size:EXT_AT[l] + 32 + size, :].astype(BF16)
        edge[1, l] = dkv[EXT_AT[l]:EXT_AT[l] + 16, :].astype(BF16)
    half_at = pl.multiple_of(WIDE_AT + 64 * (1 - me.odd), 16)
    w_send[...] = dkv[pl.ds(half_at, 64), :].astype(BF16)
    to_right = rcopy(edge.at[0], e_got.at[0], e_send.at[0], e_recv.at[0], me.right)
    to_left = rcopy(edge.at[1], e_got.at[1], e_send.at[1], e_recv.at[1], me.left)
    wide_core = rcopy(w_send, w_mid, e_send.at[2], e_recv.at[2], me.core)
    not_last, not_first = place < 7, place > 0
    wide_core.start()

    @pl.when(not_last)
    def _():
        to_right.start()

    @pl.when(not_first)
    def _():
        to_left.start()
    if near:
        for cp in mine_copies:
            cp.wait()
        advance(ffn, 0)
    run(INNER, 0, 2)
    wide_core.wait()
    own_at = pl.multiple_of(WIDE_AT + 64 * me.odd, 16)
    w_mid[...] = (w_mid[...].astype(F32) + dkv[pl.ds(own_at, 64), :]).astype(BF16)
    wide_z = [rcopy(w_mid.at[pl.ds(pl.multiple_of(16 * me.z_index[k], 16), 16)], w_got.at[k], e_send.at[3 + k], e_recv.at[3 + k], me.zs[k])
              for k in range(3)]
    for cp in wide_z:
        cp.start()
    if near:
        advance(ffn, 1)
    run(INNER, 2, 4)

    @pl.loop(0, 4)
    def _(g):
        d_ref = dqt.at[g]
        eye = identity(TILE)
        for j in range(TILES):
            cols = slice(TILE * j, TILE * j + TILE)
            r = d_ref[:, cols].astype(F32) + mm(coarse_cols(d_ref, 1024, j), sp[:, cols])
            dq[cols, lanes_of(g)] = mm_bt(eye, r.astype(BF16)).astype(BF16)
    for cp in wide_z:
        cp.wait()

    @pl.when(not_last)
    def _():
        to_right.wait_send()
        to_left.wait_recv()
        for l, size in enumerate(SIZES):
            rows = slice(EXT_AT[l] + size, EXT_AT[l] + 16 + size)
            dkv[rows, :] += e_got[1, l].astype(F32)

    @pl.when(not_first)
    def _():
        to_left.wait_send()
        to_right.wait_recv()
        for l, size in enumerate(SIZES):
            rows = slice(EXT_AT[l] + 16, EXT_AT[l] + 32)
            dkv[rows, :] += e_got[0, l].astype(F32)
    v = w_mid[pl.ds(pl.multiple_of(16 * me.h, 16), 16), :].astype(F32)
    for k in range(3):
        v = v + w_got[k].astype(F32)
    wide_row, wide_lane = iota((16, 2 * D), 0), iota((16, 2 * D), 1)
    w_own = (v * jnp.where(wide_lane >= D, 1.0, jnp.where(wide_row < 8, 0.5 ** 7, 0.5 ** 8))).astype(BF16)
    lane_all = iota((1, 2 * D), 1)

    def coarse_rows(at, n, level):
        return (dkv[at:at + n, :] * jnp.where(lane_all < D, 0.5 ** level, 1.0)).astype(BF16)
    for name in ("spt", "a1", "tok", "dh1", "wq", "vecs"):
        loads[name].wait()
    top = jnp.concatenate([coarse_rows(EXT_AT[3] + 16, 128, 3), coarse_rows(EXT_AT[4] + 16, 64, 4), coarse_rows(EXT_AT[5] + 16, 32, 5),
                           coarse_rows(EXT_AT[6] + 16, 16, 6), w_own], axis=0)
    avec[...] = jnp.zeros_like(avec)
    aw[...] = jnp.zeros_like(aw)
    if near:
        avec[5:9, :] = gvec[5:9, :]
        advance(ffn, 2)
    for j in range(TILES):
        rows = slice(TILE * j, TILE * j + TILE)
        x = jnp.concatenate([coarse_rows(EXT_AT[1] + 16 + 128 * j, 128, 1), coarse_rows(EXT_AT[2] + 16 + 128 * (j // 2), 128, 2), top], axis=0)
        d = (dkv[16 + TILE * j:16 + TILE * j + TILE, :] + mm(spt[rows, :], x)).astype(BF16)
        parts = (dq[rows, :], d[:, 0:D], d[:, D:2 * D])
        a = a1[rows, :]
        da1 = jnp.zeros((TILE, D), F32)
        for c in range(3):
            aw[c] += mm_at(a, parts[c])
            avec[2 + c:3 + c, :] += jnp.sum(parts[c].astype(F32), axis=0, keepdims=True)
            da1 = da1 + mm_bt(parts[c], wq[c].reshape(D, D))
        v = tok[rows, :].astype(F32)
        center = v - jnp.mean(v, axis=-1, keepdims=True)
        inverse = lax.rsqrt(jnp.mean(center * center, axis=-1, keepdims=True) + EPS)
        n = center * inverse
        e = da1 * vecs[0:1, :]
        dv = inverse * (e - jnp.mean(e, axis=-1, keepdims=True) - n * jnp.mean(e * n, axis=-1, keepdims=True))
        tok_s[rows, :] = (dh1[rows, :] + dv).astype(BF16)
        avec[0:1, :] += jnp.sum(da1 * n, axis=0, keepdims=True)
        avec[1:2, :] += jnp.sum(da1, axis=0, keepdims=True)
    done = pltpu.make_async_copy(tok_s, tok_o, out_sem.at[0])
    done.start()
    if not near:
        gq_o[...] = aw[...].astype(BF16)
        small_o[0][...] = avec[...]
        done.wait()
        return
    for c in range(3):
        gq[:, :, :, :, c] = aw[c].astype(BF16).reshape(4, 2, 2, 2, 16, D)
    for a in last[1:]:
        a.start(0)
    gv[...] = pack_small(avec[...], gb1)
    last[0].start(0)
    for a in ffn:
        a.wait(3)
    for k in range(3):
        gffn_o[k][...] = ffn[k].result()
    for stage in range(3):
        for a in last:
            a.wait(stage)
            a.add(stage)
            a.start(stage + 1)
    for a in last:
        a.wait(3)
    gq_o[:, :, 0:256] = last[1].result()
    gq_o[:, :, 256:512] = last[2].result()
    t = last[0].result()
    for k, r in enumerate((0, 1, None, 5, 6, 7)):
        if r is None:
            small_o[k][...] = t[2:5, 0:16]
        else:
            small_o[k][...] = t[r:r + 1, 0:16]
    small_o[6][...] = t[:, 32:40]
    small_o[7][...] = t[0:1, 16:32]
    done.wait()


def backward(near, saved, wq, vecs, tok, da, dh1, gffn, gvec, gb1):
    kvx, qx, bias, a1, ao, iz, sp, spt = saved
    grid = (4, 2, 2, 2)
    vm = [VMEM(v.shape, v.dtype) for v in (kvx, qx, bias, a1, ao, iz, sp, spt, da, tok, dh1, wq, vecs)]
    scratch = vm + [VMEM((4, 160, 2048), BF16), VMEM((4, 2, 2048), F32), VMEM((4, 128, 2048), BF16), VMEM((EXT, 2 * D), F32),
                    VMEM((TOK, D), BF16), VMEM((2, 7, 16, 2 * D), BF16), VMEM((2, 7, 16, 2 * D), BF16), VMEM((64, 2 * D), BF16),
                    VMEM((3, 16, 2 * D), BF16), VMEM((64, 2 * D), BF16), VMEM((3, D, D), F32), VMEM((16, D), F32), VMEM((TOK, D), BF16),
                    SEM((13,)), SEM((1,)), SEM((6,)), SEM((6,))]
    if near:
        gffn = [g.reshape(grid + (g.shape[0] // 32, g.shape[1])) for g in gffn]
        shapes = [S((TOK, D), BF16), S((3, 16, D), F32)]
        shapes += [S((1, 16), F32), S((1, 16), F32), S((3, 16), F32), S((1, 16), F32), S((1, 16), F32), S((1, 16), F32), S((8, 8), F32), S((1, 16), F32)]
        shapes += [S(g.shape[4:], F32) for g in gffn]
        pieces = [(g.shape[4:], BF16) for g in gffn] + [((8, 128), F32), ((3, 16, 256), BF16), ((3, 16, 256), BF16)]
        scratch += [VMEM(grid + (3, 16, D), BF16), VMEM(grid + (8, 128), F32), [VMEM((4, 2, 2) + g.shape[4:], BF16) for g in gffn], SEM((3,)),
                    SEM((6, 6)), SEM((6, 6))]
        for shape, kind in pieces:
            scratch += scatter_bufs(shape, kind)
    else:
        gffn = gffn[0:3]
        shapes = [S((TOK, D), BF16), S((3, D, D), BF16), S((16, D), F32)]
    ordered = (da, ao, iz, sp, kvx, qx, bias, spt, a1, tok, dh1, wq, vecs)
    return pl.pallas_call(
        functools.partial(backward_kernel, near),
        out_shape=shapes,
        in_specs=[ANY] * 16 + [IN_VMEM] * 2,
        out_specs=[ANY] + [IN_VMEM] * (len(shapes) - 1),
        scratch_shapes=scratch,
        compiler_params=pltpu.CompilerParams(collective_id=1, has_side_effects=True, vmem_limit_bytes=62 << 20),
        name="backward",
    )(*ordered, *gffn, gvec, gb1)


BOTH = ("head", "span")


def shards(tokens, segment_ids, first_gain, first_shift, project_weight, project_bias, output_weight, output_bias,
           second_gain, second_shift, expand_weight, expand_bias, reduce_weight, reduce_bias, cotangent):
    tok, cot = tokens[0], cotangent[0]
    near = lax.axis_size("head") == 4 and lax.axis_size("span") == 8
    if near:
        vectors = (first_gain, first_shift, project_bias, output_bias, second_gain, second_shift, reduce_bias, expand_bias)
        vectors = [v if v.ndim == 2 else v[None] for v in vectors]
        *saved, wq, vecs, b1, wo, w1, w2 = forward(True, tok, segment_ids, project_weight, *vectors, output_weight, expand_weight, reduce_weight)
        wo, w1, w2 = wo.reshape(D, D), w1.reshape(D, FF), w2.reshape(FF, D)
    else:
        def full(v, axis=0):
            return lax.all_gather(v, BOTH, axis=axis, tiled=True)
        wq, wo, w1, w2 = full(project_weight, 1), full(output_weight), full(expand_weight), full(reduce_weight)
        rows = [full(first_gain), full(first_shift), *full(project_bias, 1), full(output_bias), full(second_gain), full(second_shift), full(reduce_bias)]
        vecs = jnp.pad(jnp.stack(rows), ((0, 7), (0, 0)))
        b1 = full(expand_bias)[None]
        saved = forward(False, tok, segment_ids, wq, vecs)
    ao = saved[4]
    out, dh1, da, *gffn, gvec, gb1 = middle(tok, ao, cot, wo, w1, w2, vecs, b1)
    dtok, gwq, *rest = backward(near, saved, wq, vecs, tok, da, dh1, gffn, gvec, gb1)
    if near:
        small, (gwo, gw1, gw2) = rest[0:8], rest[8:11]
        small = [v if v.shape[0] == 3 else v.reshape(-1) for v in small]
    else:
        def part(v, axis=0):
            return lax.psum_scatter(v.astype(F32), BOTH, scatter_dimension=axis, tiled=True)
        vec = rest[0]
        gwq, gwo, gw1, gw2 = part(gwq, 1), part(gffn[0]), part(gffn[1]), part(gffn[2])
        small = (part(vec[0]), part(vec[1]), part(vec[2:5], 1), part(gvec[5]), part(gvec[6]), part(gvec[7]), part(gb1[0]), part(gvec[8]))
    return (out[None], dtok[None], small[0], small[1], gwq, small[2], gwo, small[3], small[4], small[5], gw1, small[6], gw2, small[7])


def solution(mesh):
    token, row, matrix = P("span", "head", None), P(BOTH), P(BOTH, None)
    three, bias = P(None, BOTH, None), P(None, BOTH)
    params = (row, row, three, bias, matrix, row, row, row, matrix, row, matrix, row)
    return jax.shard_map(shards, mesh=mesh, in_specs=(token, P("span", None)) + params + (token,),
                         out_specs=(token, token) + params, check_vma=False)
```

time: 2090 us -> 163 us (0.08)
  waiting for transfers between devices: 689 us -> 0 us
  local copies, waits for them, and re-layouts: 569 us -> 9.85 us
  matrix products: 333 us -> 0 us
  other arithmetic: 271 us -> 0 us
  blocking collectives: 182 us -> 0 us
  Pallas kernels: 0 us -> 152 us
    reduce_scatter x5 -> x0, waiting for transfers between devices: 578 us -> none  [the longest x1 139 us: shards(): lax.psum_scatter(grad_up_w, ('head', 'span'), scatter_dimension=0, tiled=...]
    dot_general x66 -> x0, matrix products: 333 us -> none  [the longest x9 57.3 us: level_backward(): jnp.einsum('hijb,bihd->bjhd', weights, grad_block, precision=highest)]
    pallas_call x0 -> x3, Pallas kernels: none -> 152 us  [the longest x1 67.9 us: backward(): pl.pallas_call(functools.partial(backward_kernel, near), out_shape=shapes...]
    reduce_sum x47 -> x0, other arithmetic: 106 us -> none  [the longest x40 94.5 us: pair_sum(): values_in.reshape((values_in.shape[0] // 2, 2) + values_in.shape[1:])]
    unnamed x573 -> x34, local copies, waits for them, and re-layouts: 109 us -> 8.52 us
    all_gather x2 -> x0, blocking collectives: 98.4 us -> none  [the longest x1 56.8 us: shards(): lax.all_gather(output_weight, ('head', 'span'), axis=0, tiled=True)]
    concatenate x57 -> x0, local copies, waits for them, and re-layouts: 89.8 us -> none  [windows(): return jnp.concatenate([shaped[:-2], shaped[1:-1], shaped[2:]], axis=1)]
    unnamed x11 -> x0, waiting for transfers between devices: 87.3 us -> none
  transfers between devices with their start and end apart: 15 -> 0, of which waited for: 7 -> 0; matrix products, arithmetic and copies ran while one was open for 30% -> 0% of each run, Pallas kernels for 0% -> 0%
where the time goes in v3:
time: 163 us
  Pallas kernels  152 us (93%)
  local copies, waits for them, and re-layouts  9.85 us (6%)
    pallas_call x1, Pallas kernels, backward(): pl.pallas_call(functools.partial(backward_kernel, near), out_shape=shapes...  67.9 us
    pallas_call x1, Pallas kernels, forward(): pl.pallas_call(functools.partial(forward_kernel, near), out_shape=shapes,...  56.1 us
    pallas_call x1, Pallas kernels, middle(): pl.pallas_call(middle_kernel, grid=(TOK // TILE,), out_shape=[S((TOK, D),...  28.2 us
    unnamed x34, local copies, waits for them, and re-layouts  8.52 us

profile of v3, /device:TPU:0, one launch (start us, length us, event | category | flops | bytes accessed | tf_op | source)
XLA Modules:
  0.0 162.8 jit_solution(4244329563653606500)
XLA Ops:
  0.7 56.1 %forward.1 = (bf16[2384,1152]{1,0:T(8,128)(2,1)}, bf16[2048,512]{1,0:T(8,128)(2,1)}, f32[2736,128]{1,0:T(8,128)}, bf16[1024,512]{1,0:T(8,128)(2,1)}, bf16[512,10...) custom-call(bf16[1024,512]{1,0:T(8,128)(2,1)} %bitcast.23, ...), custom_call_target="tpu_custom_call" | custom-call | tf_op jit(solution)/shard_map/forward/pallas_call | solution.py:616
  56.7 28.2 %middle.1 = (bf16[1024,512]{1,0:T(8,128)(2,1)}, f32[1024,512]{1,0:T(8,128)}, bf16[512,1024]{1,0:T(8,128)(2,1)}, bf16[512,512]{1,0:T(8,128)(2,1)}, bf16[512,2048]...) custom-call(bf16[1024,512]{1,0:T(8,128)(2,1)} %bitcast.24, ...), custom_call_target="tpu_custom_call" | custom-call | tf_op jit(solution)/shard_map/middle/pallas_call | solution.py:695
  84.9 67.9 %backward.1 = (bf16[1024,512]{1,0:T(8,128)(2,1)}, f32[3,16,512]{2,1,0:T(8,128)}, f32[1,16]{1,0:T(1,128)}, f32[1,16]{1,0:T(1,128)}, f32[3,16]{1,0:T(4,128)}, /*in...) custom-call(bf16[512,1024]{1,0:T(8,128)(2,1)} %get-tuple-element.56., ...), custom_call_target="tpu_custom_call" | custom-call | tf_op jit(solution)/shard_map/backward/pallas_call | solution.py:986
  152.8 0.0 copy-start.10
  152.8 0.0 copy-start.9
  152.8 0.0 copy-start.2
  152.8 0.0 copy-start.4
  152.8 0.0 copy-start.3
  152.9 0.0 copy-start.8
  152.9 0.0 copy-start.7
  152.9 0.0 copy-start.6
  152.9 0.0 copy-start.1
  152.9 0.0 copy-start
  152.9 0.0 copy-start.5
  152.9 1.3 reshape.78
  154.2 2.3 %copy.41 = bf16[1,1024,512]{2,1,0:T(8,128)(2,1)} copy(bf16[1,1024,512]{2,1,0:T(8,128)(2,1)} %bitcast.31) | data formatting | bytes 2097152
  156.5 0.0 copy-done.10
  156.5 0.5 copy.42
  157.0 0.0 copy-done.9
  157.0 0.5 copy.43
  157.5 0.0 copy-done.2
  157.5 0.6 copy.44
  158.2 0.0 copy-done.4
  158.2 0.6 copy.45
  158.8 0.0 copy-done.3
  158.8 0.6 copy.46
  159.4 0.0 copy-done.8
  159.4 0.5 copy.47
  159.9 0.0 copy-done.7
  159.9 0.5 copy.48
  160.4 0.0 copy-done.6
  160.4 0.5 copy.49
  160.9 0.0 copy-done.1
  160.9 0.7 copy.50
  161.6 0.0 copy-done
  161.6 0.7 copy.51
  162.2 0.0 copy-done.5
  162.2 0.5 copy.52
Async XLA Ops:
  152.8 3.7 %copy-start.10 = (f32[1,16]{1,0:T(1,128)S(1)}, f32[1,16]{1,0:T(1,128)}, u32[]{:S(2)}) copy-start(f32[1,16]{1,0:T(1,128)} %get-tuple-element.72) | copy-start | bytes 196
  152.8 4.2 %copy-start.9 = (f32[1,16]{1,0:T(1,128)S(1)}, f32[1,16]{1,0:T(1,128)}, u32[]{:S(2)}) copy-start(f32[1,16]{1,0:T(1,128)} %get-tuple-element.73) | copy-start | bytes 196
  152.8 4.7 %copy-start.2 = (f32[3,16,512]{2,1,0:T(8,128)S(1)}, f32[3,16,512]{2,1,0:T(8,128)}, u32[]{:S(2)}) copy-start(f32[3,16,512]{2,1,0:T(8,128)} %get-tuple-element.102) | copy-start | bytes 294916
  152.8 5.3 %copy-start.4 = (f32[3,16]{1,0:T(4,128)S(1)}, f32[3,16]{1,0:T(4,128)}, u32[]{:S(2)}) copy-start(f32[3,16]{1,0:T(4,128)} %get-tuple-element.103) | copy-start | bytes 580
  152.8 5.9 %copy-start.3 = (f32[16,512]{1,0:T(8,128)S(1)}, f32[16,512]{1,0:T(8,128)}, u32[]{:S(2)}) copy-start(f32[16,512]{1,0:T(8,128)} %get-tuple-element.104) | copy-start | bytes 98308
  152.9 6.5 %copy-start.8 = (f32[1,16]{1,0:T(1,128)S(1)}, f32[1,16]{1,0:T(1,128)}, u32[]{:S(2)}) copy-start(f32[1,16]{1,0:T(1,128)} %get-tuple-element.77) | copy-start | bytes 196
  152.9 7.0 %copy-start.7 = (f32[1,16]{1,0:T(1,128)S(1)}, f32[1,16]{1,0:T(1,128)}, u32[]{:S(2)}) copy-start(f32[1,16]{1,0:T(1,128)} %get-tuple-element.78) | copy-start | bytes 196
  152.9 7.5 %copy-start.6 = (f32[1,16]{1,0:T(1,128)S(1)}, f32[1,16]{1,0:T(1,128)}, u32[]{:S(2)}) copy-start(f32[1,16]{1,0:T(1,128)} %get-tuple-element.79) | copy-start | bytes 196
  152.9 8.0 %copy-start.1 = (f32[16,2048]{1,0:T(8,128)S(1)}, f32[16,2048]{1,0:T(8,128)}, u32[]{:S(2)}) copy-start(f32[16,2048]{1,0:T(8,128)} %get-tuple-element.108) | copy-start | bytes 393220
  152.9 8.7 %copy-start = (f32[64,512]{1,0:T(8,128)S(1)}, f32[64,512]{1,0:T(8,128)}, u32[]{:S(2)}) copy-start(f32[64,512]{1,0:T(8,128)} %get-tuple-element.110) | copy-start | bytes 393220
  152.9 9.3 %copy-start.5 = (f32[1,16]{1,0:T(1,128)S(1)}, f32[1,16]{1,0:T(1,128)}, u32[]{:S(2)}) copy-start(f32[1,16]{1,0:T(1,128)} %get-tuple-element.83) | copy-start | bytes 196

commit v4 on v3

--- a/solution.py
+++ b/solution.py
@@ -87,8 +87,6 @@
 
 
 TILES = TOK // TILE
-LABEL = 2 * D
-WIDE = 2 * D + 128
 BIAS_MIXED = 15 * 160
 BIASES = BIAS_MIXED + 336
 
@@ -155,6 +153,53 @@
 def coarse_blocks():
     return ([(128 * j, 0, 256 * j, 256) for j in range(4)] + [(512 + 128 * j, 1, 512 * j, 512) for j in range(2)]
             + [(768, 2, 0, 1024), (896, 3, 0, 1024)])
+
+
+def near_rows(side):
+    o, i = iota((96, 128), 0), iota((96, 128), 1)
+    level = (o >> 4) + 1
+    block = i >> 4
+    fine = jnp.maximum(block - 1, 0)
+    value_out, value_in = (o >> 3) & 1, jnp.where(block < 2, block, (i >> 3) & 1)
+    width, size = jnp.left_shift(1, fine), jnp.left_shift(1, level)
+    if side == 0:
+        start = ((o & 7) - 8) * size
+        at = jnp.where(block < 2, (i & 15) - 16, (i & 7) - 16) * width
+    else:
+        start = (o & 7) * size
+        at = jnp.where(block < 2, i & 15, (i & 7) + 8) * width
+    inside = (value_out == value_in) & (at >= start) & (at + width <= start + size)
+    share = jnp.where(value_out == 1, 1.0, width.astype(F32) / size.astype(F32))
+    return jnp.where(inside, share, 0.0).astype(BF16)
+
+
+def wide_rows(value):
+    r, i = iota((128, 128), 0), iota((128, 128), 1)
+    k, j = r & 15, (i & 15) - 8 * value
+    own = ((r >> 4) == (i >> 4)) & (j >= 0) & (j < 8)
+    fine, rough = own & (k < 8) & (j == k), own & (k >= 8) & (k < 12) & ((j >> 1) == k - 8)
+    return jnp.where(fine, 1.0, jnp.where(rough, 1.0 if value else 0.5, 0.0)).astype(BF16)
+
+
+def far_and_near(side, far, near):
+    return jnp.concatenate([far, near] if side == 0 else [near, far], axis=0)
+
+
+def border(side, l):
+    return EXT_AT[l] + (16 + SIZES[l] if side else 0)
+
+
+def own_border(side, l):
+    return EXT_AT[l] + (SIZES[l] if side else 16)
+
+
+def pick_far(side, rows):
+    return rows[0:8] if side else rows[8:16]
+
+
+def column_of(row, n):
+    spread = jnp.where(iota((n, n), 0) == iota((n, n), 1), jnp.broadcast_to(row, (n, n)), 0.0)
+    return jnp.broadcast_to(jnp.sum(spread, axis=1, keepdims=True), (n, 128)).astype(BF16)
 
 
 def where_am_i():
@@ -182,9 +227,12 @@
         if near:
             y, x = s // 4, (s // 2) % 2
             self.y, self.x, self.c = y, x, odd
+            self.s = s
             self.px = {"span": y * 4 + (1 - x) * 2 + odd}
             self.py = {"span": (1 - y) * 4 + x * 2 + odd}
-            self.greeted += [self.px, self.py]
+            self.s_index = [lax.rem(s + d, 8) for d in range(1, 8)]
+            self.spans = [{"span": o} for o in self.s_index]
+            self.greeted = self.zs + self.spans + [opposite]
 
 
 def greet(devices):
@@ -291,6 +339,79 @@
         return acc
 
 
+class SmallGather:
+    def __init__(self, me, tile, full, local, send, recv):
+        self.me, self.tile, self.full, self.local, self.send, self.recv = me, tile, full, local, send, recv
+
+    def first(self):
+        dst = self.full.at[self.me.h, self.me.s]
+        return [rcopy(self.tile, dst, self.send.at[k], self.recv.at[k], self.me.zs[k]) for k in range(3)]
+
+    def second(self):
+        ref = self.full.at[:, self.me.s]
+        return [rcopy(ref, ref, self.send.at[3 + k], self.recv.at[3 + k], self.me.spans[k]) for k in range(7)]
+
+    def own(self):
+        return pltpu.make_async_copy(self.tile, self.full.at[self.me.h, self.me.s], self.local)
+
+
+class SmallScatter:
+    def __init__(self, me, grad, got, total, got_z, send, recv):
+        self.me, self.grad, self.got, self.total, self.got_z, self.send, self.recv = me, grad, got, total, got_z, send, recv
+
+    def first(self):
+        m = self.me
+        return [rcopy(self.grad.at[:, m.s_index[k]], self.got.at[k], self.send.at[k], self.recv.at[k], m.spans[k]) for k in range(7)]
+
+    def second(self):
+        m = self.me
+        return [rcopy(self.total.at[m.z_index[k]], self.got_z.at[k], self.send.at[7 + k], self.recv.at[7 + k], m.zs[k]) for k in range(3)]
+
+    def add(self):
+        v = self.grad[:, self.me.s]
+        for k in range(7):
+            v = v + self.got[k]
+        self.total[...] = v
+
+    def result(self):
+        v = self.total[self.me.h]
+        for k in range(3):
+            v = v + self.got_z[k]
+        return v
+
+
+def start_all(copies):
+    for cp in copies:
+        cp.start()
+
+
+def wait_all(copies):
+    for cp in copies:
+        cp.wait()
+
+
+FFN_SHAPES = ((16, D), (16, FF // 2), (16, FF // 2), (32, D), (32, D))
+
+
+def ffn_index(k, whole):
+    half = (k - 1) % 2
+    if k == 0:
+        return 0, ()
+    if k < 3:
+        return 1, (slice(None), whole(FF // 2 * half, FF // 2))
+    return 2, (whole(32 * half, 32),)
+
+
+def ffn_view(refs, k, index):
+    which, tail = ffn_index(k, pl.ds)
+    return refs[which].at[index + tail]
+
+
+def ffn_values(refs, k, index):
+    which, tail = ffn_index(k, lambda at, n: slice(at, at + n))
+    return refs[which][index + tail]
+
+
 def scatter_bufs(shape, dtype):
     return [VMEM((4, 2, 2) + shape, dtype), VMEM((4, 2) + shape, dtype), VMEM((4,) + shape, dtype), VMEM((3,) + shape, dtype)]
 
@@ -330,9 +451,9 @@
         b1[0:1, D * q:D * q + D] = jnp.sum(jnp.where(ok, x, 0.0), axis=0, keepdims=True)
 
 
-def fill_bias(bias, kvx, labq, place, tiles):
+def fill_bias(bias, labk, labq, place, tiles):
     def matching(i):
-        kl = kvx[tile_at(i):tile_at(i) + tile_keys(i), LABEL:WIDE].astype(F32)
+        kl = labk[tile_at(i):tile_at(i) + tile_keys(i), :].astype(F32)
         return (kl == labq[i:i + 1, :]) & (kl != 0.0)
 
     r, c = iota((160, 128), 0), iota((160, 128), 1)
@@ -381,9 +502,9 @@
     if near:
         wq_o, vecs_o, b1_o = take(3)
         ffn_o = take(3)
-    kvx, qx, bias, a1, ao, iz, sp, spt, xh, labq, n0, nc, z0, out_sem, e_send, e_recv = take(16)
-    if near:
-        wq, vecs, b1, vt, vg, local, send, recv = take(8)
+    kvx, qx, bias, a1, ao, iz, sp, spt, xh, labq, n0, nc, z0, labk, seg2, msg, got, wbuf, out_sem, e_send, e_recv = take(21)
+    if near:
+        wq, vecs, b1, vt, vg, local, send, recv, send_v, recv_v = take(10)
     me = Peers(near)
     place = me.place
     outs = []
@@ -393,56 +514,87 @@
         cp.start()
         outs.append(cp)
 
-    for l, size in enumerate(SIZES):
-        kvx[EXT_AT[l]:EXT_AT[l] + 16, :] = jnp.zeros((16, WIDE), BF16)
-        kvx[EXT_AT[l] + 16 + size:EXT_AT[l] + 32 + size, :] = jnp.zeros((16, WIDE), BF16)
+    got[...] = jnp.zeros_like(got)
     if near:
         small_rows(vt, *small)
     greet(me.greeted)
-    if near:
-        lane = (pl.ds(0, 256), pl.ds(256, 256))
-        first = [Gather(me, vt, lambda h, y, x, c: vg.at[h, y, x, c], False, local.at[0], send.at[0], recv.at[0])]
+    ids_core = rcopy(seg, seg2, e_send.at[6], e_recv.at[6], me.core)
+    ids_core.start()
+    if near:
+        small_g = SmallGather(me, vt, vg, local.at[15], send_v, recv_v)
+        small_g.own().start()
+        start_all(small_g.first())
+        first = []
         for k in range(2):
-            first.append(Gather(me, wq_in.at[:, :, lane[k]], lambda h, y, x, c, k=k: wq.at[:, h, y, x, c, :, lane[k]], k == 1,
-                                local.at[1 + k], send.at[1 + k], recv.at[1 + k]))
-        later = [Gather(me, ffn_in[k], lambda h, y, x, c, k=k: ffn_o[k].at[h, y, x, c], k == 2,
-                        local.at[3 + k], send.at[3 + k], recv.at[3 + k]) for k in range(3)]
-
-    def advance(group, stage):
-        if near:
-            for a in (first if group == 0 else later):
-                if stage >= 0:
-                    a.wait(stage)
-                if stage < 3:
-                    a.start(stage + 1)
-
-    advance(0, -1)
+            lanes = pl.ds(256 * k, 256)
+            first.append(Gather(me, wq_in.at[:, :, lanes], lambda h, y, x, c, lanes=lanes: wq.at[:, h, y, x, c, :, lanes], k == 1,
+                                local.at[k], send.at[k], recv.at[k]))
+        later = [Gather(me, ffn_view(ffn_in, k, ()), lambda h, y, x, c, k=k: ffn_view(ffn_o, k, (h, y, x, c)), k in (2, 4),
+                        local.at[2 + k], send.at[2 + k], recv.at[2 + k]) for k in range(5)]
+
+    def step(group, stage, *pieces):
+        if not near:
+            return
+        for k in pieces:
+            a = (first if group == 0 else later)[k]
+            if stage >= 0:
+                a.wait(stage)
+            if stage < 3:
+                a.start(stage + 1)
+
+    step(0, -1, 0, 1)
     fill_pool(sp)
     fill_spread(spt)
     emit(sp, sp_o)
     emit(spt, spt_o)
-    advance(0, 0)
-    advance(1, -1)
-    ids = seg[:, pl.ds(pl.multiple_of(me.h * TOK, TOK), TOK)].astype(F32)
+    if near:
+        small_g.own().wait()
+        wait_all(small_g.first())
+        start_all(small_g.second())
+    step(0, 0, 0, 1)
+    step(1, -1, 0, 1, 2, 3, 4)
+    ids_core.wait()
+
+    def chunk(ref, k):
+        return ref[:, pl.ds(pl.multiple_of(TOK * k, TOK), TOK)].astype(F32)
+    odd = me.odd.astype(F32)
+    ids = chunk(seg, me.h)
+    ids_left = jnp.where(me.h > 0, chunk(seg, lax.rem(me.h + 3, 4)), chunk(seg2, 3) * odd)
+    ids_right = jnp.where(me.h < 3, chunk(seg, lax.rem(me.h + 1, 4)), chunk(seg2, 0) * (1.0 - odd))
     ids_b = jnp.broadcast_to(ids, (128, TOK)).astype(BF16)
     sq_b = jnp.broadcast_to(ids * ids, (128, TOK)).astype(BF16)
     eye = identity(TILE)
     for j in range(TILES):
-        kvx[16 + TILE * j:16 + TILE * j + TILE, LABEL:WIDE] = mm_bt(eye, ids_b[:, TILE * j:TILE * j + TILE]).astype(BF16)
+        labk[16 + TILE * j:16 + TILE * j + TILE, :] = mm_bt(eye, ids_b[:, TILE * j:TILE * j + TILE]).astype(BF16)
     for i in range(8):
         labq[i:i + 1, :] = ids[:, 128 * i:128 * i + 128]
-    wide_at = pl.multiple_of(WIDE_AT + 16 * place, 16)
-
-    def put_coarse(b, value, cols):
+    row, t = iota((128, TOK), 0), iota((128, TOK), 1)
+    level, level_row = row >> 4, iota((1, 128), 1) >> 4
+    for side, v in ((0, ids_left), (1, ids_right)):
+        base = jnp.right_shift(TOK, level) - 16 if side == 0 else 0
+        sel = ones_where(jnp.right_shift(t, level) == base + (row & 15))
+        x = mm_bt(two_rows(v, v * v).astype(BF16), sel)
+        col = column_of(labels_of(x[0:1], x[1:2], jnp.left_shift(1, level_row).astype(F32)), 128)
+        for l in range(7):
+            labk[border(side, l):border(side, l) + 16, :] = col[16 * l:16 * l + 16]
+    even_ids = [jnp.where(me.odd == 0, chunk(seg, k), chunk(seg2, k)) for k in range(4)]
+    odd_ids = [jnp.where(me.odd == 0, chunk(seg2, k), chunk(seg, k)) for k in range(4)]
+    all_ids = jnp.concatenate(even_ids + odd_ids, axis=0)
+    x = mm_bt(jnp.concatenate([all_ids, all_ids * all_ids], axis=0).astype(BF16), sp[496:512, :])
+    lab = labels_of(x[0:8], x[8:16], jnp.where(iota((8, 16), 1) < 8, 128.0, 256.0))
+    lab = jnp.broadcast_to(lab[:, None, :], (8, 16, 16)).reshape(128, 16)
+    lab = jnp.sum(jnp.where((iota((128, 16), 0) & 15) == iota((128, 16), 1), lab, 0.0), axis=1, keepdims=True)
+    labk[WIDE_AT:EXT, :] = jnp.broadcast_to(lab, (128, 128)).astype(BF16)
+
+    def put_coarse(dst, b, value, cols):
         at, block, _t, _n = coarse_blocks()[b]
         if block < 3:
             level = block + 1
             row = EXT_AT[level] + 16 + at - (0, 512, 768)[block]
-            kvx[row:row + 128, cols] = value
+            dst[row:row + 128, cols] = value
         else:
             for level, a, n in ((4, 0, 64), (5, 64, 32), (6, 96, 16)):
-                kvx[EXT_AT[level] + 16:EXT_AT[level] + 16 + n, cols] = value[a:a + n]
-            kvx[pl.ds(wide_at, 16), cols] = value[112:128]
+                dst[EXT_AT[level] + 16:EXT_AT[level] + 16 + n, cols] = value[a:a + n]
 
     for b, (at, block, t, n) in enumerate(coarse_blocks()):
         s = sp[128 * block:128 * block + 128, t:t + n]
@@ -451,19 +603,18 @@
         times_r = (1 << rows_level).astype(F32) if block == 3 else float(2 ** (block + 1))
         times_c = (1 << cols_level).astype(F32) if block == 3 else float(2 ** (block + 1))
         lab = labels_of(mm_bt(s, ids_b[:, t:t + n]), mm_bt(s, sq_b[:, t:t + n]), times_r)
-        put_coarse(b, lab.astype(BF16), slice(LABEL, WIDE))
+        put_coarse(labk, b, lab.astype(BF16), slice(0, 128))
         row = labels_of(mm_bt(ids_b[0:8, t:t + n], s), mm_bt(sq_b[0:8, t:t + n], s), times_c)
         labq[8 + b:9 + b, :] = row[0:1, :]
-    fill_bias(bias, kvx, labq, place, INNER)
-    advance(0, 1)
+    step(0, 1, 0, 1)
+    fill_bias(bias, labk, labq, place, range(16))
+    emit(bias, bias_o)
     for j in range(TILES):
         v = tok[TILE * j:TILE * j + TILE, :].astype(F32)
         center = v - jnp.mean(v, axis=-1, keepdims=True)
         xh[TILE * j:TILE * j + TILE, :] = center * lax.rsqrt(jnp.mean(center * center, axis=-1, keepdims=True) + EPS)
-    advance(0, 2)
-    advance(1, 0)
-    if near:
-        first[0].wait(3)
+    if near:
+        wait_all(small_g.second())
         unpack_small(vg, vecs, b1)
         emit(vecs, vecs_o)
         emit(b1, b1_o)
@@ -471,9 +622,10 @@
         rows = slice(TILE * j, TILE * j + TILE)
         a1[rows, :] = (xh[rows, :] * vecs[0:1, :] + vecs[1:2, :]).astype(BF16)
     emit(a1, a1_o)
-    if near:
-        first[1].wait(3)
-        first[2].wait(3)
+    step(0, 2, 0, 1)
+    step(1, 0, 0, 1, 2, 3, 4)
+    step(0, 3, 0, 1)
+    if near:
         emit(wq, wq_o)
     for c in range(3):
         w = wq[c].reshape(D, D)
@@ -483,6 +635,7 @@
                 qx[TILE * j:TILE * j + TILE, :] = r * jnp.array(0.125, BF16)
             else:
                 kvx[16 + TILE * j:16 + TILE * j + TILE, D * (c - 1):D * c] = r
+    step(1, 1, 0, 1, 2)
     for b, (at, block, t, n) in enumerate(coarse_blocks()):
         s = sp[128 * block:128 * block + 128, t:t + n]
         if block == 3:
@@ -491,28 +644,35 @@
         else:
             shrink = 0.5 ** (block + 1)
         qx[1024 + at:1024 + at + 128, :] = (mm(s, qx[t:t + n, :]) * shrink).astype(BF16)
-        put_coarse(b, (mm(s, kvx[16 + t:16 + t + n, 0:D]) * shrink).astype(BF16), slice(0, D))
-        put_coarse(b, mm(s, kvx[16 + t:16 + t + n, D:2 * D]).astype(BF16), slice(D, 2 * D))
-    to_right, to_left = [], []
-    for l, size in enumerate(SIZES):
-        at = EXT_AT[l]
-        to_right.append(rcopy(kvx.at[pl.ds(at + size, 16)], kvx.at[pl.ds(at, 16)], e_send.at[l], e_recv.at[l], me.right))
-        to_left.append(rcopy(kvx.at[pl.ds(at + 16, 16)], kvx.at[pl.ds(at + 16 + size, 16)], e_send.at[7 + l], e_recv.at[7 + l], me.left))
-    own_wide = kvx.at[pl.ds(wide_at, 16)]
-    wide_z = [rcopy(own_wide, own_wide, e_send.at[14 + k], e_recv.at[14 + k], me.zs[k]) for k in range(3)]
-    four = kvx.at[pl.ds(pl.multiple_of(WIDE_AT + 64 * me.odd, 16), 64)]
-    wide_core = rcopy(four, four, e_send.at[17], e_recv.at[17], me.core)
+        kc, vc = mm(s, kvx[16 + t:16 + t + n, 0:D]) * shrink, mm(s, kvx[16 + t:16 + t + n, D:2 * D])
+        put_coarse(kvx, b, kc.astype(BF16), slice(0, D))
+        put_coarse(kvx, b, vc.astype(BF16), slice(D, 2 * D))
+        if block == 3:
+            wbuf[place] = jnp.concatenate([kc[112:120], vc[112:120]], axis=0).astype(BF16)
+    step(1, 1, 3, 4)
+    for side in range(2):
+        for l in range(7):
+            at = own_border(side, l)
+            k16, v16 = kvx[at:at + 16, 0:D], kvx[at:at + 16, D:2 * D]
+            if l == 0:
+                msg[side, 0], msg[side, 1] = k16, v16
+            else:
+                far = [pick_far(side, v.astype(F32)) for v in (k16, v16)]
+                msg[side, l + 1] = jnp.concatenate(far, axis=0).astype(BF16)
+    to_right = rcopy(msg.at[1], got.at[0], e_send.at[0], e_recv.at[0], me.right)
+    to_left = rcopy(msg.at[0], got.at[1], e_send.at[1], e_recv.at[1], me.left)
+    wide_z = [rcopy(wbuf.at[place], wbuf.at[place], e_send.at[2 + k], e_recv.at[2 + k], me.zs[k]) for k in range(3)]
+    four = wbuf.at[pl.ds(4 * me.odd, 4)]
+    wide_core = rcopy(four, four, e_send.at[5], e_recv.at[5], me.core)
     not_last, not_first = place < 7, place > 0
 
     @pl.when(not_last)
     def _():
-        for cp in to_right:
-            cp.start()
+        to_right.start()
 
     @pl.when(not_first)
     def _():
-        for cp in to_left:
-            cp.start()
+        to_left.start()
     for cp in wide_z:
         cp.start()
     emit(qx, qx_o)
@@ -537,39 +697,56 @@
             high, low = split(two_rows(z0_, z1_))
             nc[g, :, cols] = jnp.concatenate([n.astype(BF16), high, low], axis=0)
 
-    def run(tiles, lo, hi):
-        @pl.loop(lo, hi)
-        def _(g):
-            for i in tiles:
-                tile(g, i)
-    run(INNER, 0, 1)
-    advance(1, 1)
-    for cp in wide_z:
-        cp.wait()
-    wide_core.start()
-    run(INNER, 1, 4)
-    advance(1, 2)
+    @pl.loop(0, 4)
+    def _(g):
+        for k in range(4):
+            @pl.when(g == k)
+            def _():
+                if k == 3:
+                    step(1, 2, 0, 2)
+                if k == 1:
+                    wait_all(wide_z)
+                    wide_core.start()
+        for i in INNER:
+            tile(g, i)
+
+    wide_core.wait()
+    w = wbuf[...].reshape(128, D)
+    kvx[WIDE_AT:EXT, 0:D] = mm(wide_rows(0), w).astype(BF16)
+    kvx[WIDE_AT:EXT, D:2 * D] = mm(wide_rows(1), w).astype(BF16)
 
     @pl.when(not_last)
     def _():
-        for cp in to_right:
-            cp.wait_send()
-        for cp in to_left:
-            cp.wait_recv()
+        to_right.wait_send()
+        to_left.wait_recv()
 
     @pl.when(not_first)
     def _():
-        for cp in to_left:
-            cp.wait_send()
-        for cp in to_right:
-            cp.wait_recv()
-    wide_core.wait()
+        to_left.wait_send()
+        to_right.wait_recv()
+    for side in range(2):
+        m = got[side].reshape(128, D)
+        closer = mm(near_rows(side), m)
+        m = m.astype(F32)
+        for l in range(7):
+            at = border(side, l)
+            if l == 0:
+                k16, v16 = m[0:16], m[16:32]
+            else:
+                a, b = 16 * (l + 1), 16 * (l - 1)
+                k16 = far_and_near(side, m[a:a + 8], closer[b:b + 8])
+                v16 = far_and_near(side, m[a + 8:a + 16], closer[b + 8:b + 16])
+            kvx[at:at + 16, 0:D] = k16.astype(BF16)
+            kvx[at:at + 16, D:2 * D] = v16.astype(BF16)
     emit(kvx, kvx_o)
-    fill_bias(bias, kvx, labq, place, OUTER)
-    emit(bias, bias_o)
 
     @pl.loop(0, 4)
     def _(g):
+        for k in range(4):
+            @pl.when(g == k)
+            def _():
+                if k > 0:
+                    step(1, 2, (None, 1, 4, 3)[k])
         for i in OUTER:
             tile(g, i)
         c_ref = nc.at[g]
@@ -585,11 +762,8 @@
             ao[pl.ds(pl.multiple_of(g * 128 + 64, 64), 64), cols] = (n[64:128] * i1).astype(BF16)
     emit(ao, ao_o)
     emit(iz, iz_o)
-    if near:
-        for a in later:
-            a.wait(3)
-    for cp in outs:
-        cp.wait()
+    step(1, 3, 0, 1, 2, 3, 4)
+    wait_all(outs)
 
 
 ANY = pl.BlockSpec(memory_space=pl.ANY)
@@ -600,16 +774,17 @@
 
 def forward(near, tok, seg, *params):
     grid = (4, 2, 2, 2)
-    shapes = [S((EXT, WIDE), BF16), S((2048, D), BF16), S((BIASES, 128), F32), S((TOK, D), BF16), S((D, TOK), BF16),
+    shapes = [S((EXT, 2 * D), BF16), S((2048, D), BF16), S((BIASES, 128), F32), S((TOK, D), BF16), S((D, TOK), BF16),
               S((4, 2, TOK), F32), S((512, TOK), BF16), S((TOK, 512), BF16)]
     scratch = [VMEM(s.shape, s.dtype) for s in shapes] + [
         VMEM((TOK, D), F32), VMEM((16, 128), F32), VMEM((4, 128, TOK), F32), VMEM((4, 160, TOK), BF16), VMEM((4, 2, TOK), F32),
-        SEM((16,)), SEM((18,)), SEM((18,))]
+        VMEM((EXT, 128), BF16), VMEM(seg.shape, I32), VMEM((2, 8, 16, D), BF16), VMEM((2, 8, 16, D), BF16), VMEM((8, 16, D), BF16),
+        SEM((16,)), SEM((7,)), SEM((7,))]
     if near:
         shapes += [S((3,) + grid + (16, D), BF16), S((16, D), F32), S((1, FF), F32)]
         shapes += [S(grid + a.shape, a.dtype) for a in params[9:]]
         scratch += [VMEM((3,) + grid + (16, D), BF16), VMEM((16, D), F32), VMEM((1, FF), F32), VMEM((8, 128), F32),
-                    VMEM(grid + (8, 128), F32), SEM((6,)), SEM((6, 6)), SEM((6, 6))]
+                    VMEM((4, 8, 8, 128), F32), SEM((16,)), SEM((7, 6)), SEM((7, 6)), SEM((10,)), SEM((10,))]
         specs = [IN_VMEM] * 9 + [ANY] * 3
     else:
         specs = [IN_VMEM] * 2
@@ -723,7 +898,7 @@
     for q in range(4):
         ok = ((row >> 3) == ((n + 512 * q) >> 6)) & ((row & 7) == ((n >> 3) & 7))
         out = out + moved(jnp.broadcast_to(b1[0:1, D * q:D * q + D], (256, D)), ok, last)
-    return out.reshape(4, 2, 2, 2, 8, 128)
+    return out.reshape(4, 8, 8, 128)
 
 
 def backward_kernel(near, *refs):
@@ -739,10 +914,10 @@
     small_o = take(8 if near else 1)
     gffn_o = take(3 if near else 0)
     kvx, qx, bias, a1, ao, iz, sp, spt, da, tok, dh1, wq, vecs = take(13)
-    gr, rm, dqt, dkv, dq, edge, e_got, w_send, w_got, w_mid, aw, avec, tok_s, in_sem, out_sem, e_send, e_recv = take(17)
-    if near:
-        gq, gv, f_mine, f_sem, send, recv = take(6)
-        bufs = [take(4) for _ in range(6)]
+    gr, rm, dqt, dkv, dq, edge, e_got, w_all, w_got, w_mid, gq, avec, tok_s, dall, in_sem, out_sem, e_send, e_recv = take(18)
+    if near:
+        gv, f_mine, f_sem, send, recv, send_v, recv_v, v_got, v_sum, v_z = take(10)
+        bufs = [take(4) for _ in range(11)]
     me = Peers(near)
     place = me.place
     loads = {}
@@ -754,29 +929,44 @@
     greet(me.greeted)
     mine_copies = []
     if near:
-        lane = (pl.ds(0, 256), pl.ds(256, 256))
-        ffn = []
         for k in range(3):
             cp = pltpu.make_async_copy(gffn[k].at[:, :, :, me.c], f_mine[k], f_sem.at[k])
             cp.start()
             mine_copies.append(cp)
-            ffn.append(Scatter(me, lambda c, k=k: gffn[k].at[:, :, :, c], lambda h, y, x, k=k: f_mine[k][h, y, x], k == 2,
-                               bufs[k], send.at[k], recv.at[k]))
-        last = [Scatter(me, lambda c: gv.at[:, :, :, c], lambda h, y, x: gv[h, y, x, me.c], False, bufs[3], send.at[3], recv.at[3])]
-        for k in range(2):
-            last.append(Scatter(me, lambda c, k=k: gq.at[:, :, :, c, :, :, lane[k]],
-                                lambda h, y, x, k=k: gq[h, y, x, me.c, :, :, 256 * k:256 * k + 256], k == 1,
-                                bufs[4 + k], send.at[4 + k], recv.at[4 + k]))
-
-    def advance(group, stage):
-        for a in group:
-            if stage >= 0:
-                a.wait(stage)
+        every = slice(None)
+        ffn = [Scatter(me, lambda c, k=k: ffn_view(gffn, k, (every, every, every, c)), lambda h, y, x, k=k: ffn_values(f_mine, k, (h, y, x)),
+                       k in (2, 4), bufs[k], send.at[k], recv.at[k]) for k in range(5)]
+        last = []
+        for k in range(6):
+            lo = 256 * (k % 2)
+            last.append(Scatter(me, lambda c, k=k, lo=lo: gq.at[k // 2, :, :, :, c, :, pl.ds(lo, 256)],
+                                lambda h, y, x, k=k, lo=lo: gq[k // 2, h, y, x, me.c, :, lo:lo + 256], k % 2 == 1,
+                                bufs[5 + k], send.at[5 + k], recv.at[5 + k]))
+        small_s = SmallScatter(me, gv, v_got, v_sum, v_z, send_v, recv_v)
+        for a in ffn:
+            a.start(0)
+
+    def put_ffn(k):
+        which, tail = ffn_index(k, lambda at, n: slice(at, at + n))
+        gffn_o[which][tail or (slice(None),)] = ffn[k].result()
+
+    def put_last(k):
+        gq_o[k // 2, :, 256 * (k % 2):256 * (k % 2) + 256] = last[k].result()
+
+    def step(group, stage, *pieces):
+        if not near:
+            return
+        for k in pieces:
+            a = (ffn if group == 0 else last)[k]
+            a.wait(stage)
+            if stage < 3:
                 a.add(stage)
-            a.start(stage + 1)
-
-    if near:
-        advance(ffn, -1)
+                a.start(stage + 1)
+            elif group == 0:
+                put_ffn(k)
+            else:
+                put_last(k)
+
     for name in ("da", "ao", "iz", "sp"):
         loads[name].wait()
     masks = head_masks(128)
@@ -820,20 +1010,34 @@
         dkv[keys, lanes_of(g, D)] += mm_bt(e.astype(BF16), gb)
         dqt[g, :, cols] = (own_blocks(mm_at(kw, ds)) * (0.125 / tile_times(i))).astype(BF16)
 
-    def run(tiles, lo, hi):
-        @pl.loop(lo, hi)
-        def _(g):
-            for i in tiles:
-                tile(g, i)
-    run(OUTER, 0, 4)
-    for l, size in enumerate(SIZES):
-        edge[0, l] = dkv[EXT_AT[l] + 16 + size:EXT_AT[l] + 32 + size, :].astype(BF16)
-        edge[1, l] = dkv[EXT_AT[l]:EXT_AT[l] + 16, :].astype(BF16)
-    half_at = pl.multiple_of(WIDE_AT + 64 * (1 - me.odd), 16)
-    w_send[...] = dkv[pl.ds(half_at, 64), :].astype(BF16)
-    to_right = rcopy(edge.at[0], e_got.at[0], e_send.at[0], e_recv.at[0], me.right)
-    to_left = rcopy(edge.at[1], e_got.at[1], e_send.at[1], e_recv.at[1], me.left)
-    wide_core = rcopy(w_send, w_mid, e_send.at[2], e_recv.at[2], me.core)
+    if near:
+        wait_all(mine_copies)
+    step(0, 0, 0, 1, 2, 3, 4)
+
+    @pl.loop(0, 4)
+    def _(g):
+        for i in OUTER:
+            tile(g, i)
+    for side in range(2):
+        base, closer = [], []
+        for l in range(7):
+            at = border(side, l)
+            k16, v16 = dkv[at:at + 16, 0:D], dkv[at:at + 16, D:2 * D]
+            if l == 0:
+                base += [k16, v16]
+            elif side == 0:
+                base += [k16[0:8], v16[0:8]]
+                closer += [k16[8:16], v16[8:16]]
+            else:
+                base += [k16[8:16], v16[8:16]]
+                closer += [k16[0:8], v16[0:8]]
+        folded = mm_at(near_rows(side), jnp.concatenate(closer, axis=0).astype(BF16))
+        edge[side] = (jnp.concatenate(base, axis=0) + folded).astype(BF16).reshape(8, 16, D)
+    d_wide = mm_at(wide_rows(0), dkv[WIDE_AT:EXT, 0:D].astype(BF16)) + mm_at(wide_rows(1), dkv[WIDE_AT:EXT, D:2 * D].astype(BF16))
+    w_all[...] = d_wide.astype(BF16).reshape(8, 16, D)
+    to_right = rcopy(edge.at[1], e_got.at[0], e_send.at[0], e_recv.at[0], me.right)
+    to_left = rcopy(edge.at[0], e_got.at[1], e_send.at[1], e_recv.at[1], me.left)
+    wide_core = rcopy(w_all.at[pl.ds(4 * (1 - me.odd), 4)], w_mid, e_send.at[2], e_recv.at[2], me.core)
     not_last, not_first = place < 7, place > 0
     wide_core.start()
 
@@ -844,21 +1048,23 @@
     @pl.when(not_first)
     def _():
         to_left.start()
-    if near:
-        for cp in mine_copies:
-            cp.wait()
-        advance(ffn, 0)
-    run(INNER, 0, 2)
+    step(0, 1, 0, 1, 2)
+
+    @pl.loop(0, 2)
+    def _(g):
+        for i in INNER:
+            tile(g, i)
     wide_core.wait()
-    own_at = pl.multiple_of(WIDE_AT + 64 * me.odd, 16)
-    w_mid[...] = (w_mid[...].astype(F32) + dkv[pl.ds(own_at, 64), :]).astype(BF16)
-    wide_z = [rcopy(w_mid.at[pl.ds(pl.multiple_of(16 * me.z_index[k], 16), 16)], w_got.at[k], e_send.at[3 + k], e_recv.at[3 + k], me.zs[k])
-              for k in range(3)]
-    for cp in wide_z:
-        cp.start()
-    if near:
-        advance(ffn, 1)
-    run(INNER, 2, 4)
+    for k in range(4):
+        w_mid[k] = (w_mid[k].astype(F32) + w_all[4 * me.odd + k].astype(F32)).astype(BF16)
+    wide_z = [rcopy(w_mid.at[me.z_index[k]], w_got.at[k], e_send.at[3 + k], e_recv.at[3 + k], me.zs[k]) for k in range(3)]
+    start_all(wide_z)
+
+    @pl.loop(2, 4)
+    def _(g):
+        for i in INNER:
+            tile(g, i)
+    step(0, 1, 3, 4)
 
     @pl.loop(0, 4)
     def _(g):
@@ -868,53 +1074,67 @@
             cols = slice(TILE * j, TILE * j + TILE)
             r = d_ref[:, cols].astype(F32) + mm(coarse_cols(d_ref, 1024, j), sp[:, cols])
             dq[cols, lanes_of(g)] = mm_bt(eye, r.astype(BF16)).astype(BF16)
+    for name in ("spt", "a1", "tok", "dh1", "wq", "vecs"):
+        loads[name].wait()
+    avec[...] = jnp.zeros_like(avec)
+
+    def projection_grad(c, d):
+        aw = mm_at(a1[...], d).astype(BF16)
+        avec[2 + c:3 + c, :] = jnp.sum(d.astype(F32), axis=0, keepdims=True)
+        gq[c] = aw.reshape(4, 2, 2, 2, 16, D)
+        if near:
+            for a in last[2 * c:2 * c + 2]:
+                a.start(0)
+    projection_grad(0, dq[...])
+    step(0, 2, 0, 1, 2)
     for cp in wide_z:
         cp.wait()
+
+    def add_edge(side):
+        m = e_got[side].reshape(128, D).astype(F32)
+        for l in range(7):
+            if l == 0:
+                at, n = own_border(side, 0), 16
+            else:
+                at, n = own_border(side, l) + (0 if side else 8), 8
+            a = 16 * (l + 1) if l else 0
+            dkv[at:at + n, 0:D] += m[a:a + n]
+            dkv[at:at + n, D:2 * D] += m[a + n:a + 2 * n]
 
     @pl.when(not_last)
     def _():
         to_right.wait_send()
         to_left.wait_recv()
-        for l, size in enumerate(SIZES):
-            rows = slice(EXT_AT[l] + size, EXT_AT[l] + 16 + size)
-            dkv[rows, :] += e_got[1, l].astype(F32)
+        add_edge(1)
 
     @pl.when(not_first)
     def _():
         to_left.wait_send()
         to_right.wait_recv()
-        for l, size in enumerate(SIZES):
-            rows = slice(EXT_AT[l] + 16, EXT_AT[l] + 32)
-            dkv[rows, :] += e_got[0, l].astype(F32)
-    v = w_mid[pl.ds(pl.multiple_of(16 * me.h, 16), 16), :].astype(F32)
+        add_edge(0)
+    v = w_mid[me.h].astype(F32)
     for k in range(3):
         v = v + w_got[k].astype(F32)
-    wide_row, wide_lane = iota((16, 2 * D), 0), iota((16, 2 * D), 1)
-    w_own = (v * jnp.where(wide_lane >= D, 1.0, jnp.where(wide_row < 8, 0.5 ** 7, 0.5 ** 8))).astype(BF16)
+    v = jnp.concatenate([v[0:8] * 0.5 ** 7, v[8:16]], axis=1)
+    w_own = jnp.concatenate([v, jnp.zeros((8, 2 * D), F32)], axis=0).astype(BF16)
     lane_all = iota((1, 2 * D), 1)
 
     def coarse_rows(at, n, level):
         return (dkv[at:at + n, :] * jnp.where(lane_all < D, 0.5 ** level, 1.0)).astype(BF16)
-    for name in ("spt", "a1", "tok", "dh1", "wq", "vecs"):
-        loads[name].wait()
     top = jnp.concatenate([coarse_rows(EXT_AT[3] + 16, 128, 3), coarse_rows(EXT_AT[4] + 16, 64, 4), coarse_rows(EXT_AT[5] + 16, 32, 5),
                            coarse_rows(EXT_AT[6] + 16, 16, 6), w_own], axis=0)
-    avec[...] = jnp.zeros_like(avec)
-    aw[...] = jnp.zeros_like(aw)
-    if near:
-        avec[5:9, :] = gvec[5:9, :]
-        advance(ffn, 2)
     for j in range(TILES):
         rows = slice(TILE * j, TILE * j + TILE)
         x = jnp.concatenate([coarse_rows(EXT_AT[1] + 16 + 128 * j, 128, 1), coarse_rows(EXT_AT[2] + 16 + 128 * (j // 2), 128, 2), top], axis=0)
-        d = (dkv[16 + TILE * j:16 + TILE * j + TILE, :] + mm(spt[rows, :], x)).astype(BF16)
-        parts = (dq[rows, :], d[:, 0:D], d[:, D:2 * D])
-        a = a1[rows, :]
-        da1 = jnp.zeros((TILE, D), F32)
-        for c in range(3):
-            aw[c] += mm_at(a, parts[c])
-            avec[2 + c:3 + c, :] += jnp.sum(parts[c].astype(F32), axis=0, keepdims=True)
-            da1 = da1 + mm_bt(parts[c], wq[c].reshape(D, D))
+        dall[rows, :] = (dkv[16 + TILE * j:16 + TILE * j + TILE, :] + mm(spt[rows, :], x)).astype(BF16)
+    projection_grad(1, dall[:, 0:D])
+    step(0, 2, 3, 4)
+    step(1, 0, 0, 1)
+    projection_grad(2, dall[:, D:2 * D])
+    step(1, 0, 2, 3)
+    for j in range(TILES):
+        rows = slice(TILE * j, TILE * j + TILE)
+        da1 = mm_bt(dq[rows, :], wq[0].reshape(D, D)) + mm_bt(dall[rows, 0:D], wq[1].reshape(D, D)) + mm_bt(dall[rows, D:2 * D], wq[2].reshape(D, D))
         v = tok[rows, :].astype(F32)
         center = v - jnp.mean(v, axis=-1, keepdims=True)
         inverse = lax.rsqrt(jnp.mean(center * center, axis=-1, keepdims=True) + EPS)
@@ -924,39 +1144,39 @@
         tok_s[rows, :] = (dh1[rows, :] + dv).astype(BF16)
         avec[0:1, :] += jnp.sum(da1 * n, axis=0, keepdims=True)
         avec[1:2, :] += jnp.sum(da1, axis=0, keepdims=True)
+        if j == 0:
+            step(1, 0, 4, 5)
+        elif j == 1:
+            step(1, 1, 0, 1)
+        elif j == 2:
+            step(1, 1, 2, 3)
     done = pltpu.make_async_copy(tok_s, tok_o, out_sem.at[0])
     done.start()
     if not near:
-        gq_o[...] = aw[...].astype(BF16)
+        gq_o[...] = gq[...]
         small_o[0][...] = avec[...]
         done.wait()
         return
-    for c in range(3):
-        gq[:, :, :, :, c] = aw[c].astype(BF16).reshape(4, 2, 2, 2, 16, D)
-    for a in last[1:]:
-        a.start(0)
+    avec[5:9, :] = gvec[5:9, :]
     gv[...] = pack_small(avec[...], gb1)
-    last[0].start(0)
-    for a in ffn:
-        a.wait(3)
-    for k in range(3):
-        gffn_o[k][...] = ffn[k].result()
-    for stage in range(3):
-        for a in last:
-            a.wait(stage)
-            a.add(stage)
-            a.start(stage + 1)
-    for a in last:
-        a.wait(3)
-    gq_o[:, :, 0:256] = last[1].result()
-    gq_o[:, :, 256:512] = last[2].result()
-    t = last[0].result()
+    start_all(small_s.first())
+    step(1, 1, 4, 5)
+    step(1, 2, 0, 1)
+    wait_all(small_s.first())
+    small_s.add()
+    start_all(small_s.second())
+    step(1, 2, 2, 3, 4, 5)
+    step(0, 3, 0, 1, 2, 3, 4)
+    step(1, 3, 0, 1, 2, 3, 4, 5)
+    wait_all(small_s.second())
+    t = small_s.result()
     for k, r in enumerate((0, 1, None, 5, 6, 7)):
         if r is None:
             small_o[k][...] = t[2:5, 0:16]
         else:
             small_o[k][...] = t[r:r + 1, 0:16]
-    small_o[6][...] = t[:, 32:40]
+    for r in range(8):
+        small_o[6][0:1, 8 * r:8 * r + 8] = t[r:r + 1, 32:40]
     small_o[7][...] = t[0:1, 16:32]
     done.wait()
 
@@ -966,22 +1186,22 @@
     grid = (4, 2, 2, 2)
     vm = [VMEM(v.shape, v.dtype) for v in (kvx, qx, bias, a1, ao, iz, sp, spt, da, tok, dh1, wq, vecs)]
     scratch = vm + [VMEM((4, 160, 2048), BF16), VMEM((4, 2, 2048), F32), VMEM((4, 128, 2048), BF16), VMEM((EXT, 2 * D), F32),
-                    VMEM((TOK, D), BF16), VMEM((2, 7, 16, 2 * D), BF16), VMEM((2, 7, 16, 2 * D), BF16), VMEM((64, 2 * D), BF16),
-                    VMEM((3, 16, 2 * D), BF16), VMEM((64, 2 * D), BF16), VMEM((3, D, D), F32), VMEM((16, D), F32), VMEM((TOK, D), BF16),
+                    VMEM((TOK, D), BF16), VMEM((2, 8, 16, D), BF16), VMEM((2, 8, 16, D), BF16), VMEM((8, 16, D), BF16),
+                    VMEM((3, 16, D), BF16), VMEM((4, 16, D), BF16), VMEM((3,) + grid + (16, D), BF16), VMEM((16, D), F32), VMEM((TOK, D), BF16), VMEM((TOK, 2 * D), BF16),
                     SEM((13,)), SEM((1,)), SEM((6,)), SEM((6,))]
     if near:
         gffn = [g.reshape(grid + (g.shape[0] // 32, g.shape[1])) for g in gffn]
         shapes = [S((TOK, D), BF16), S((3, 16, D), F32)]
-        shapes += [S((1, 16), F32), S((1, 16), F32), S((3, 16), F32), S((1, 16), F32), S((1, 16), F32), S((1, 16), F32), S((8, 8), F32), S((1, 16), F32)]
+        shapes += [S((1, 16), F32), S((1, 16), F32), S((3, 16), F32), S((1, 16), F32), S((1, 16), F32), S((1, 16), F32), S((1, 64), F32), S((1, 16), F32)]
         shapes += [S(g.shape[4:], F32) for g in gffn]
-        pieces = [(g.shape[4:], BF16) for g in gffn] + [((8, 128), F32), ((3, 16, 256), BF16), ((3, 16, 256), BF16)]
-        scratch += [VMEM(grid + (3, 16, D), BF16), VMEM(grid + (8, 128), F32), [VMEM((4, 2, 2) + g.shape[4:], BF16) for g in gffn], SEM((3,)),
-                    SEM((6, 6)), SEM((6, 6))]
+        pieces = [(shape, BF16) for shape in FFN_SHAPES] + [((16, 256), BF16)] * 6
+        scratch += [VMEM((4, 8, 8, 128), F32), [VMEM((4, 2, 2) + g.shape[4:], BF16) for g in gffn], SEM((3,)), SEM((11, 6)), SEM((11, 6)),
+                    SEM((10,)), SEM((10,)), VMEM((7, 4, 8, 128), F32), VMEM((4, 8, 128), F32), VMEM((3, 8, 128), F32)]
         for shape, kind in pieces:
             scratch += scatter_bufs(shape, kind)
     else:
         gffn = gffn[0:3]
-        shapes = [S((TOK, D), BF16), S((3, D, D), BF16), S((16, D), F32)]
+        shapes = [S((TOK, D), BF16), S((3,) + grid + (16, D), BF16), S((16, D), F32)]
     ordered = (da, ao, iz, sp, kvx, qx, bias, spt, a1, tok, dh1, wq, vecs)
     return pl.pallas_call(
         functools.partial(backward_kernel, near),
@@ -992,6 +1212,22 @@
         compiler_params=pltpu.CompilerParams(collective_id=1, has_side_effects=True, vmem_limit_bytes=62 << 20),
         name="backward",
     )(*ordered, *gffn, gvec, gb1)
+
+
+def finish_kernel(n, *refs):
+    for k in range(n):
+        refs[n + k][...] = refs[k][...]
+
+
+def finish(*values):
+    n = len(values)
+    return pl.pallas_call(
+        functools.partial(finish_kernel, n),
+        out_shape=[S(v.shape, v.dtype) for v in values],
+        in_specs=[IN_VMEM] * n,
+        out_specs=[IN_VMEM] * n,
+        name="finish",
+    )(*values)
 
 
 BOTH = ("head", "span")
@@ -1018,12 +1254,13 @@
     out, dh1, da, *gffn, gvec, gb1 = middle(tok, ao, cot, wo, w1, w2, vecs, b1)
     dtok, gwq, *rest = backward(near, saved, wq, vecs, tok, da, dh1, gffn, gvec, gb1)
     if near:
+        dtok, gwq, *rest = finish(dtok, gwq, *rest)
         small, (gwo, gw1, gw2) = rest[0:8], rest[8:11]
         small = [v if v.shape[0] == 3 else v.reshape(-1) for v in small]
     else:
         def part(v, axis=0):
             return lax.psum_scatter(v.astype(F32), BOTH, scatter_dimension=axis, tiled=True)
-        vec = rest[0]
+        vec, gwq = rest[0], gwq.reshape(3, D, D)
         gwq, gwo, gw1, gw2 = part(gwq, 1), part(gffn[0]), part(gffn[1]), part(gffn[2])
         small = (part(vec[0]), part(vec[1]), part(vec[2:5], 1), part(gvec[5]), part(gvec[6]), part(gvec[7]), part(gb1[0]), part(gvec[8]))
     return (out[None], dtok[None], small[0], small[1], gwq, small[2], gwo, small[3], small[4], small[5], gw1, small[6], gw2, small[7])

time: 163 us -> 139 us (0.85)
  Pallas kernels: 152 us -> 138 us
  local copies, waits for them, and re-layouts: 9.85 us -> 0 us
    pallas_call x1, Pallas kernels: 67.9 us -> 52.9 us  [backward(): pl.pallas_call(functools.partial(backward_kernel, near), out_shape=shapes...]
    unnamed x34 -> x0, local copies, waits for them, and re-layouts: 8.52 us -> none
    pallas_call x0 -> x1, Pallas kernels: none -> 2.53 us  [finish(): pl.pallas_call(functools.partial(finish_kernel, n), out_shape=[S(v.shape,...]
    pallas_call x1, Pallas kernels: 56.1 us -> 54.2 us  [forward(): pl.pallas_call(functools.partial(forward_kernel, near), out_shape=shapes,...]
where the time goes in v4:
time: 139 us
  Pallas kernels  138 us (99%)
    pallas_call x1, Pallas kernels, forward(): pl.pallas_call(functools.partial(forward_kernel, near), out_shape=shapes,...  54.2 us
    pallas_call x1, Pallas kernels, backward(): pl.pallas_call(functools.partial(backward_kernel, near), out_shape=shapes...  52.9 us
    pallas_call x1, Pallas kernels, middle(): pl.pallas_call(middle_kernel, grid=(TOK // TILE,), out_shape=[S((TOK, D),...  28.2 us

profile of v4, /device:TPU:0, one launch (start us, length us, event | category | flops | bytes accessed | tf_op | source)
XLA Modules:
  0.0 138.6 jit_solution(10116226669706224203)
XLA Ops:
  0.7 54.2 %forward.1 = (bf16[2384,1024]{1,0:T(8,128)(2,1)}, bf16[2048,512]{1,0:T(8,128)(2,1)}, f32[2736,128]{1,0:T(8,128)}, bf16[1024,512]{1,0:T(8,128)(2,1)}, bf16[512,10...) custom-call(bf16[1024,512]{1,0:T(8,128)(2,1)} %bitcast.24, ...), custom_call_target="tpu_custom_call" | custom-call | tf_op jit(solution)/shard_map/forward/pallas_call | solution.py:791
  54.8 28.2 %middle.1 = (bf16[1024,512]{1,0:T(8,128)(2,1)}, f32[1024,512]{1,0:T(8,128)}, bf16[512,1024]{1,0:T(8,128)(2,1)}, bf16[512,512]{1,0:T(8,128)(2,1)}, bf16[512,2048]...) custom-call(bf16[1024,512]{1,0:T(8,128)(2,1)} %bitcast.25, ...), custom_call_target="tpu_custom_call" | custom-call | tf_op jit(solution)/shard_map/middle/pallas_call | solution.py:870
  83.0 52.9 %backward.1 = (bf16[1024,512]{1,0:T(8,128)(2,1)}, f32[3,16,512]{2,1,0:T(8,128)}, f32[1,16]{1,0:T(1,128)}, f32[1,16]{1,0:T(1,128)}, f32[3,16]{1,0:T(4,128)}, /*in...) custom-call(bf16[512,1024]{1,0:T(8,128)(2,1)} %get-tuple-element.69., ...), custom_call_target="tpu_custom_call" | custom-call | tf_op jit(solution)/shard_map/backward/pallas_call | solution.py:1206
  135.9 2.5 %finish.1 = (bf16[1024,512]{1,0:T(8,128)(2,1)}, f32[3,16,512]{2,1,0:T(8,128)}, f32[1,16]{1,0:T(1,128)}, f32[1,16]{1,0:T(1,128)}, f32[3,16]{1,0:T(4,128)}, /*inde...) custom-call(bf16[1024,512]{1,0:T(8,128)(2,1)} %get-tuple-element.84., ...), custom_call_target="tpu_custom_call" | custom-call | tf_op jit(solution)/shard_map/finish/pallas_call | solution.py:1224
